TPU v7x, 512 devices: a whole 4x4x16 slice. The times are simulated.
512 devices in a mesh: ctx: 128 (over z, y, core), head: 4 (over x).
Axes of the slice: x: 4, y: 4, z: 16, core: 2. Of those that a mesh axis runs over, the one named last changes fastest.
Arguments:
- layer_input: bfloat16 [32768, 2048], P('ctx', 'head'), may hold values from -24 to 24
- queries: bfloat16 [32768, 1024], P('ctx', 'head'), may hold values from -6 to 6
- keys: bfloat16 [32768, 512], P('ctx', 'head'), may hold values from -6 to 6
- values: bfloat16 [32768, 512], P('ctx', 'head'), may hold values from -6 to 6
- result_cotangent: bfloat16 [32768, 1024], P('ctx', 'head'), may hold values from -0.3125 to 0.3125
- log_decay: float32 [4, 32768], P('head', 'ctx'), may hold values from -2 to 0
Outputs:
- weight_k_grad: bfloat16 [2048, 512], P('ctx', 'head')
- weight_v_grad: bfloat16 [2048, 512], P('ctx', 'head')
All inputs are finite; a program needn't handle non-finite values.
Results may differ from a plain program's by a relative error of at most 0.0057.
Values may be sent and summed in bfloat16 or wider, within the bound.
No kernel may reach another device: no remote copies, remote signals or barrier semaphores. Data moves between devices by JAX's collectives and lax.ppermute only.
A program may use at most 64 MiB of HBM per device.

v0:
```python
import jax
import jax.numpy as jnp
from jax import lax
from jax.sharding import PartitionSpec as P

E = 128
WINDOW = 256


neg_fill = -1e30


def entering(array, axis, combine, identity):
    size, position = (lax.axis_size(axis), lax.axis_index(axis))
    everything = jax.tree.map(lambda part: lax.all_gather(part, axis), array)
    start = jax.tree.map(
        lambda part, zero: jnp.broadcast_to(jnp.asarray(zero, part.dtype), part.shape),
        array,
        identity,
    )

    def turn(k, before):
        at = size - 1 - k
        reached = at > position
        new = combine(before, jax.tree.map(lambda part: part[at], everything))
        return jax.tree.map(lambda a, b: jnp.where(reached, a, b), new, before)

    return lax.fori_loop(0, size, turn, start)


def shifted(value, axis, steps):
    count = lax.axis_size(axis)
    leading, last = (max(0, -steps), min(count, count - steps))
    return lax.ppermute(value, axis, [(source, source + steps) for source in range(leading, last)])


def band_grads(q_block, h_block, key_rows, value_rows, query_pos, key_pos):
    head_dim = key_rows.shape[1]
    group_size = q_block.shape[1] // head_dim
    row_count = q_block.shape[0]
    q_heads = q_block.reshape(row_count, group_size, head_dim)
    h_heads = h_block.reshape(row_count, group_size, head_dim)
    factor = head_dim ** (-0.5)
    scores = (
        jnp.einsum("trd,jd->rtj", q_heads, key_rows, preferred_element_type=jnp.float32) * factor
    )
    offset = query_pos[:, None] - key_pos[None, :]
    inside = (offset >= 0) & (offset < WINDOW) & (key_pos[None, :] >= 0)
    scores = jnp.where(inside[None], scores, neg_fill)
    row_max = jnp.max(scores, axis=2, keepdims=True)
    expo = jnp.exp(scores - row_max)
    attend = expo / jnp.sum(expo, axis=2, keepdims=True)
    attend_low = attend.astype(jnp.bfloat16)
    dprob = jnp.einsum("trd,jd->rtj", h_heads, value_rows, preferred_element_type=jnp.float32)
    row_delta = jnp.sum(attend * dprob, axis=2, keepdims=True)
    dscore = (attend * (dprob - row_delta)).astype(jnp.bfloat16)
    key_part = (
        jnp.einsum("rtj,trd->jd", dscore, q_heads, preferred_element_type=jnp.float32) * factor
    )
    value_part = jnp.einsum("rtj,trd->jd", attend_low, h_heads, preferred_element_type=jnp.float32)
    return (key_part, value_part)


def linear_terms(q_block, h_block, key_rows, value_rows, log_rates, lin_scale):
    head_dim = key_rows.shape[1]
    group_size = q_block.shape[1] // head_dim
    length = q_block.shape[0]
    q_heads = q_block.reshape(length, group_size, head_dim)
    h_heads = h_block.reshape(length, group_size, head_dim)
    log_sums = jnp.cumsum(log_rates)
    row_after = lax.broadcasted_iota(jnp.int32, (length, length), 0)
    row_before = lax.broadcasted_iota(jnp.int32, (length, length), 1)
    mixing = jnp.exp(
        jnp.where(row_after >= row_before, log_sums[:, None] - log_sums[None, :], neg_fill)
    )
    key_mix = (
        mixing[None]
        * jnp.einsum("trd,jd->rtj", h_heads, value_rows, preferred_element_type=jnp.float32)
    ).astype(jnp.bfloat16)
    value_mix = (
        mixing[None]
        * jnp.einsum("trd,jd->rtj", q_heads, key_rows, preferred_element_type=jnp.float32)
    ).astype(jnp.bfloat16)
    key_part = (
        jnp.einsum("rtj,trd->jd", key_mix, q_heads, preferred_element_type=jnp.float32) * lin_scale
    )
    value_part = (
        jnp.einsum("rtj,trd->jd", value_mix, h_heads, preferred_element_type=jnp.float32)
        * lin_scale
    )
    weighted = (jnp.exp(log_sums)[:, None, None] * h_heads).astype(jnp.bfloat16)
    block_grad = (
        jnp.einsum("trd,tre->de", q_heads, weighted, preferred_element_type=jnp.float32) * lin_scale
    )
    return (
        key_part,
        value_part,
        block_grad,
        jnp.exp(log_sums[-1]),
        jnp.exp(log_sums[-1] - log_sums),
    )


def compose(earlier, later):
    return (later[0] * earlier[0], later[0][:, None, None] * earlier[1] + later[1])


def on_device(layer_input, queries, keys, values, result_cotangent, log_decay):
    length = queries.shape[0]
    head_dim = E
    lin_scale = 1.0 / (32 * head_dim)
    halves = result_cotangent * 0.5
    row_start = lax.axis_index("ctx") * length
    query_pos = row_start + jnp.arange(length, dtype=jnp.int32)
    key_pos = row_start - WINDOW + jnp.arange(length + WINDOW, dtype=jnp.int32)
    linear_parts = [linear_terms(queries, halves, keys, values, log_decay[0], lin_scale)]
    decays = jnp.stack([part[3] for part in linear_parts])
    block_grads = jnp.stack([part[2] for part in linear_parts])
    identity = (jnp.ones_like(decays), jnp.zeros_like(block_grads))
    _, incoming = entering((decays, block_grads), "ctx", compose, identity)
    preceding_keys, prior_v = shifted((keys, values), "ctx", 1)
    full_k = jnp.concatenate([preceding_keys, keys], axis=0)
    full_v = jnp.concatenate([prior_v, values], axis=0)
    band_parts = [band_grads(queries, halves, full_k, full_v, query_pos, key_pos)]
    win_k = jnp.concatenate([part[0] for part in band_parts], axis=1)
    win_v = jnp.concatenate([part[1] for part in band_parts], axis=1)
    back_k, back_v = shifted((win_k[:WINDOW], win_v[:WINDOW]), "ctx", -1)
    win_k = win_k[WINDOW:]
    win_v = win_v[WINDOW:]
    zero_rows = jnp.zeros((length - WINDOW, win_k.shape[1]), jnp.float32)
    win_k = win_k + jnp.concatenate([zero_rows, back_k], axis=0)
    win_v = win_v + jnp.concatenate([zero_rows, back_v], axis=0)
    state_in = incoming[0]
    tail_decay = linear_parts[0][4][:, None]
    lin_keys = linear_parts[0][0] + tail_decay * jnp.dot(
        values.astype(jnp.float32), state_in.T, precision=lax.Precision.HIGHEST
    )
    lin_values = linear_parts[0][1] + tail_decay * jnp.dot(
        keys.astype(jnp.float32), state_in, precision=lax.Precision.HIGHEST
    )
    key_grad = (lin_keys + win_k).astype(jnp.bfloat16)
    value_grad = (lin_values + win_v).astype(jnp.bfloat16)
    both_grads = jnp.concatenate([key_grad, value_grad], axis=1)
    partial_value = lax.dot_general(
        lax.all_gather(layer_input, "head", axis=1, tiled=True),
        both_grads,
        (((0,), (0,)), ((), ())),
        preferred_element_type=jnp.float32,
    )
    owned = lax.psum_scatter(partial_value, "ctx", scatter_dimension=0, tiled=True)
    key_width = key_grad.shape[1]
    return (owned[:, :key_width].astype(jnp.bfloat16), owned[:, key_width:].astype(jnp.bfloat16))


def solution(mesh):
    in_specs = (
        P("ctx", "head"),
        P("ctx", "head"),
        P("ctx", "head"),
        P("ctx", "head"),
        P("ctx", "head"),
        P("head", "ctx"),
    )
    out_specs = (P("ctx", "head"), P("ctx", "head"))
    return jax.shard_map(
        on_device, mesh=mesh, in_specs=in_specs, out_specs=out_specs, check_vma=False
    )
```

profile of v0, /device:TPU:6, one launch (start us, length us, event | category | flops | bytes accessed | tf_op | source)
XLA Modules:
  0.0 861.4 jit_solution(1830601965258238545)
XLA Ops:
  9.6 1.7 fusion.22
  11.4 1.7 collective-permute-start
  13.1 3.8 collective-permute-start.1
  25.1 255.8 %all-reduce = f32[128]{0:T(128)S(1)} all-reduce(f32[128]{0:T(128)S(1)} %dynamic-update-slice), channel_id=1, replica_groups=mesh['ctx'=128,'head'=4] {'ctx'}, use_global_device_ids=true, to_apply=%add | all-reduce | flops 128 | bytes 1024
  282.3 2.2 multiply_reduce_fusion
  284.5 2.0 fusion.12
  290.1 9.0 %copy.50 = f32[16384,128]{1,0:T(8,128)} copy(f32[16384,128]{0,1:T(8,128)} %all-gather.6.cloned.1.call-done) | data formatting | bytes 16777216
  299.1 286.2 %while.16 = (s32[]{:T(128)}, f32[1,128,128]{2,1,0:T(8,128)S(1)}, s32[]{:T(128)}, f32[128,1]{0,1:T(1,128)S(1)}, f32[128,1,128,128]{3,2,1,0:T(8,128)}, /*index=5*/s32[]{:T(128)}, s32[]{:T(128)}, s32[]{:T(128)}, s32[]{:T(128)}) while((s32[]{:T(128)}, f32[1,128,128]{2,1,0:T(8,128)S(1)}, s32[]{:T(128)}, f32[128,1]{0,1:T(1,128)S(1)}, ...), condition=%wide.region_3.4_spmd.clone, body=%wide.region_2.3_spmd.clone.sunk | while | flops 65544 | bytes 196787 | solution.py:28
  299.8 1.5 fusion.99
  302.0 1.5 fusion.99
  304.3 1.5 fusion.99
  306.5 1.5 fusion.99
  308.7 1.5 fusion.99
  311.0 1.5 fusion.99
  313.2 1.5 fusion.99
  315.4 1.5 fusion.99
  322.2 1.5 fusion.99
  353.5 1.5 fusion.99
  364.6 1.5 fusion.99
  395.9 1.5 fusion.99
  407.1 1.5 fusion.99
  438.4 1.5 fusion.99
  449.6 1.5 fusion.99
  480.9 1.5 fusion.99
  492.1 1.5 fusion.99
  523.4 1.5 fusion.99
  534.6 1.5 fusion.99
  565.9 1.5 fusion.99
  577.1 1.5 fusion.99
  585.9 1.7 convolution_bitcast_fusion
  587.6 1.9 copy.51
  589.5 263.2 %reduce-scatter.4.cloned.1.call-done = f32[16,256]{1,0:T(8,128)} async-done(((f32[2048,256]{1,0:T(8,128)}), f32[16,256]{1,0:T(8,128)}) %reduce-scatter.4.cloned.1.call-update) | async-done | bytes 16400
  (287 shorter events, 268.2 us)
Async XLA Ops:
  7.2 277.4 %copy-start = (bf16[256,256]{1,0:T(8,128)(2,1)S(1)}, bf16[256,256]{1,0:T(8,128)(2,1)}, u32[]{:S(2)}) copy-start(bf16[256,256]{1,0:T(8,128)(2,1)} %param.9) | copy-start | bytes 393220
  7.2 277.4 %copy-start.2 = (bf16[256,128]{1,0:T(8,128)(2,1)S(1)}, bf16[256,128]{1,0:T(8,128)(2,1)}, u32[]{:S(2)}) copy-start(bf16[256,128]{1,0:T(8,128)(2,1)} %param.10) | copy-start | bytes 196612
  7.2 282.9 %all-gather.6.cloned.1.call-start = ((), (), s32[]{:S(2)}) async-start(), calls=%async_computation.2 | async-start | bytes 8454144 | tf_op jit(solution)/shard_map/all_gather | solution.py:15
  11.3 574.6 %all-gather.4.cloned.1.call-start = ((), (), s32[]{:S(2)}) async-start(), calls=%async_computation.1 | async-start | bytes 1310720 | tf_op jit(solution)/shard_map/all_gather | solution.py:145
  11.4 269.5 %collective-permute-start = (bf16[256,128]{1,0:T(8,128)(2,1)}, bf16[256,128]{1,0:T(8,128)(2,1)S(1)}, u32[]{:S(2)}, u32[]{:S(2)}) collective-permute-start(bf16[256,128]{1,0:T(8,128)(2,1)} %param.10), channel_id=1, source_target_pairs={{0,4},{4,8},{8,12},{12,16},{16,20},{20,24},{24,28},{28,32},{32,36}... | collective-permute-start | bytes 196616 | tf_op jit(solution)/shard_map/ppermute | solution.py:34
  13.1 269.2 %collective-permute-start.1 = (bf16[256,128]{1,0:T(8,128)(2,1)}, bf16[256,128]{1,0:T(8,128)(2,1)S(1)}, u32[]{:S(2)}, u32[]{:S(2)}) collective-permute-start(bf16[256,128]{1,0:T(8,128)(2,1)} %param.11), channel_id=1, source_target_pairs={{0,4},{4,8},{8,12},{12,16},{16,20},{20,24},{24,28},{28,32},{32,36}... | collective-permute-start | bytes 196616 | tf_op jit(solution)/shard_map/ppermute | solution.py:34
  16.9 835.8 %reduce-scatter.4.cloned.1.call-start = ((), (), s32[]{:S(2)}) async-start(), calls=%async_computation.3 | async-start | bytes 2113536
  286.6 298.8 %collective-permute-start.2 = (f32[256,128]{0,1:T(8,128)S(1)}, f32[256,128]{0,1:T(8,128)S(1)}, u32[]{:S(2)}, u32[]{:S(2)}) collective-permute-start(f32[256,128]{0,1:T(8,128)S(1)} %slice.41), channel_id=1, source_target_pairs={{4,0},{8,4},{12,8},{16,12},{20,16},{24,20},{28,24},{32,28},{36,32}... | collective-permute-start | bytes 393224 | tf_op jit(solution)/shard_map/ppermute | solution.py:34
  288.6 296.7 %copy-start.1 = (bf16[256,128]{1,0:T(8,128)(2,1)S(1)}, bf16[256,128]{1,0:T(8,128)(2,1)}, u32[]{:S(2)}) copy-start(bf16[256,128]{1,0:T(8,128)(2,1)} %param.11) | copy-start | bytes 196612
  288.7 297.0 %collective-permute-start.3 = (f32[256,128]{0,1:T(8,128)S(1)}, f32[256,128]{0,1:T(8,128)S(1)}, u32[]{:S(2)}, u32[]{:S(2)}) collective-permute-start(f32[256,128]{0,1:T(8,128)S(1)} %slice.43), channel_id=1, source_target_pairs={{4,0},{8,4},{12,8},{16,12},{20,16},{24,20},{28,24},{32,28},{36,32}... | collective-permute-start | bytes 393224 | tf_op jit(solution)/shard_map/ppermute | solution.py:34
Sparse Core Ops, SparseCore 0:
  11.4 151.6 all-gather.5
  165.2 24.8 all-gather.3
  589.6 262.9 reduce-scatter.3
where the time goes:
time: 869 us; the launch traced here: 861 us
  waiting for transfers between devices  263 us (30%)
  blocking collectives  256 us (29%)
  other arithmetic  201 us (23%)
  local copies, waits for them, and re-layouts  102 us (12%)
  between operations  14.7 us (2%)
  matrix products  12.9 us (1%)
    unnamed x4, waiting for transfers between devices  263 us
    unnamed x1, blocking collectives  256 us
    select_n x128, other arithmetic, turn(): return jax.tree.map(lambda a, b: jnp.where(reached, a, b), new, before)  198 us
    dynamic_slice x128, local copies, waits for them, and re-layouts, turn(): new = combine(before, jax.tree.map(lambda part: part[at], everything))  85.1 us
  transfers between devices with their start and end apart: 7, of which 1 were waited for; matrix products, arithmetic and copies ran while one was open for 36% of the time, Pallas kernels for 0%

commit v1 on v0

v1 whole, which is shorter than its diff:
```python
import jax
import jax.numpy as jnp
from jax import lax
from jax.sharding import Mesh, PartitionSpec as P

E = 128
WINDOW = 256
NZ, NY, NC = 16, 4, 2
NP = NY * NC

neg_fill = -1e30

PLANE = ("y", "core")
CTX = ("z", "y", "core")


def shifted(value, steps):
    count = NZ * NP
    leading, last = (max(0, -steps), min(count, count - steps))
    return lax.ppermute(value, CTX, [(source, source + steps) for source in range(leading, last)])


def band_grads(q_block, h_block, key_rows, value_rows, query_pos, key_pos):
    head_dim = key_rows.shape[1]
    group_size = q_block.shape[1] // head_dim
    row_count = q_block.shape[0]
    q_heads = q_block.reshape(row_count, group_size, head_dim)
    h_heads = h_block.reshape(row_count, group_size, head_dim)
    factor = head_dim ** (-0.5)
    scores = (
        jnp.einsum("trd,jd->rtj", q_heads, key_rows, preferred_element_type=jnp.float32) * factor
    )
    offset = query_pos[:, None] - key_pos[None, :]
    inside = (offset >= 0) & (offset < WINDOW) & (key_pos[None, :] >= 0)
    scores = jnp.where(inside[None], scores, neg_fill)
    row_max = jnp.max(scores, axis=2, keepdims=True)
    expo = jnp.exp(scores - row_max)
    attend = expo / jnp.sum(expo, axis=2, keepdims=True)
    attend_low = attend.astype(jnp.bfloat16)
    dprob = jnp.einsum("trd,jd->rtj", h_heads, value_rows, preferred_element_type=jnp.float32)
    row_delta = jnp.sum(attend * dprob, axis=2, keepdims=True)
    dscore = (attend * (dprob - row_delta)).astype(jnp.bfloat16)
    key_part = (
        jnp.einsum("rtj,trd->jd", dscore, q_heads, preferred_element_type=jnp.float32) * factor
    )
    value_part = jnp.einsum("rtj,trd->jd", attend_low, h_heads, preferred_element_type=jnp.float32)
    return (key_part, value_part)


def linear_terms(q_block, h_block, key_rows, value_rows, log_rates, lin_scale):
    head_dim = key_rows.shape[1]
    group_size = q_block.shape[1] // head_dim
    length = q_block.shape[0]
    q_heads = q_block.reshape(length, group_size, head_dim)
    h_heads = h_block.reshape(length, group_size, head_dim)
    log_sums = jnp.cumsum(log_rates)
    row_after = lax.broadcasted_iota(jnp.int32, (length, length), 0)
    row_before = lax.broadcasted_iota(jnp.int32, (length, length), 1)
    mixing = jnp.exp(
        jnp.where(row_after >= row_before, log_sums[:, None] - log_sums[None, :], neg_fill)
    )
    key_mix = (
        mixing[None]
        * jnp.einsum("trd,jd->rtj", h_heads, value_rows, preferred_element_type=jnp.float32)
    ).astype(jnp.bfloat16)
    value_mix = (
        mixing[None]
        * jnp.einsum("trd,jd->rtj", q_heads, key_rows, preferred_element_type=jnp.float32)
    ).astype(jnp.bfloat16)
    key_part = (
        jnp.einsum("rtj,trd->jd", key_mix, q_heads, preferred_element_type=jnp.float32) * lin_scale
    )
    value_part = (
        jnp.einsum("rtj,trd->jd", value_mix, h_heads, preferred_element_type=jnp.float32)
        * lin_scale
    )
    weighted = (jnp.exp(log_sums)[:, None, None] * h_heads).astype(jnp.bfloat16)
    block_grad = (
        jnp.einsum("trd,tre->de", q_heads, weighted, preferred_element_type=jnp.float32) * lin_scale
    )
    return (key_part, value_part, block_grad, log_sums)


def between(logs, first):
    count = logs.shape[0]
    i = lax.broadcasted_iota(jnp.int32, (count, count), 0)
    l = lax.broadcasted_iota(jnp.int32, (count, count), 1)
    total = jnp.sum(jnp.where((l > first) & (l < i), logs[None, :], 0.0), axis=1)
    return jnp.where(jnp.arange(count) > first, jnp.exp(total), 0.0)


def state_entering(block_grad, log_total):
    rows = E // NP
    tail = jnp.broadcast_to(log_total, (NP, 8, E))
    sent = jnp.concatenate([block_grad.reshape(NP, rows, E), tail], axis=1)
    got = lax.all_to_all(sent, PLANE, 0, 0, tiled=True)
    grads, logs = got[:, :rows], got[:, rows, 0]
    inner = jnp.stack([between(logs, k) for k in range(-1, NP)])
    own = jnp.einsum("kl,lrd->krd", inner, grads, precision=lax.Precision.HIGHEST)
    plane_log = jnp.sum(logs)
    out = jnp.concatenate([own[0], jnp.broadcast_to(plane_log, (8, E))], axis=0)
    planes = lax.all_to_all(
        jnp.broadcast_to(out[None], (NZ, rows + 8, E)), "z", 0, 0, tiled=True
    )
    weights = between(planes[:, rows, 0], lax.axis_index("z"))
    later = jnp.sum(weights[:, None, None] * planes[:, :rows], axis=0)
    k = lax.broadcasted_iota(jnp.int32, (NP, NP), 0)
    l = lax.broadcasted_iota(jnp.int32, (NP, NP), 1)
    after = jnp.exp(jnp.sum(jnp.where(l > k, logs[None, :], 0.0), axis=1))
    entering = own[1:] + after[:, None, None] * later[None]
    back = lax.all_to_all(entering, PLANE, 0, 0, tiled=True)
    return back.reshape(E, E)


def on_device(layer_input, queries, keys, values, result_cotangent, log_decay):
    length = queries.shape[0]
    head_dim = E
    lin_scale = 1.0 / (32 * head_dim)
    halves = result_cotangent * 0.5
    row_start = lax.axis_index(CTX) * length
    query_pos = row_start + jnp.arange(length, dtype=jnp.int32)
    key_pos = row_start - WINDOW + jnp.arange(length + WINDOW, dtype=jnp.int32)
    inputs = lax.all_gather(layer_input, "head", axis=1, tiled=True)
    prior = shifted(jnp.concatenate([keys, values], axis=1), 1)
    lin_k, lin_v, block_grad, log_sums = linear_terms(
        queries, halves, keys, values, log_decay[0], lin_scale
    )
    state_in = state_entering(block_grad, log_sums[-1])
    full_k = jnp.concatenate([prior[:, :head_dim], keys], axis=0)
    full_v = jnp.concatenate([prior[:, head_dim:], values], axis=0)
    win_k, win_v = band_grads(queries, halves, full_k, full_v, query_pos, key_pos)
    back = shifted(
        jnp.concatenate([win_k[:WINDOW], win_v[:WINDOW]], axis=1).astype(jnp.bfloat16), -1
    ).astype(jnp.float32)
    tail_decay = jnp.exp(log_sums[-1] - log_sums)[:, None]
    state_low = state_in.astype(jnp.bfloat16)
    lin_k = lin_k + tail_decay * lax.dot_general(
        values, state_low, (((1,), (1,)), ((), ())), preferred_element_type=jnp.float32
    )
    lin_v = lin_v + tail_decay * jnp.dot(keys, state_low, preferred_element_type=jnp.float32)
    key_grad = (lin_k + win_k[WINDOW:] + back[:, :head_dim]).astype(jnp.bfloat16)
    value_grad = (lin_v + win_v[WINDOW:] + back[:, head_dim:]).astype(jnp.bfloat16)
    both_grads = jnp.concatenate([key_grad, value_grad], axis=1)
    partial_value = lax.dot_general(
        inputs,
        both_grads,
        (((0,), (0,)), ((), ())),
        preferred_element_type=jnp.float32,
    ).astype(jnp.bfloat16)
    width = 2 * head_dim
    rows = partial_value.shape[0] // (NZ * NP)
    parts = partial_value.reshape(NZ, NP, rows, width).transpose(1, 0, 2, 3)
    parts = lax.all_to_all(parts, PLANE, 0, 0, tiled=True)
    parts = jnp.sum(parts.astype(jnp.float32), axis=0).astype(jnp.bfloat16)
    parts = lax.all_to_all(parts, "z", 0, 0, tiled=True)
    owned = jnp.sum(parts.astype(jnp.float32), axis=0)
    return (owned[:, :head_dim].astype(jnp.bfloat16), owned[:, head_dim:].astype(jnp.bfloat16))


def solution(mesh):
    fine = Mesh(mesh.devices.reshape(NZ, NY, NC, mesh.devices.shape[1]), CTX + ("head",))
    rows = P(CTX, "head")
    in_specs = (rows, rows, rows, rows, rows, P("head", CTX))
    return jax.shard_map(
        on_device, mesh=fine, in_specs=in_specs, out_specs=(rows, rows), check_vma=False
    )
```

time: 869 us -> 117 us (0.13)
  waiting for transfers between devices: 263 us -> 16.8 us
  blocking collectives: 256 us -> 38.3 us
  other arithmetic: 201 us -> 3.61 us
  local copies, waits for them, and re-layouts: 102 us -> 7.51 us
  starting transfers between devices: 8.35 us -> 26.8 us
    unnamed x4 -> x1, waiting for transfers between devices: 263 us -> 0.02 us
    unnamed x1 -> x0, blocking collectives: 256 us -> none
    select_n x128 -> x10, other arithmetic: 198 us -> 0.05 us  [between(): return jnp.where(jnp.arange(count) > first, jnp.exp(total), 0.0)]
    dynamic_slice x128 -> x0, local copies, waits for them, and re-layouts: 85.1 us -> none  [turn(): new = combine(before, jax.tree.map(lambda part: part[at], everything))]
    all_to_all x0 -> x2, blocking collectives: none -> 38.3 us  [the longest x1 19.9 us: on_device(): parts = lax.all_to_all(parts, 'z', 0, 0, tiled=True)]
    all_to_all x0 -> x3, starting transfers between devices: none -> 23 us  [the longest x1 15.2 us: state_entering(): lax.all_to_all(jnp.broadcast_to(out[None], (NZ, rows + 8, E)), 'z', 0, 0,...]
    all_to_all x0 -> x3, waiting for transfers between devices: none -> 16.7 us  [the longest x1 10.4 us: state_entering(): lax.all_to_all(jnp.broadcast_to(out[None], (NZ, rows + 8, E)), 'z', 0, 0,...]
    unnamed x14 -> x8, local copies, waits for them, and re-layouts: 15.1 us -> 0.02 us
  transfers between devices with their start and end apart: 7 -> 6, of which waited for: 1 -> 3; matrix products, arithmetic and copies ran while one was open for 36% -> 10% of each run, Pallas kernels for 0% -> 0%
where the time goes in v1:
time: 117 us; the launch traced here: 116 us
  blocking collectives  38.3 us (33%)
  starting transfers between devices  26.8 us (23%)
  waiting for transfers between devices  16.8 us (14%)
  between operations  14.5 us (12%)
  matrix products  8.96 us (8%)
  local copies, waits for them, and re-layouts  7.51 us (6%)
  other arithmetic  3.61 us (3%)
    all_to_all x1, blocking collectives, on_device(): parts = lax.all_to_all(parts, 'z', 0, 0, tiled=True)  19.9 us
    all_to_all x1, blocking collectives, on_device(): parts = lax.all_to_all(parts, PLANE, 0, 0, tiled=True)  18.4 us
    all_to_all x1, starting transfers between devices, state_entering(): lax.all_to_all(jnp.broadcast_to(out[None], (NZ, rows + 8, E)), 'z', 0, 0,...  15.2 us
    all_to_all x1, waiting for transfers between devices, state_entering(): lax.all_to_all(jnp.broadcast_to(out[None], (NZ, rows + 8, E)), 'z', 0, 0,...  10.4 us
    all_to_all x1, waiting for transfers between devices, state_entering(): back = lax.all_to_all(entering, PLANE, 0, 0, tiled=True)  4.67 us
    all_to_all x1, starting transfers between devices, state_entering(): got = lax.all_to_all(sent, PLANE, 0, 0, tiled=True)  4.47 us
    ppermute x2, starting transfers between devices, shifted(): lax.ppermute(value, CTX, [(source, source + steps) for source in range(le...  3.79 us
    all_to_all x1, starting transfers between devices, state_entering(): back = lax.all_to_all(entering, PLANE, 0, 0, tiled=True)  3.33 us
  transfers between devices with their start and end apart: 6, of which 3 were waited for; matrix products, arithmetic and copies ran while one was open for 10% of the time, Pallas kernels for 0%

profile of v1, /device:TPU:6, one launch (start us, length us, event | category | flops | bytes accessed | tf_op | source)
XLA Modules:
  0.0 116.4 jit_solution(14168107579116000794)
XLA Ops:
  7.2 1.0 reduce-window.9
  8.5 0.6 slice.65
  9.1 1.0 copy.177
  10.1 1.2 fusion.23
  11.3 1.3 %concatenate.22 = f32[8,24,128]{2,1,0:T(8,128)} pad(f32[8,16,128]{2,1,0:T(8,128)S(1)} %bitcast.223, f32[]{:T(128)} %bitcast.5), padding=0_0x0_8x0_0 | pad | bytes 163844 | tf_op jit(solution)/shard_map/concatenate | solution.py:95
  12.6 4.5 %all-to-all-start = ((f32[8,24,128]{2,1,0:T(8,128)}), f32[8,24,128]{2,1,0:T(8,128)S(1)}, u32[]{:S(2)}, u32[]{:S(2)}) async-start(f32[8,24,128]{2,1,0:T(8,128)} %concatenate.22), calls=%async_computation | async-start | bytes 196608 | tf_op jit(solution)/shard_map/all_to_all | solution.py:96
  17.2 2.5 %collective-permute-start = (bf16[256,256]{1,0:T(8,128)(2,1)S(1)}, bf16[256,256]{1,0:T(8,128)(2,1)S(1)}, u32[]{:S(2)}, u32[]{:S(2)}) collective-permute-start(bf16[256,256]{1,0:T(8,128)(2,1)S(1)} %pad_maximum_fusion), channel_id=1, source_target_pairs={{0,4},{4,8},{8,12},{12,16},{16,20},{20,24},{24,28},{28,32},{32,36}... | collective-permute-start | bytes 393224 | tf_op jit(solution)/shard_map/ppermute | solution.py:20
  20.0 0.4 fusion.22
  20.6 0.4 fusion.21
  21.0 0.2 fusion.27
  21.2 1.7 %all-to-all-done = f32[8,24,128]{2,1,0:T(8,128)S(1)} async-done(((f32[8,24,128]{2,1,0:T(8,128)}), f32[8,24,128]{2,1,0:T(8,128)S(1)}, u32[]{:S(2)}, u32[]{:S(2)}) %all-to-all-start) | async-done | bytes 98336 | tf_op jit(solution)/shard_map/all_to_all | solution.py:96
  22.9 0.6 slice_reduce_fusion.1
  23.5 0.3 select_reduce_fusion.1
  24.7 0.3 fusion.61
  25.0 0.6 concatenate.23
  25.7 0.7 broadcast_in_dim.125
  26.4 15.2 %all-to-all-start.1 = ((f32[16,24,128]{2,1,0:T(8,128)}), f32[16,24,128]{2,1,0:T(8,128)S(1)}, u32[]{:S(2)}, u32[]{:S(2)}) async-start(f32[16,24,128]{2,1,0:T(8,128)} %broadcast_in_dim.125), calls=%async_computation.1 | async-start | bytes 393216 | tf_op jit(solution)/shard_map/all_to_all | solution.py:102
  41.6 0.5 fusion.108
  42.1 1.3 %multiply_reduce_fusion = (f32[2,256]{1,0:T(2,128)S(1)}, f32[2,256,512]{1,2,0:T(8,128)}) fusion(f32[2,256,512]{1,2,0:T(8,128)S(1)} %get-tuple-element.21, f32[2,256]{1,0:T(2,128)S(1)} %get-tuple-element.20, bf16[256,128]{1,0:T(8,128)(2,1)S(1)} %copy-done, bf16[256,128]{1,0:T(8,128)(2,1)S(1)} %get-tuple-element.16, bf16[256,256]{1,0:T(8,128)(2,1)S(1)} %copy-done.3), kind=kOutput, calls=%fused_computation.35 | convolution fusion | flops 68222464 | bytes 2363392 | tf_op jit(solution)/shard_map/trd,jd->rtj/dot_general | solution.py:40
  43.5 2.0 %fusion.12 = f32[512,128]{0,1:T(8,128)S(1)} fusion(bf16[256,2,128]{0,2,1:T(8,128)(2,1)S(1)} %bitcast.220, f32[2,256,512]{1,2,0:T(8,128)} %get-tuple-element.23, f32[2,256]{1,0:T(2,128)S(1)} %get-tuple-element.22, f32[2,256]{1,0:T(2,128)S(1)} %get-tuple-element.20, pred[256,512]{0,1:T(8,128)(4,1)S(1)} %fusion.27, bf16[256,128]{1,0:T(8,128)(2,1)S(1)} %copy-done.1, ...), kind=kOutput, calls=%fused_computation.19 | convolution fusion | flops 136381440 | bytes 1839104 | tf_op jit(solution)/shard_map/rtj,trd->jd/dot_general | solution.py:44
  45.5 0.7 convolution_bitcast_fusion.2
  46.3 1.3 %collective-permute-start.1 = (bf16[256,256]{0,1:T(8,128)(2,1)S(1)}, bf16[256,256]{0,1:T(8,128)(2,1)S(1)}, u32[]{:S(2)}, u32[]{:S(2)}) collective-permute-start(bf16[256,256]{0,1:T(8,128)(2,1)S(1)} %pad_maximum_fusion.1), channel_id=1, source_target_pairs={{4,0},{8,4},{12,8},{16,12},{20,16},{24,20},{28,24},{32,28},{36,32}... | collective-permute-start | bytes 393224 | tf_op jit(solution)/shard_map/ppermute | solution.py:20
  47.6 10.4 %all-to-all-done.1 = f32[16,24,128]{2,1,0:T(8,128)S(1)} async-done(((f32[16,24,128]{2,1,0:T(8,128)}), f32[16,24,128]{2,1,0:T(8,128)S(1)}, u32[]{:S(2)}, u32[]{:S(2)}) %all-to-all-start.1) | async-done | bytes 196640 | tf_op jit(solution)/shard_map/all_to_all | solution.py:102
  58.5 0.6 copy.114
  59.1 3.3 %all-to-all-start.2 = ((bf16[8,16,128]{2,1,0:T(8,128)(2,1)}), bf16[8,16,128]{2,1,0:T(8,128)(2,1)S(1)}, u32[]{:S(2)}, u32[]{:S(2)}) async-start(bf16[8,16,128]{2,1,0:T(8,128)(2,1)} %copy.114), calls=%async_computation.2 | async-start | bytes 65536 | tf_op jit(solution)/shard_map/all_to_all | solution.py:111
  62.4 0.7 subtract_exponential_fusion
  63.1 4.7 %all-to-all-done.2 = bf16[8,16,128]{2,1,0:T(8,128)(2,1)S(1)} async-done(((bf16[8,16,128]{2,1,0:T(8,128)(2,1)}), bf16[8,16,128]{2,1,0:T(8,128)(2,1)S(1)}, u32[]{:S(2)}, u32[]{:S(2)}) %all-to-all-start.2) | async-done | bytes 32800 | tf_op jit(solution)/shard_map/all_to_all | solution.py:111
  68.2 1.7 %fusion.1 = bf16[2048,256]{0,1:T(8,128)(2,1)S(1)} fusion(bf16[256,2048]{1,0:T(8,128)(2,1)} %all-gather.2.cloned.1.call-done, bf16[256,128]{0,1:T(8,128)(2,1)S(1)} %fusion.39, bf16[256,128]{0,1:T(8,128)(2,1)S(1)} %fusion.40), kind=kOutput, calls=%fused_computation.2 | convolution fusion | flops 269221888 | bytes 2228224 | tf_op jit(solution)/shard_map/dot_general | solution.py:144
  69.9 0.5 copy.125
  70.5 18.4 %all_to_all.25 = bf16[8,16,16,256]{3,2,1,0:T(8,128)(2,1)S(1)} all-to-all(bf16[8,16,16,256]{3,2,1,0:T(8,128)(2,1)S(1)} %copy.126), channel_id=1, replica_groups=mesh['z'=16,'y'=4,'core'=2,'head'=4] {'y','core'}, dimensions={0} | all-to-all | bytes 2097152 | tf_op jit(solution)/shard_map/all_to_all | solution.py:153
  89.1 19.9 %all_to_all.26 = bf16[16,16,256]{2,1,0:T(8,128)(2,1)S(1)} all-to-all(bf16[16,16,256]{2,1,0:T(8,128)(2,1)S(1)} %reduce_sum.171), channel_id=1, replica_groups=mesh['z'=16,'y'=4,'core'=2,'head'=4] {'z'}, dimensions={0} | all-to-all | bytes 262144 | tf_op jit(solution)/shard_map/all_to_all | solution.py:155
  109.0 0.6 fusion.107
  (75 shorter events, 2.9 us)
Async XLA Ops:
  7.2 12.8 %copy-start.3 = (bf16[256,256]{1,0:T(8,128)(2,1)S(1)}, bf16[256,256]{1,0:T(8,128)(2,1)}, u32[]{:S(2)}) copy-start(bf16[256,256]{1,0:T(8,128)(2,1)} %param.10) | copy-start | bytes 393220
  7.2 9.9 %copy-start.1 = (bf16[256,128]{1,0:T(8,128)(2,1)S(1)}, bf16[256,128]{1,0:T(8,128)(2,1)}, u32[]{:S(2)}) copy-start(bf16[256,128]{1,0:T(8,128)(2,1)} %param.8) | copy-start | bytes 196612
  7.2 9.9 %copy-start = (bf16[256,128]{1,0:T(8,128)(2,1)S(1)}, bf16[256,128]{1,0:T(8,128)(2,1)}, u32[]{:S(2)}) copy-start(bf16[256,128]{1,0:T(8,128)(2,1)} %param.9) | copy-start | bytes 196612
  12.6 10.3 %all-to-all-start = ((f32[8,24,128]{2,1,0:T(8,128)}), f32[8,24,128]{2,1,0:T(8,128)S(1)}, u32[]{:S(2)}, u32[]{:S(2)}) async-start(f32[8,24,128]{2,1,0:T(8,128)} %concatenate.22), calls=%async_computation | async-start | bytes 196608 | tf_op jit(solution)/shard_map/all_to_all | solution.py:96
  17.1 3.5 %copy-start.2 = (bf16[256,256]{1,0:T(8,128)(2,1)S(1)}, bf16[256,256]{1,0:T(8,128)(2,1)}, u32[]{:S(2)}) copy-start(bf16[256,256]{1,0:T(8,128)(2,1)} %param.7) | copy-start | bytes 393220
  17.1 51.2 %all-gather.2.cloned.1.call-start = ((), (), s32[]{:S(2)}) async-start(), calls=%async_computation.5 | async-start | bytes 1310720 | tf_op jit(solution)/shard_map/all_gather | solution.py:123
  17.2 24.4 %collective-permute-start = (bf16[256,256]{1,0:T(8,128)(2,1)S(1)}, bf16[256,256]{1,0:T(8,128)(2,1)S(1)}, u32[]{:S(2)}, u32[]{:S(2)}) collective-permute-start(bf16[256,256]{1,0:T(8,128)(2,1)S(1)} %pad_maximum_fusion), channel_id=1, source_target_pairs={{0,4},{4,8},{8,12},{12,16},{16,20},{20,24},{24,28},{28,32},{32,36}... | collective-permute-start | bytes 393224 | tf_op jit(solution)/shard_map/ppermute | solution.py:20
  26.4 31.6 %all-to-all-start.1 = ((f32[16,24,128]{2,1,0:T(8,128)}), f32[16,24,128]{2,1,0:T(8,128)S(1)}, u32[]{:S(2)}, u32[]{:S(2)}) async-start(f32[16,24,128]{2,1,0:T(8,128)} %broadcast_in_dim.125), calls=%async_computation.1 | async-start | bytes 393216 | tf_op jit(solution)/shard_map/all_to_all | solution.py:102
  46.3 16.8 %collective-permute-start.1 = (bf16[256,256]{0,1:T(8,128)(2,1)S(1)}, bf16[256,256]{0,1:T(8,128)(2,1)S(1)}, u32[]{:S(2)}, u32[]{:S(2)}) collective-permute-start(bf16[256,256]{0,1:T(8,128)(2,1)S(1)} %pad_maximum_fusion.1), channel_id=1, source_target_pairs={{4,0},{8,4},{12,8},{16,12},{20,16},{24,20},{28,24},{32,28},{36,32}... | collective-permute-start | bytes 393224 | tf_op jit(solution)/shard_map/ppermute | solution.py:20
  59.1 8.7 %all-to-all-start.2 = ((bf16[8,16,128]{2,1,0:T(8,128)(2,1)}), bf16[8,16,128]{2,1,0:T(8,128)(2,1)S(1)}, u32[]{:S(2)}, u32[]{:S(2)}) async-start(bf16[8,16,128]{2,1,0:T(8,128)(2,1)} %copy.114), calls=%async_computation.2 | async-start | bytes 65536 | tf_op jit(solution)/shard_map/all_to_all | solution.py:111
Sparse Core Ops, SparseCore 0:
  20.0 35.4 all-gather.1

commit v2 on v1

v2 whole, which is shorter than its diff:
```python
import jax
import jax.numpy as jnp
from jax import lax
from jax.experimental import pallas as pl
from jax.experimental.pallas import tpu as pltpu
from jax.sharding import Mesh, PartitionSpec as P

E = 128
LEN = 256
NZ, NY, NC = 16, 4, 2
NP = NY * NC
NH = 4
XD = 512
ROWS = E // NP
LIN = 1.0 / (32 * E)
FACTOR = E ** (-0.5)
F32, BF16 = jnp.float32, jnp.bfloat16

neg_fill = -1e30

PLANE = ("y", "core")
CTX = ("z", "y", "core")

NN = (((1,), (0,)), ((), ()))
NT = (((1,), (1,)), ((), ()))
TN = (((0,), (0,)), ((), ()))


def mm(a, b, dims):
    return lax.dot_general(a, b, dims, preferred_element_type=F32)


def vmem(count):
    return [pl.BlockSpec(memory_space=pltpu.VMEM)] * count


SMEM = pl.BlockSpec(memory_space=pltpu.SMEM)


def cost(flops, nbytes):
    return pl.CostEstimate(flops=flops, bytes_accessed=nbytes, transcendentals=0)


def params(mib):
    return pltpu.CompilerParams(vmem_limit_bytes=mib << 20)


def log_sums(ld):
    t = lax.broadcasted_iota(jnp.int32, (LEN, LEN), 0)
    u = lax.broadcasted_iota(jnp.int32, (LEN, LEN), 1)
    column = jnp.sum(jnp.where(u <= t, ld, 0.0), axis=1, keepdims=True)
    row = jnp.sum(jnp.where(u == t, column, 0.0), axis=0, keepdims=True)
    return column, row


def summary_kernel(q_ref, c_ref, ld_ref, out_ref):
    column, _ = log_sums(ld_ref[...])
    grow = jnp.exp(column)
    total = jnp.zeros((E, E), F32)
    for r in range(2):
        cols = slice(r * E, (r + 1) * E)
        half = c_ref[:, cols].astype(F32) * 0.5
        total += mm(q_ref[:, cols], (grow * half).astype(BF16), TN)
    last = jnp.broadcast_to(column[LEN - 1 :, :], (8, E))
    for m in range(NP):
        out_ref[m, :ROWS, :] = total[m * ROWS : (m + 1) * ROWS] * LIN
        out_ref[m, ROWS:, :] = last


def summary(q, c, ld):
    return pl.pallas_call(
        summary_kernel,
        out_shape=jax.ShapeDtypeStruct((NP, ROWS + 8, E), F32),
        in_specs=vmem(3),
        out_specs=vmem(1)[0],
        cost_estimate=cost(2 * LEN * E * E * 2, 400000),
        compiler_params=params(8),
        name="summary",
    )(q, c, ld)


def local_kernel(idx_ref, q_ref, c_ref, k_ref, v_ref, prior_ref, ld_ref, own_ref, back_ref):
    column, row = log_sums(ld_ref[...])
    j = lax.broadcasted_iota(jnp.int32, (LEN, LEN), 0)
    t = lax.broadcasted_iota(jnp.int32, (LEN, LEN), 1)
    inside = j <= t
    mixing = jnp.exp(jnp.where(inside, row - column, neg_fill))
    outside = jnp.where(idx_ref[0] > 0, 0.0, neg_fill)
    k, v = k_ref[...], v_ref[...]
    prior_k, prior_v = prior_ref[:, :E], prior_ref[:, E:]
    own_k, own_v = jnp.zeros((LEN, E), F32), jnp.zeros((LEN, E), F32)
    win_k, win_v = jnp.zeros((LEN, E), F32), jnp.zeros((LEN, E), F32)
    old_k, old_v = jnp.zeros((LEN, E), F32), jnp.zeros((LEN, E), F32)
    zero = jnp.zeros((LEN, LEN), BF16)
    for r in range(2):
        cols = slice(r * E, (r + 1) * E)
        q = q_ref[:, cols]
        half = (c_ref[:, cols].astype(F32) * 0.5).astype(BF16)
        raw = mm(k, q, NT)
        prod = mm(v, half, NT)
        scores = jnp.where(inside, raw * FACTOR, mm(prior_k, q, NT) * FACTOR + outside)
        dprob = jnp.where(inside, prod, mm(prior_v, half, NT))
        expo = jnp.exp(scores - jnp.max(scores, axis=0, keepdims=True))
        attend = expo / jnp.sum(expo, axis=0, keepdims=True)
        delta = jnp.sum(attend * dprob, axis=0, keepdims=True)
        dscore = (attend * (dprob - delta)).astype(BF16)
        low = attend.astype(BF16)
        own_k += mm((mixing * prod).astype(BF16), q, NN)
        own_v += mm((mixing * raw).astype(BF16), half, NN)
        win_k += mm(jnp.where(inside, dscore, zero), q, NN)
        win_v += mm(jnp.where(inside, low, zero), half, NN)
        old_k += mm(jnp.where(inside, zero, dscore), q, NN)
        old_v += mm(jnp.where(inside, zero, low), half, NN)
    own_ref[:, :E] = own_k * LIN + win_k * FACTOR
    own_ref[:, E:] = own_v * LIN + win_v
    back_ref[:, :E] = old_k * FACTOR
    back_ref[:, E:] = old_v


def local(idx, q, c, k, v, prior, ld):
    shape = jax.ShapeDtypeStruct((LEN, 2 * E), F32)
    return pl.pallas_call(
        local_kernel,
        out_shape=(shape, shape),
        in_specs=[SMEM] + vmem(6),
        out_specs=tuple(vmem(2)),
        cost_estimate=cost(2 * 20 * LEN * LEN * E, 1200000),
        compiler_params=params(16),
        name="local",
    )(idx, q, c, k, v, prior, ld)


def plane_kernel(got_ref, out_ref):
    log = jnp.zeros((8, E), F32)
    low, high = jnp.zeros((8, E), F32), jnp.zeros((8, E), F32)
    for k in range(NP):
        weight = jnp.exp(log)
        low += weight * got_ref[k, 0:8, :]
        high += weight * got_ref[k, 8:16, :]
        log += got_ref[k, ROWS:, :]
    for z in range(NZ):
        out_ref[z, 0:8, :] = low
        out_ref[z, 8:16, :] = high
        out_ref[z, ROWS:, :] = log


def plane_total(got):
    return pl.pallas_call(
        plane_kernel,
        out_shape=jax.ShapeDtypeStruct((NZ, ROWS + 8, E), F32),
        in_specs=vmem(1),
        out_specs=vmem(1)[0],
        cost_estimate=cost(0, 300000),
        compiler_params=params(4),
        name="plane_total",
    )(got)


def enter_kernel(idx_ref, got_ref, planes_ref, out_ref):
    mine = idx_ref[1]
    log = jnp.zeros((8, E), F32)
    low, high = jnp.zeros((8, E), F32), jnp.zeros((8, E), F32)
    for z in range(NZ):
        later = z > mine
        weight = jnp.where(later, jnp.exp(log), 0.0)
        low += weight * planes_ref[z, 0:8, :]
        high += weight * planes_ref[z, 8:16, :]
        log += jnp.where(later, planes_ref[z, ROWS:, :], 0.0)
    for k in range(NP - 1, -1, -1):
        out_ref[k, 0:8, :] = low
        out_ref[k, 8:16, :] = high
        decay = jnp.exp(got_ref[k, ROWS:, :])
        low = got_ref[k, 0:8, :] + decay * low
        high = got_ref[k, 8:16, :] + decay * high


def enter(idx, got, planes):
    return pl.pallas_call(
        enter_kernel,
        out_shape=jax.ShapeDtypeStruct((NP, ROWS, E), F32),
        in_specs=[SMEM] + vmem(2),
        out_specs=vmem(1)[0],
        cost_estimate=cost(0, 400000),
        compiler_params=params(4),
        name="enter",
    )(idx, got, planes)


def weight_kernel(
    idx_ref, state_ref, own_ref, back_ref, k_ref, v_ref, ld_ref, *refs
):
    x_refs, (keep_ref, send_ref, part) = refs[:NH], refs[NH:]
    column, _ = log_sums(ld_ref[...])
    tail = jnp.exp(column[LEN - 1 :, :] - column)
    state = state_ref[...].reshape(E, E)
    high = state.astype(BF16)
    low = (state - high.astype(F32)).astype(BF16)
    k, v = k_ref[...], v_ref[...]
    far_k = mm(v, high, NT) + mm(v, low, NT)
    far_v = mm(k, high, NN) + mm(k, low, NN)
    key_grad = (own_ref[:, :E] + back_ref[:, :E] + tail * far_k).astype(BF16)
    value_grad = (own_ref[:, E:] + back_ref[:, E:] + tail * far_v).astype(BF16)
    grad = jnp.concatenate([key_grad, value_grad], axis=1)
    core, head = idx_ref[2], idx_ref[3]
    for i in range(NH):
        found = mm(x_refs[i][...], grad, TN).reshape(NH, NY, NC, 16, 2 * E)
        for y in range(NY):
            for c in range(NC):
                part[c, y] = found[:, y, c]
        where = pl.ds(lax.rem(head + NH - i, NH) * NH, NH)
        keep_ref[:, where] = part[core]
        send_ref[:, where] = part[1 - core].astype(BF16)


def weight_parts(idx, state, own, back, k, v, ld, xs):
    whole = (NY, NZ, 16, 2 * E)
    return pl.pallas_call(
        weight_kernel,
        out_shape=(jax.ShapeDtypeStruct(whole, F32), jax.ShapeDtypeStruct(whole, BF16)),
        in_specs=[SMEM] + vmem(6 + NH),
        out_specs=tuple(vmem(2)),
        scratch_shapes=[pltpu.VMEM((NC, NY, NH, 16, 2 * E), F32)],
        cost_estimate=cost(2 * NH * XD * LEN * 2 * E, 3500000),
        compiler_params=params(16),
        name="weight_parts",
    )(idx, state, own, back, k, v, ld, *xs)


def merge_kernel(keep_ref, other_ref, out_ref):
    out_ref[...] = (keep_ref[...] + other_ref[...].astype(F32)).astype(BF16)


def merge(keep, other):
    return pl.pallas_call(
        merge_kernel,
        out_shape=jax.ShapeDtypeStruct(other.shape, BF16),
        in_specs=vmem(2),
        out_specs=vmem(1)[0],
        cost_estimate=cost(0, 2000000),
        compiler_params=params(8),
        name="merge",
    )(keep, other)


def fold_kernel(parts_ref, out_ref):
    total = parts_ref[0].astype(F32)
    for y in range(1, NY):
        total += parts_ref[y].astype(F32)
    out_ref[...] = total.astype(BF16)


def fold(parts):
    return pl.pallas_call(
        fold_kernel,
        out_shape=jax.ShapeDtypeStruct(parts.shape[1:], BF16),
        in_specs=vmem(1),
        out_specs=vmem(1)[0],
        cost_estimate=cost(0, 700000),
        compiler_params=params(8),
        name="fold",
    )(parts)


def finish_kernel(parts_ref, key_ref, value_ref):
    total = parts_ref[0].astype(F32)
    for z in range(1, NZ):
        total += parts_ref[z].astype(F32)
    key_ref[...] = total[:, :E].astype(BF16)
    value_ref[...] = total[:, E:].astype(BF16)


def finish(parts):
    shape = jax.ShapeDtypeStruct((16, E), BF16)
    return pl.pallas_call(
        finish_kernel,
        out_shape=(shape, shape),
        in_specs=vmem(1),
        out_specs=tuple(vmem(2)),
        cost_estimate=cost(0, 150000),
        compiler_params=params(4),
        name="finish",
    )(parts)


def shifted(value, steps):
    count = NZ * NP
    leading, last = (max(0, -steps), min(count, count - steps))
    return lax.ppermute(value, CTX, [(source, source + steps) for source in range(leading, last)])


def on_device(layer_input, queries, keys, values, result_cotangent, log_decay):
    axes = (CTX, "z", "core", "head")
    idx = jnp.stack([lax.axis_index(axis) for axis in axes]).astype(jnp.int32)
    got = lax.all_to_all(summary(queries, result_cotangent, log_decay), PLANE, 0, 0, tiled=True)
    prior = shifted(jnp.concatenate([keys, values], axis=1), 1)
    xs = [layer_input] + [
        lax.ppermute(layer_input, "head", [(i, (i + s) % NH) for i in range(NH)])
        for s in range(1, NH)
    ]
    planes = lax.all_to_all(plane_total(got), "z", 0, 0, tiled=True)
    own, old = local(idx, queries, result_cotangent, keys, values, prior, log_decay)
    back = shifted(old, -1)
    state = lax.all_to_all(enter(idx, got, planes), PLANE, 0, 0, tiled=True)
    keep, send = weight_parts(idx, state, own, back, keys, values, log_decay, xs)
    other = lax.ppermute(send, "core", [(0, 1), (1, 0)])
    parts = fold(lax.all_to_all(merge(keep, other), "y", 0, 0, tiled=True))
    return finish(lax.all_to_all(parts, "z", 0, 0, tiled=True))


def solution(mesh):
    fine = Mesh(mesh.devices.reshape(NZ, NY, NC, NH), CTX + ("head",))
    rows = P(CTX, "head")
    in_specs = (rows, rows, rows, rows, rows, P("head", CTX))
    return jax.shard_map(
        on_device, mesh=fine, in_specs=in_specs, out_specs=(rows, rows), check_vma=False
    )
```

time: 117 us -> 106 us (0.906)
  the two profiles are of different devices: /device:TPU:6 before, /device:TPU:32 now
where the time goes in v2:
time: 106 us
  blocking collectives  49.1 us (46%)
  starting transfers between devices  39.6 us (37%)
  waiting for transfers between devices  7.39 us (7%)
  Pallas kernels  5.86 us (6%)
  local copies, waits for them, and re-layouts  3.09 us (3%)
    all_to_all x1, blocking collectives, on_device(): return finish(lax.all_to_all(parts, 'z', 0, 0, tiled=True))  26.5 us
    all_to_all x1, starting transfers between devices, on_device(): planes = lax.all_to_all(plane_total(got), 'z', 0, 0, tiled=True)  15.3 us
    all_to_all x1, blocking collectives, on_device(): parts = fold(lax.all_to_all(merge(keep, other), 'y', 0, 0, tiled=True))  12.5 us
    ppermute x3, starting transfers between devices, on_device(): lax.ppermute(layer_input, 'head', [(i, (i + s) % NH) for i in range(NH)])  12 us
    all_to_all x1, blocking collectives, on_device(): lax.all_to_all(summary(queries, result_cotangent, log_decay), PLANE, 0, 0...  10.1 us
    ppermute x2, starting transfers between devices, shifted(): lax.ppermute(value, CTX, [(source, source + steps) for source in range(le...  6.97 us
    all_to_all x1, waiting for transfers between devices, on_device(): state = lax.all_to_all(enter(idx, got, planes), PLANE, 0, 0, tiled=True)  5.5 us
    all_to_all x1, starting transfers between devices, on_device(): state = lax.all_to_all(enter(idx, got, planes), PLANE, 0, 0, tiled=True)  3.35 us
  transfers between devices with their start and end apart: 8, of which 2 were waited for; matrix products, arithmetic and copies ran while one was open for 0% of the time, Pallas kernels for 3%

profile of v2, /device:TPU:32, one launch (start us, length us, event | category | flops | bytes accessed | tf_op | source)
XLA Modules:
  0.0 105.9 jit_solution(461654742401517715)
XLA Ops:
  0.6 0.0 copy-start.3
  0.6 0.9 copy-done.3
  1.5 0.9 copy-done.5
  2.4 0.7 copy-done.7
  3.1 0.3 summary.1
  3.4 10.1 %all_to_all.25.got_ref = f32[8,24,128]{2,1,0:T(8,128)S(1)} all-to-all(f32[8,24,128]{2,1,0:T(8,128)S(1)} %summary.1), channel_id=1, replica_groups=mesh['z'=16,'y'=4,'core'=2,'head'=4] {'y','core'}, dimensions={0} | all-to-all | bytes 196608 | tf_op jit(solution)/shard_map/all_to_all | solution.py:294
  13.5 0.7 plane_total.1
  14.2 15.3 %all-to-all-start.1 = ((f32[16,24,128]{2,1,0:T(8,128)}), f32[16,24,128]{2,1,0:T(8,128)S(1)}, u32[]{:S(2)}, u32[]{:S(2)}) async-start(f32[16,24,128]{2,1,0:T(8,128)} %plane_total.1), calls=%async_computation.1 | async-start | bytes 393216 | tf_op jit(solution)/shard_map/all_to_all | solution.py:300
  29.5 0.0 copy-start.4
  29.5 0.0 copy-start.6
  29.6 2.1 %collective-permute-start = (bf16[256,256]{1,0:T(8,128)(2,1)S(1)}, bf16[256,256]{1,0:T(8,128)(2,1)S(1)}, u32[]{:S(2)}, u32[]{:S(2)}) collective-permute-start(bf16[256,256]{1,0:T(8,128)(2,1)S(1)} %pad_maximum_fusion), channel_id=1, source_target_pairs={{0,4},{4,8},{8,12},{12,16},{16,20},{20,24},{24,28},{28,32},{32,36}... | collective-permute-start | bytes 393224 | tf_op jit(solution)/shard_map/ppermute | solution.py:288
  31.7 4.9 %collective-permute-start.3 = (bf16[256,512]{1,0:T(8,128)(2,1)S(1)}, bf16[256,512]{1,0:T(8,128)(2,1)S(1)}, u32[]{:S(2)}, u32[]{:S(2)}) collective-permute-start(bf16[256,512]{1,0:T(8,128)(2,1)S(1)} %copy-done.2), channel_id=1, source_target_pairs={{0,2},{1,3},{2,0},{3,1},{4,6},{5,7},{6,4},{7,5},{8,10},{9,11},{10,... | collective-permute-start | bytes 786440 | tf_op jit(solution)/shard_map/ppermute | solution.py:297
  36.6 2.5 %collective-permute-start.2 = (bf16[256,512]{1,0:T(8,128)(2,1)S(1)}, bf16[256,512]{1,0:T(8,128)(2,1)S(1)}, u32[]{:S(2)}, u32[]{:S(2)}) collective-permute-start(bf16[256,512]{1,0:T(8,128)(2,1)S(1)} %copy-done.2), channel_id=1, source_target_pairs={{0,1},{1,2},{2,3},{3,0},{4,5},{5,6},{6,7},{7,4},{8,9},{9,10},{10,1... | collective-permute-start | bytes 786440 | tf_op jit(solution)/shard_map/ppermute | solution.py:297
  39.1 4.6 %collective-permute-start.4 = (bf16[256,512]{1,0:T(8,128)(2,1)S(1)}, bf16[256,512]{1,0:T(8,128)(2,1)S(1)}, u32[]{:S(2)}, u32[]{:S(2)}) collective-permute-start(bf16[256,512]{1,0:T(8,128)(2,1)S(1)} %copy-done.2), channel_id=1, source_target_pairs={{0,3},{1,0},{2,1},{3,2},{4,7},{5,4},{6,5},{7,6},{8,11},{9,8},{10,9... | collective-permute-start | bytes 786440 | tf_op jit(solution)/shard_map/ppermute | solution.py:297
  43.7 0.0 copy-start.8
  43.7 0.1 pad_add_fusion.idx_ref
  43.8 0.0 collective-permute-done.prior_ref
  43.8 0.6 copy-done.8
  44.4 1.6 %local.1 = (f32[256,256]{1,0:T(8,128)S(1)}, f32[256,256]{1,0:T(8,128)S(1)}) custom-call(s32[4]{0:T(128)S(1)} %pad_add_fusion.idx_ref, bf16[256,256]{1,0:T(8,128)(2,1)S(1)} %copy-done.4, bf16[256,256]{1,0:T(8,128)(2,1)S(1)} %copy-done.6, bf16[256,128]{1,0:T(8,128)(2,1)S(1)} %copy-done, bf16[256,128]{1,0:T(8,128)(2,1)S(1)} %copy-done.1, ...), custom_call_target="tpu_custom_call" | custom-call | flops 335544320 | bytes 1200000 | tf_op jit(solution)/shard_map/local/pallas_call | solution.py:122
  45.9 4.9 %collective-permute-start.1 = (f32[256,256]{1,0:T(8,128)S(1)}, f32[256,256]{1,0:T(8,128)S(1)}, u32[]{:S(2)}, u32[]{:S(2)}) collective-permute-start(f32[256,256]{1,0:T(8,128)S(1)} %get-tuple-element.7), channel_id=1, source_target_pairs={{4,0},{8,4},{12,8},{16,12},{20,16},{24,20},{28,24},{32,28},{36,32}... | collective-permute-start | bytes 786440 | tf_op jit(solution)/shard_map/ppermute | solution.py:288
  50.9 0.0 all-to-all-done.1.planes_ref
  50.9 1.2 %enter.1 = f32[8,16,128]{2,1,0:T(8,128)} custom-call(s32[4]{0:T(128)S(1)} %pad_add_fusion.idx_ref, f32[8,24,128]{2,1,0:T(8,128)S(1)} %all_to_all.25.got_ref, f32[16,24,128]{2,1,0:T(8,128)S(1)} %all-to-all-done.1.planes_ref), custom_call_target="tpu_custom_call" | custom-call | bytes 400000 | tf_op jit(solution)/shard_map/enter/pallas_call | solution.py:178
  52.1 3.3 %all-to-all-start.2 = ((f32[8,16,128]{2,1,0:T(8,128)}), f32[8,16,128]{2,1,0:T(8,128)S(1)}, u32[]{:S(2)}, u32[]{:S(2)}) async-start(f32[8,16,128]{2,1,0:T(8,128)} %enter.1), calls=%async_computation.2 | async-start | bytes 131072 | tf_op jit(solution)/shard_map/all_to_all | solution.py:303
  55.5 5.5 %all-to-all-done.2.state_ref = f32[8,16,128]{2,1,0:T(8,128)S(1)} async-done(((f32[8,16,128]{2,1,0:T(8,128)}), f32[8,16,128]{2,1,0:T(8,128)S(1)}, u32[]{:S(2)}, u32[]{:S(2)}) %all-to-all-start.2) | async-done | bytes 65568 | tf_op jit(solution)/shard_map/all_to_all | solution.py:303
  61.0 1.3 %weight_parts.1 = (f32[4,16,16,256]{3,2,1,0:T(8,128)S(1)}, bf16[4,16,16,256]{3,2,1,0:T(8,128)(2,1)S(1)}) custom-call(s32[4]{0:T(128)S(1)} %pad_add_fusion.idx_ref, f32[8,16,128]{2,1,0:T(8,128)S(1)} %all-to-all-done.2.state_ref, f32[256,256]{1,0:T(8,128)S(1)} %get-tuple-element.6.own_ref, f32[256,256]{1,0:T(8,128)S(1)} %collective-permute-done.1.back_ref, ...), custom_call_target="tpu_custom_call" | custom-call | flops 268435456 | bytes 3500000 | tf_op jit(solution)/shard_map/weight_parts/pallas_call | solution.py:217
  62.3 1.9 %collective-permute-start.5 = (bf16[4,16,16,256]{3,2,1,0:T(8,128)(2,1)S(1)}, bf16[4,16,16,256]{3,2,1,0:T(8,128)(2,1)S(1)}, u32[]{:S(2)}, u32[]{:S(2)}) collective-permute-start(bf16[4,16,16,256]{3,2,1,0:T(8,128)(2,1)S(1)} %get-tuple-element.9), channel_id=1, source_target_pairs={{0,4},{4,0},{1,5},{5,1},{2,6},{6,2},{3,7},{7,3},{8,12},{12,8},{9,1... | collective-permute-start | bytes 1572872 | tf_op jit(solution)/shard_map/ppermute | solution.py:305
  64.2 1.9 %collective-permute-done.5.other_ref = bf16[4,16,16,256]{3,2,1,0:T(8,128)(2,1)S(1)} collective-permute-done((bf16[4,16,16,256]{3,2,1,0:T(8,128)(2,1)S(1)}, bf16[4,16,16,256]{3,2,1,0:T(8,128)(2,1)S(1)}, u32[]{:S(2)}, u32[]{:S(2)}) %collective-permute-start.5) | collective-permute-done | bytes 524320 | tf_op jit(solution)/shard_map/ppermute | solution.py:305
  66.1 0.1 merge.1
  66.2 12.5 %all_to_all.26.parts_ref = bf16[4,16,16,256]{3,2,1,0:T(8,128)(2,1)S(1)} all-to-all(bf16[4,16,16,256]{3,2,1,0:T(8,128)(2,1)S(1)} %merge.1), channel_id=1, replica_groups=mesh['z'=16,'y'=4,'core'=2,'head'=4] {'y'}, dimensions={0} | all-to-all | bytes 1048576 | tf_op jit(solution)/shard_map/all_to_all | solution.py:306
  78.7 0.1 fold.1
  78.7 26.5 %all_to_all.27.parts_ref = bf16[16,16,256]{2,1,0:T(8,128)(2,1)S(1)} all-to-all(bf16[16,16,256]{2,1,0:T(8,128)(2,1)S(1)} %fold.1), channel_id=1, replica_groups=mesh['z'=16,'y'=4,'core'=2,'head'=4] {'z'}, dimensions={0} | all-to-all | bytes 262144 | tf_op jit(solution)/shard_map/all_to_all | solution.py:307
  105.3 0.6 finish.1
  (15 shorter events, 0.0 us)
Async XLA Ops:
  0.6 0.9 copy-start.3
  1.5 0.9 copy-start.5
  2.4 0.7 copy-start.7
  14.2 15.4 %copy-start = (bf16[256,128]{1,0:T(8,128)(2,1)S(1)}, bf16[256,128]{1,0:T(8,128)(2,1)}, u32[]{:S(2)}) copy-start(bf16[256,128]{1,0:T(8,128)(2,1)} %k_ref.3) | copy-start | bytes 196612
  14.2 15.4 %copy-start.1 = (bf16[256,128]{1,0:T(8,128)(2,1)S(1)}, bf16[256,128]{1,0:T(8,128)(2,1)}, u32[]{:S(2)}) copy-start(bf16[256,128]{1,0:T(8,128)(2,1)} %v_ref.3) | copy-start | bytes 196612
  14.2 17.5 %copy-start.2 = (bf16[256,512]{1,0:T(8,128)(2,1)S(1)}, bf16[256,512]{1,0:T(8,128)(2,1)}, u32[]{:S(2)}) copy-start(bf16[256,512]{1,0:T(8,128)(2,1)} %refs_0_.1) | copy-start | bytes 786436
  14.2 36.7 %all-to-all-start.1 = ((f32[16,24,128]{2,1,0:T(8,128)}), f32[16,24,128]{2,1,0:T(8,128)S(1)}, u32[]{:S(2)}, u32[]{:S(2)}) async-start(f32[16,24,128]{2,1,0:T(8,128)} %plane_total.1), calls=%async_computation.1 | async-start | bytes 393216 | tf_op jit(solution)/shard_map/all_to_all | solution.py:300
  29.5 14.2 %copy-start.4 = (bf16[256,256]{1,0:T(8,128)(2,1)S(1)}, bf16[256,256]{1,0:T(8,128)(2,1)}, u32[]{:S(2)}) copy-start(bf16[256,256]{1,0:T(8,128)(2,1)} %q_ref.3) | copy-start | bytes 393220
  29.5 14.2 %copy-start.6 = (bf16[256,256]{1,0:T(8,128)(2,1)S(1)}, bf16[256,256]{1,0:T(8,128)(2,1)}, u32[]{:S(2)}) copy-start(bf16[256,256]{1,0:T(8,128)(2,1)} %c_ref.3) | copy-start | bytes 393220
  29.6 14.2 %collective-permute-start = (bf16[256,256]{1,0:T(8,128)(2,1)S(1)}, bf16[256,256]{1,0:T(8,128)(2,1)S(1)}, u32[]{:S(2)}, u32[]{:S(2)}) collective-permute-start(bf16[256,256]{1,0:T(8,128)(2,1)S(1)} %pad_maximum_fusion), channel_id=1, source_target_pairs={{0,4},{4,8},{8,12},{12,16},{16,20},{20,24},{24,28},{28,32},{32,36}... | collective-permute-start | bytes 393224 | tf_op jit(solution)/shard_map/ppermute | solution.py:288
  31.7 23.8 %collective-permute-start.3 = (bf16[256,512]{1,0:T(8,128)(2,1)S(1)}, bf16[256,512]{1,0:T(8,128)(2,1)S(1)}, u32[]{:S(2)}, u32[]{:S(2)}) collective-permute-start(bf16[256,512]{1,0:T(8,128)(2,1)S(1)} %copy-done.2), channel_id=1, source_target_pairs={{0,2},{1,3},{2,0},{3,1},{4,6},{5,7},{6,4},{7,5},{8,10},{9,11},{10,... | collective-permute-start | bytes 786440 | tf_op jit(solution)/shard_map/ppermute | solution.py:297
  36.6 18.8 %collective-permute-start.2 = (bf16[256,512]{1,0:T(8,128)(2,1)S(1)}, bf16[256,512]{1,0:T(8,128)(2,1)S(1)}, u32[]{:S(2)}, u32[]{:S(2)}) collective-permute-start(bf16[256,512]{1,0:T(8,128)(2,1)S(1)} %copy-done.2), channel_id=1, source_target_pairs={{0,1},{1,2},{2,3},{3,0},{4,5},{5,6},{6,7},{7,4},{8,9},{9,10},{10,1... | collective-permute-start | bytes 786440 | tf_op jit(solution)/shard_map/ppermute | solution.py:297
  39.1 16.4 %collective-permute-start.4 = (bf16[256,512]{1,0:T(8,128)(2,1)S(1)}, bf16[256,512]{1,0:T(8,128)(2,1)S(1)}, u32[]{:S(2)}, u32[]{:S(2)}) collective-permute-start(bf16[256,512]{1,0:T(8,128)(2,1)S(1)} %copy-done.2), channel_id=1, source_target_pairs={{0,3},{1,0},{2,1},{3,2},{4,7},{5,4},{6,5},{7,6},{8,11},{9,8},{10,9... | collective-permute-start | bytes 786440 | tf_op jit(solution)/shard_map/ppermute | solution.py:297
  43.7 0.7 copy-start.8
  45.9 9.5 %collective-permute-start.1 = (f32[256,256]{1,0:T(8,128)S(1)}, f32[256,256]{1,0:T(8,128)S(1)}, u32[]{:S(2)}, u32[]{:S(2)}) collective-permute-start(f32[256,256]{1,0:T(8,128)S(1)} %get-tuple-element.7), channel_id=1, source_target_pairs={{4,0},{8,4},{12,8},{16,12},{20,16},{24,20},{28,24},{32,28},{36,32}... | collective-permute-start | bytes 786440 | tf_op jit(solution)/shard_map/ppermute | solution.py:288
  52.1 8.9 %all-to-all-start.2 = ((f32[8,16,128]{2,1,0:T(8,128)}), f32[8,16,128]{2,1,0:T(8,128)S(1)}, u32[]{:S(2)}, u32[]{:S(2)}) async-start(f32[8,16,128]{2,1,0:T(8,128)} %enter.1), calls=%async_computation.2 | async-start | bytes 131072 | tf_op jit(solution)/shard_map/all_to_all | solution.py:303
  62.3 3.8 %collective-permute-start.5 = (bf16[4,16,16,256]{3,2,1,0:T(8,128)(2,1)S(1)}, bf16[4,16,16,256]{3,2,1,0:T(8,128)(2,1)S(1)}, u32[]{:S(2)}, u32[]{:S(2)}) collective-permute-start(bf16[4,16,16,256]{3,2,1,0:T(8,128)(2,1)S(1)} %get-tuple-element.9), channel_id=1, source_target_pairs={{0,4},{4,0},{1,5},{5,1},{2,6},{6,2},{3,7},{7,3},{8,12},{12,8},{9,1... | collective-permute-start | bytes 1572872 | tf_op jit(solution)/shard_map/ppermute | solution.py:305

commit v3 on v2

--- a/solution.py
+++ b/solution.py
@@ -4,6 +4,7 @@
 from jax.experimental import pallas as pl
 from jax.experimental.pallas import tpu as pltpu
 from jax.sharding import Mesh, PartitionSpec as P
+
 
 E = 128
 LEN = 256
@@ -74,7 +75,7 @@
         in_specs=vmem(3),
         out_specs=vmem(1)[0],
         cost_estimate=cost(2 * LEN * E * E * 2, 400000),
-        compiler_params=params(8),
+        compiler_params=params(60),
         name="summary",
     )(q, c, ld)
 
@@ -288,29 +289,36 @@
     return lax.ppermute(value, CTX, [(source, source + steps) for source in range(leading, last)])
 
 
+def exchange(value, axis):
+    return lax.all_to_all(value, axis, 0, 0, tiled=True)
+
+
 def on_device(layer_input, queries, keys, values, result_cotangent, log_decay):
     axes = (CTX, "z", "core", "head")
     idx = jnp.stack([lax.axis_index(axis) for axis in axes]).astype(jnp.int32)
-    got = lax.all_to_all(summary(queries, result_cotangent, log_decay), PLANE, 0, 0, tiled=True)
-    prior = shifted(jnp.concatenate([keys, values], axis=1), 1)
-    xs = [layer_input] + [
-        lax.ppermute(layer_input, "head", [(i, (i + s) % NH) for i in range(NH)])
-        for s in range(1, NH)
-    ]
-    planes = lax.all_to_all(plane_total(got), "z", 0, 0, tiled=True)
+    got = exchange(summary(queries, result_cotangent, log_decay), PLANE)
+    pair = jnp.concatenate([keys, values], axis=1)
+    prior = shifted(pair, 1)
+    xs = [layer_input]
+    for s in range(1, NH):
+        xs.append(lax.ppermute(layer_input, "head", [(i, (i + s) % NH) for i in range(NH)]))
+    total = plane_total(got)
+    planes = exchange(total, "z")
     own, old = local(idx, queries, result_cotangent, keys, values, prior, log_decay)
     back = shifted(old, -1)
-    state = lax.all_to_all(enter(idx, got, planes), PLANE, 0, 0, tiled=True)
+    entering = enter(idx, got, planes)
+    state = exchange(entering, PLANE)
     keep, send = weight_parts(idx, state, own, back, keys, values, log_decay, xs)
     other = lax.ppermute(send, "core", [(0, 1), (1, 0)])
-    parts = fold(lax.all_to_all(merge(keep, other), "y", 0, 0, tiled=True))
-    return finish(lax.all_to_all(parts, "z", 0, 0, tiled=True))
+    parts = fold(exchange(merge(keep, other), "y"))
+    return finish(exchange(parts, "z"))
 
 
 def solution(mesh):
     fine = Mesh(mesh.devices.reshape(NZ, NY, NC, NH), CTX + ("head",))
     rows = P(CTX, "head")
     in_specs = (rows, rows, rows, rows, rows, P("head", CTX))
+
     return jax.shard_map(
         on_device, mesh=fine, in_specs=in_specs, out_specs=(rows, rows), check_vma=False
     )

time: 106 us -> 106 us (level)
  local copies, waits for them, and re-layouts: 3.09 us -> 0.61 us
  Pallas kernels: 5.86 us -> 7.48 us
    unnamed x18 -> x12, local copies, waits for them, and re-layouts: 3.09 us -> 0.61 us
    pallas_call x1, Pallas kernels: 0.29 us -> 1.91 us  [summary(): pl.pallas_call(summary_kernel, out_shape=jax.ShapeDtypeStruct((NP, ROWS +...]
where the time goes in v3:
time: 106 us; the launch traced here: 105 us
  blocking collectives  49.3 us (47%)
  starting transfers between devices  39.6 us (37%)
  Pallas kernels  7.48 us (7%)
  waiting for transfers between devices  7.39 us (7%)
    all_to_all x3, blocking collectives, exchange(): return lax.all_to_all(value, axis, 0, 0, tiled=True)  49.3 us
    all_to_all x2, starting transfers between devices, exchange(): return lax.all_to_all(value, axis, 0, 0, tiled=True)  18.7 us
    ppermute x3, starting transfers between devices, on_device(): lax.ppermute(layer_input, 'head', [(i, (i + s) % NH) for i in range(NH)])  12 us
    ppermute x2, starting transfers between devices, shifted(): lax.ppermute(value, CTX, [(source, source + steps) for source in range(le...  6.96 us
    all_to_all x2, waiting for transfers between devices, exchange(): return lax.all_to_all(value, axis, 0, 0, tiled=True)  5.5 us
  transfers between devices with their start and end apart: 8, of which 2 were waited for; matrix products, arithmetic and copies ran while one was open for 0% of the time, Pallas kernels for 3%

profile of v3, /device:TPU:32, one launch (start us, length us, event | category | flops | bytes accessed | tf_op | source)
XLA Modules:
  0.0 105.2 jit_solution(5455812799532188921)
XLA Ops:
  0.6 1.9 %summary.1 = f32[8,24,128]{2,1,0:T(8,128)} custom-call(bf16[256,256]{1,0:T(8,128)(2,1)} %q_ref.3, bf16[256,256]{1,0:T(8,128)(2,1)} %c_ref.3, f32[1,256]{1,0:T(1,128)} %ld_ref.5), custom_call_target="tpu_custom_call" | custom-call | flops 16777216 | bytes 400000 | tf_op jit(solution)/shard_map/summary/pallas_call | solution.py:72
  2.5 10.3 %all_to_all.25.got_ref = f32[8,24,128]{2,1,0:T(8,128)S(1)} all-to-all(f32[8,24,128]{2,1,0:T(8,128)} %summary.1), channel_id=1, replica_groups=mesh['z'=16,'y'=4,'core'=2,'head'=4] {'y','core'}, dimensions={0} | all-to-all | bytes 196608 | tf_op jit(solution)/shard_map/all_to_all | solution.py:293
  12.8 0.7 plane_total.1
  13.5 15.3 %all-to-all-start.1 = ((f32[16,24,128]{2,1,0:T(8,128)}), f32[16,24,128]{2,1,0:T(8,128)S(1)}, u32[]{:S(2)}, u32[]{:S(2)}) async-start(f32[16,24,128]{2,1,0:T(8,128)} %plane_total.1), calls=%async_computation.1 | async-start | bytes 393216 | tf_op jit(solution)/shard_map/all_to_all | solution.py:293
  28.9 0.0 copy-start.3
  28.9 0.0 copy-start.4
  28.9 2.1 %collective-permute-start = (bf16[256,256]{1,0:T(8,128)(2,1)S(1)}, bf16[256,256]{1,0:T(8,128)(2,1)S(1)}, u32[]{:S(2)}, u32[]{:S(2)}) collective-permute-start(bf16[256,256]{1,0:T(8,128)(2,1)S(1)} %pad_maximum_fusion), channel_id=1, source_target_pairs={{0,4},{4,8},{8,12},{12,16},{16,20},{20,24},{24,28},{28,32},{32,36}... | collective-permute-start | bytes 393224 | tf_op jit(solution)/shard_map/ppermute | solution.py:289
  31.0 4.9 %collective-permute-start.3 = (bf16[256,512]{1,0:T(8,128)(2,1)S(1)}, bf16[256,512]{1,0:T(8,128)(2,1)S(1)}, u32[]{:S(2)}, u32[]{:S(2)}) collective-permute-start(bf16[256,512]{1,0:T(8,128)(2,1)S(1)} %copy-done.2), channel_id=1, source_target_pairs={{0,2},{1,3},{2,0},{3,1},{4,6},{5,7},{6,4},{7,5},{8,10},{9,11},{10,... | collective-permute-start | bytes 786440 | tf_op jit(solution)/shard_map/ppermute | solution.py:304
  35.9 2.5 %collective-permute-start.2 = (bf16[256,512]{1,0:T(8,128)(2,1)S(1)}, bf16[256,512]{1,0:T(8,128)(2,1)S(1)}, u32[]{:S(2)}, u32[]{:S(2)}) collective-permute-start(bf16[256,512]{1,0:T(8,128)(2,1)S(1)} %copy-done.2), channel_id=1, source_target_pairs={{0,1},{1,2},{2,3},{3,0},{4,5},{5,6},{6,7},{7,4},{8,9},{9,10},{10,1... | collective-permute-start | bytes 786440 | tf_op jit(solution)/shard_map/ppermute | solution.py:304
  38.4 4.6 %collective-permute-start.4 = (bf16[256,512]{1,0:T(8,128)(2,1)S(1)}, bf16[256,512]{1,0:T(8,128)(2,1)S(1)}, u32[]{:S(2)}, u32[]{:S(2)}) collective-permute-start(bf16[256,512]{1,0:T(8,128)(2,1)S(1)} %copy-done.2), channel_id=1, source_target_pairs={{0,3},{1,0},{2,1},{3,2},{4,7},{5,4},{6,5},{7,6},{8,11},{9,8},{10,9... | collective-permute-start | bytes 786440 | tf_op jit(solution)/shard_map/ppermute | solution.py:304
  43.0 0.0 copy-start.5
  43.0 0.1 pad_add_fusion.idx_ref
  43.1 0.0 collective-permute-done.prior_ref
  43.1 0.6 copy-done.5
  43.7 1.6 %local.1 = (f32[256,256]{1,0:T(8,128)S(1)}, f32[256,256]{1,0:T(8,128)S(1)}) custom-call(s32[4]{0:T(128)S(1)} %pad_add_fusion.idx_ref, bf16[256,256]{1,0:T(8,128)(2,1)S(1)} %copy-done.3, bf16[256,256]{1,0:T(8,128)(2,1)S(1)} %copy-done.4, bf16[256,128]{1,0:T(8,128)(2,1)S(1)} %copy-done, bf16[256,128]{1,0:T(8,128)(2,1)S(1)} %copy-done.1, ...), custom_call_target="tpu_custom_call" | custom-call | flops 335544320 | bytes 1200000 | tf_op jit(solution)/shard_map/local/pallas_call | solution.py:123
  45.3 4.9 %collective-permute-start.1 = (f32[256,256]{1,0:T(8,128)S(1)}, f32[256,256]{1,0:T(8,128)S(1)}, u32[]{:S(2)}, u32[]{:S(2)}) collective-permute-start(f32[256,256]{1,0:T(8,128)S(1)} %get-tuple-element.7), channel_id=1, source_target_pairs={{4,0},{8,4},{12,8},{16,12},{20,16},{24,20},{28,24},{32,28},{36,32}... | collective-permute-start | bytes 786440 | tf_op jit(solution)/shard_map/ppermute | solution.py:289
  50.2 0.0 all-to-all-done.1.planes_ref
  50.2 1.2 %enter.1 = f32[8,16,128]{2,1,0:T(8,128)} custom-call(s32[4]{0:T(128)S(1)} %pad_add_fusion.idx_ref, f32[8,24,128]{2,1,0:T(8,128)S(1)} %all_to_all.25.got_ref, f32[16,24,128]{2,1,0:T(8,128)S(1)} %all-to-all-done.1.planes_ref), custom_call_target="tpu_custom_call" | custom-call | bytes 400000 | tf_op jit(solution)/shard_map/enter/pallas_call | solution.py:179
  51.4 3.3 %all-to-all-start.2 = ((f32[8,16,128]{2,1,0:T(8,128)}), f32[8,16,128]{2,1,0:T(8,128)S(1)}, u32[]{:S(2)}, u32[]{:S(2)}) async-start(f32[8,16,128]{2,1,0:T(8,128)} %enter.1), calls=%async_computation.2 | async-start | bytes 131072 | tf_op jit(solution)/shard_map/all_to_all | solution.py:293
  54.8 0.0 collective-permute-done.3.refs_2_
  54.8 0.0 collective-permute-done.2.refs_1_
  54.8 0.0 collective-permute-done.4.refs_3_
  54.8 0.0 collective-permute-done.1.back_ref
  54.8 5.5 %all-to-all-done.2.state_ref = f32[8,16,128]{2,1,0:T(8,128)S(1)} async-done(((f32[8,16,128]{2,1,0:T(8,128)}), f32[8,16,128]{2,1,0:T(8,128)S(1)}, u32[]{:S(2)}, u32[]{:S(2)}) %all-to-all-start.2) | async-done | bytes 65568 | tf_op jit(solution)/shard_map/all_to_all | solution.py:293
  60.3 1.3 %weight_parts.1 = (f32[4,16,16,256]{3,2,1,0:T(8,128)S(1)}, bf16[4,16,16,256]{3,2,1,0:T(8,128)(2,1)S(1)}) custom-call(s32[4]{0:T(128)S(1)} %pad_add_fusion.idx_ref, f32[8,16,128]{2,1,0:T(8,128)S(1)} %all-to-all-done.2.state_ref, f32[256,256]{1,0:T(8,128)S(1)} %get-tuple-element.6.own_ref, f32[256,256]{1,0:T(8,128)S(1)} %collective-permute-done.1.back_ref, ...), custom_call_target="tpu_custom_call" | custom-call | flops 268435456 | bytes 3500000 | tf_op jit(solution)/shard_map/weight_parts/pallas_call | solution.py:218
  61.6 1.9 %collective-permute-start.5 = (bf16[4,16,16,256]{3,2,1,0:T(8,128)(2,1)S(1)}, bf16[4,16,16,256]{3,2,1,0:T(8,128)(2,1)S(1)}, u32[]{:S(2)}, u32[]{:S(2)}) collective-permute-start(bf16[4,16,16,256]{3,2,1,0:T(8,128)(2,1)S(1)} %get-tuple-element.9), channel_id=1, source_target_pairs={{0,4},{4,0},{1,5},{5,1},{2,6},{6,2},{3,7},{7,3},{8,12},{12,8},{9,1... | collective-permute-start | bytes 1572872 | tf_op jit(solution)/shard_map/ppermute | solution.py:312
  63.6 1.9 %collective-permute-done.5.other_ref = bf16[4,16,16,256]{3,2,1,0:T(8,128)(2,1)S(1)} collective-permute-done((bf16[4,16,16,256]{3,2,1,0:T(8,128)(2,1)S(1)}, bf16[4,16,16,256]{3,2,1,0:T(8,128)(2,1)S(1)}, u32[]{:S(2)}, u32[]{:S(2)}) %collective-permute-start.5) | collective-permute-done | bytes 524320 | tf_op jit(solution)/shard_map/ppermute | solution.py:312
  65.4 0.1 merge.1
  65.5 12.5 %all_to_all.26.parts_ref = bf16[4,16,16,256]{3,2,1,0:T(8,128)(2,1)S(1)} all-to-all(bf16[4,16,16,256]{3,2,1,0:T(8,128)(2,1)S(1)} %merge.1), channel_id=1, replica_groups=mesh['z'=16,'y'=4,'core'=2,'head'=4] {'y'}, dimensions={0} | all-to-all | bytes 1048576 | tf_op jit(solution)/shard_map/all_to_all | solution.py:293
  78.0 0.1 fold.1
  78.0 26.5 %all_to_all.27.parts_ref = bf16[16,16,256]{2,1,0:T(8,128)(2,1)S(1)} all-to-all(bf16[16,16,256]{2,1,0:T(8,128)(2,1)S(1)} %fold.1), channel_id=1, replica_groups=mesh['z'=16,'y'=4,'core'=2,'head'=4] {'z'}, dimensions={0} | all-to-all | bytes 262144 | tf_op jit(solution)/shard_map/all_to_all | solution.py:293
  104.6 0.6 finish.1
  (9 shorter events, 0.0 us)
Async XLA Ops:
  13.5 15.4 %copy-start = (bf16[256,128]{1,0:T(8,128)(2,1)S(1)}, bf16[256,128]{1,0:T(8,128)(2,1)}, u32[]{:S(2)}) copy-start(bf16[256,128]{1,0:T(8,128)(2,1)} %k_ref.3) | copy-start | bytes 196612
  13.5 15.4 %copy-start.1 = (bf16[256,128]{1,0:T(8,128)(2,1)S(1)}, bf16[256,128]{1,0:T(8,128)(2,1)}, u32[]{:S(2)}) copy-start(bf16[256,128]{1,0:T(8,128)(2,1)} %v_ref.3) | copy-start | bytes 196612
  13.5 17.5 %copy-start.2 = (bf16[256,512]{1,0:T(8,128)(2,1)S(1)}, bf16[256,512]{1,0:T(8,128)(2,1)}, u32[]{:S(2)}) copy-start(bf16[256,512]{1,0:T(8,128)(2,1)} %refs_0_.1) | copy-start | bytes 786436
  13.5 36.7 %all-to-all-start.1 = ((f32[16,24,128]{2,1,0:T(8,128)}), f32[16,24,128]{2,1,0:T(8,128)S(1)}, u32[]{:S(2)}, u32[]{:S(2)}) async-start(f32[16,24,128]{2,1,0:T(8,128)} %plane_total.1), calls=%async_computation.1 | async-start | bytes 393216 | tf_op jit(solution)/shard_map/all_to_all | solution.py:293
  28.9 14.2 %copy-start.3 = (bf16[256,256]{1,0:T(8,128)(2,1)S(1)}, bf16[256,256]{1,0:T(8,128)(2,1)}, u32[]{:S(2)}) copy-start(bf16[256,256]{1,0:T(8,128)(2,1)} %q_ref.3) | copy-start | bytes 393220
  28.9 14.2 %copy-start.4 = (bf16[256,256]{1,0:T(8,128)(2,1)S(1)}, bf16[256,256]{1,0:T(8,128)(2,1)}, u32[]{:S(2)}) copy-start(bf16[256,256]{1,0:T(8,128)(2,1)} %c_ref.3) | copy-start | bytes 393220
  28.9 14.2 %collective-permute-start = (bf16[256,256]{1,0:T(8,128)(2,1)S(1)}, bf16[256,256]{1,0:T(8,128)(2,1)S(1)}, u32[]{:S(2)}, u32[]{:S(2)}) collective-permute-start(bf16[256,256]{1,0:T(8,128)(2,1)S(1)} %pad_maximum_fusion), channel_id=1, source_target_pairs={{0,4},{4,8},{8,12},{12,16},{16,20},{20,24},{24,28},{28,32},{32,36}... | collective-permute-start | bytes 393224 | tf_op jit(solution)/shard_map/ppermute | solution.py:289
  31.0 23.8 %collective-permute-start.3 = (bf16[256,512]{1,0:T(8,128)(2,1)S(1)}, bf16[256,512]{1,0:T(8,128)(2,1)S(1)}, u32[]{:S(2)}, u32[]{:S(2)}) collective-permute-start(bf16[256,512]{1,0:T(8,128)(2,1)S(1)} %copy-done.2), channel_id=1, source_target_pairs={{0,2},{1,3},{2,0},{3,1},{4,6},{5,7},{6,4},{7,5},{8,10},{9,11},{10,... | collective-permute-start | bytes 786440 | tf_op jit(solution)/shard_map/ppermute | solution.py:304
  35.9 18.9 %collective-permute-start.2 = (bf16[256,512]{1,0:T(8,128)(2,1)S(1)}, bf16[256,512]{1,0:T(8,128)(2,1)S(1)}, u32[]{:S(2)}, u32[]{:S(2)}) collective-permute-start(bf16[256,512]{1,0:T(8,128)(2,1)S(1)} %copy-done.2), channel_id=1, source_target_pairs={{0,1},{1,2},{2,3},{3,0},{4,5},{5,6},{6,7},{7,4},{8,9},{9,10},{10,1... | collective-permute-start | bytes 786440 | tf_op jit(solution)/shard_map/ppermute | solution.py:304
  38.4 16.4 %collective-permute-start.4 = (bf16[256,512]{1,0:T(8,128)(2,1)S(1)}, bf16[256,512]{1,0:T(8,128)(2,1)S(1)}, u32[]{:S(2)}, u32[]{:S(2)}) collective-permute-start(bf16[256,512]{1,0:T(8,128)(2,1)S(1)} %copy-done.2), channel_id=1, source_target_pairs={{0,3},{1,0},{2,1},{3,2},{4,7},{5,4},{6,5},{7,6},{8,11},{9,8},{10,9... | collective-permute-start | bytes 786440 | tf_op jit(solution)/shard_map/ppermute | solution.py:304
  43.0 0.7 copy-start.5
  45.3 9.5 %collective-permute-start.1 = (f32[256,256]{1,0:T(8,128)S(1)}, f32[256,256]{1,0:T(8,128)S(1)}, u32[]{:S(2)}, u32[]{:S(2)}) collective-permute-start(f32[256,256]{1,0:T(8,128)S(1)} %get-tuple-element.7), channel_id=1, source_target_pairs={{4,0},{8,4},{12,8},{16,12},{20,16},{24,20},{28,24},{32,28},{36,32}... | collective-permute-start | bytes 786440 | tf_op jit(solution)/shard_map/ppermute | solution.py:289
  51.4 8.9 %all-to-all-start.2 = ((f32[8,16,128]{2,1,0:T(8,128)}), f32[8,16,128]{2,1,0:T(8,128)S(1)}, u32[]{:S(2)}, u32[]{:S(2)}) async-start(f32[8,16,128]{2,1,0:T(8,128)} %enter.1), calls=%async_computation.2 | async-start | bytes 131072 | tf_op jit(solution)/shard_map/all_to_all | solution.py:293
  61.6 3.8 %collective-permute-start.5 = (bf16[4,16,16,256]{3,2,1,0:T(8,128)(2,1)S(1)}, bf16[4,16,16,256]{3,2,1,0:T(8,128)(2,1)S(1)}, u32[]{:S(2)}, u32[]{:S(2)}) collective-permute-start(bf16[4,16,16,256]{3,2,1,0:T(8,128)(2,1)S(1)} %get-tuple-element.9), channel_id=1, source_target_pairs={{0,4},{4,0},{1,5},{5,1},{2,6},{6,2},{3,7},{7,3},{8,12},{12,8},{9,1... | collective-permute-start | bytes 1572872 | tf_op jit(solution)/shard_map/ppermute | solution.py:312

commit v4 on v3

--- a/solution.py
+++ b/solution.py
@@ -78,6 +78,23 @@
         compiler_params=params(60),
         name="summary",
     )(q, c, ld)
+
+
+def pair_kernel(own_ref, got_ref, out_ref):
+    out_ref[0] = own_ref[...].T
+    out_ref[1] = got_ref[...].T
+
+
+def pair_up(own, got):
+    return pl.pallas_call(
+        pair_kernel,
+        out_shape=jax.ShapeDtypeStruct((2, XD, LEN), BF16),
+        in_specs=vmem(2),
+        out_specs=vmem(1)[0],
+        cost_estimate=cost(0, 1000000),
+        compiler_params=params(8),
+        name="pair_up",
+    )(own, got)
 
 
 def local_kernel(idx_ref, q_ref, c_ref, k_ref, v_ref, prior_ref, ld_ref, own_ref, back_ref):
@@ -139,16 +156,20 @@
         low += weight * got_ref[k, 0:8, :]
         high += weight * got_ref[k, 8:16, :]
         log += got_ref[k, ROWS:, :]
+    row = lax.broadcasted_iota(jnp.int32, (8, E), 0)
+    first = log.astype(BF16).astype(F32)
+    second = (log - first).astype(BF16).astype(F32)
+    third = log - first - second
+    terms = jnp.where(row == 0, first, jnp.where(row == 1, second, jnp.where(row == 2, third, 0.0)))
+    sent = jnp.concatenate([low, high, terms], axis=0).astype(BF16)
     for z in range(NZ):
-        out_ref[z, 0:8, :] = low
-        out_ref[z, 8:16, :] = high
-        out_ref[z, ROWS:, :] = log
+        out_ref[z] = sent
 
 
 def plane_total(got):
     return pl.pallas_call(
         plane_kernel,
-        out_shape=jax.ShapeDtypeStruct((NZ, ROWS + 8, E), F32),
+        out_shape=jax.ShapeDtypeStruct((NZ, ROWS + 8, E), BF16),
         in_specs=vmem(1),
         out_specs=vmem(1)[0],
         cost_estimate=cost(0, 300000),
@@ -159,20 +180,16 @@
 
 def enter_kernel(idx_ref, got_ref, planes_ref, out_ref):
     mine = idx_ref[1]
-    log = jnp.zeros((8, E), F32)
-    low, high = jnp.zeros((8, E), F32), jnp.zeros((8, E), F32)
+    log = jnp.zeros((1, E), F32)
+    state = jnp.zeros((ROWS, E), F32)
     for z in range(NZ):
         later = z > mine
-        weight = jnp.where(later, jnp.exp(log), 0.0)
-        low += weight * planes_ref[z, 0:8, :]
-        high += weight * planes_ref[z, 8:16, :]
-        log += jnp.where(later, planes_ref[z, ROWS:, :], 0.0)
+        plane = planes_ref[z].astype(F32)
+        state += jnp.where(later, jnp.exp(log), 0.0) * plane[:ROWS]
+        log += jnp.where(later, jnp.sum(plane[ROWS:], axis=0, keepdims=True), 0.0)
     for k in range(NP - 1, -1, -1):
-        out_ref[k, 0:8, :] = low
-        out_ref[k, 8:16, :] = high
-        decay = jnp.exp(got_ref[k, ROWS:, :])
-        low = got_ref[k, 0:8, :] + decay * low
-        high = got_ref[k, 8:16, :] + decay * high
+        out_ref[k] = state
+        state = got_ref[k, :ROWS, :] + jnp.exp(got_ref[k, ROWS : ROWS + 1, :]) * state
 
 
 def enter(idx, got, planes):
@@ -190,7 +207,7 @@
 def weight_kernel(
     idx_ref, state_ref, own_ref, back_ref, k_ref, v_ref, ld_ref, *refs
 ):
-    x_refs, (keep_ref, send_ref, part) = refs[:NH], refs[NH:]
+    near_ref, far_ref, keep_ref, send_ref, part = refs
     column, _ = log_sums(ld_ref[...])
     tail = jnp.exp(column[LEN - 1 :, :] - column)
     state = state_ref[...].reshape(E, E)
@@ -204,27 +221,28 @@
     grad = jnp.concatenate([key_grad, value_grad], axis=1)
     core, head = idx_ref[2], idx_ref[3]
     for i in range(NH):
-        found = mm(x_refs[i][...], grad, TN).reshape(NH, NY, NC, 16, 2 * E)
+        x = (near_ref if i < 2 else far_ref)[i % 2]
+        found = mm(x, grad, NN).reshape(NH, NY, NC, 16, 2 * E)
         for y in range(NY):
             for c in range(NC):
                 part[c, y] = found[:, y, c]
-        where = pl.ds(lax.rem(head + NH - i, NH) * NH, NH)
+        where = pl.ds(lax.bitwise_xor(head, jnp.int32((0, 2, 1, 3)[i])) * NH, NH)
         keep_ref[:, where] = part[core]
         send_ref[:, where] = part[1 - core].astype(BF16)
 
 
-def weight_parts(idx, state, own, back, k, v, ld, xs):
+def weight_parts(idx, state, own, back, k, v, ld, near, far):
     whole = (NY, NZ, 16, 2 * E)
     return pl.pallas_call(
         weight_kernel,
         out_shape=(jax.ShapeDtypeStruct(whole, F32), jax.ShapeDtypeStruct(whole, BF16)),
-        in_specs=[SMEM] + vmem(6 + NH),
+        in_specs=[SMEM] + vmem(8),
         out_specs=tuple(vmem(2)),
         scratch_shapes=[pltpu.VMEM((NC, NY, NH, 16, 2 * E), F32)],
         cost_estimate=cost(2 * NH * XD * LEN * 2 * E, 3500000),
         compiler_params=params(16),
         name="weight_parts",
-    )(idx, state, own, back, k, v, ld, *xs)
+    )(idx, state, own, back, k, v, ld, near, far)
 
 
 def merge_kernel(keep_ref, other_ref, out_ref):
@@ -299,16 +317,16 @@
     got = exchange(summary(queries, result_cotangent, log_decay), PLANE)
     pair = jnp.concatenate([keys, values], axis=1)
     prior = shifted(pair, 1)
-    xs = [layer_input]
-    for s in range(1, NH):
-        xs.append(lax.ppermute(layer_input, "head", [(i, (i + s) % NH) for i in range(NH)]))
+    opposite = lax.ppermute(layer_input, "head", [(i, i ^ 2) for i in range(NH)])
+    near = pair_up(layer_input, opposite)
+    far = lax.ppermute(near, "head", [(i, i ^ 1) for i in range(NH)])
     total = plane_total(got)
     planes = exchange(total, "z")
     own, old = local(idx, queries, result_cotangent, keys, values, prior, log_decay)
     back = shifted(old, -1)
     entering = enter(idx, got, planes)
     state = exchange(entering, PLANE)
-    keep, send = weight_parts(idx, state, own, back, keys, values, log_decay, xs)
+    keep, send = weight_parts(idx, state, own, back, keys, values, log_decay, near, far)
     other = lax.ppermute(send, "core", [(0, 1), (1, 0)])
     parts = fold(exchange(merge(keep, other), "y"))
     return finish(exchange(parts, "z"))

time: 106 us -> 105 us (level)
  the two profiles are of different devices: /device:TPU:32 before, /device:TPU:2 now
where the time goes in v4:
time: 105 us; the launch traced here: 104 us
  blocking collectives  52.3 us (50%)
  starting transfers between devices  30.6 us (29%)
  waiting for transfers between devices  12.9 us (12%)
  Pallas kernels  7.62 us (7%)
    all_to_all x3, blocking collectives, exchange(): return lax.all_to_all(value, axis, 0, 0, tiled=True)  52.3 us
    all_to_all x2, starting transfers between devices, exchange(): return lax.all_to_all(value, axis, 0, 0, tiled=True)  18.6 us
    all_to_all x2, waiting for transfers between devices, exchange(): return lax.all_to_all(value, axis, 0, 0, tiled=True)  10.2 us
    ppermute x1, starting transfers between devices, on_device(): lax.ppermute(layer_input, 'head', [(i, i ^ 2) for i in range(NH)])  4.04 us
    ppermute x1, starting transfers between devices, on_device(): far = lax.ppermute(near, 'head', [(i, i ^ 1) for i in range(NH)])  3.47 us
    ppermute x2, starting transfers between devices, shifted(): lax.ppermute(value, CTX, [(source, source + steps) for source in range(le...  2.59 us
  transfers between devices with their start and end apart: 7, of which 4 were waited for; matrix products, arithmetic and copies ran while one was open for 0% of the time, Pallas kernels for 5%

profile of v4, /device:TPU:2, one launch (start us, length us, event | category | flops | bytes accessed | tf_op | source)
XLA Modules:
  0.0 104.3 jit_solution(4870886874122314230)
XLA Ops:
  0.6 4.0 %collective-permute-start.2 = (bf16[256,512]{1,0:T(8,128)(2,1)}, bf16[256,512]{1,0:T(8,128)(2,1)S(1)}, u32[]{:S(2)}, u32[]{:S(2)}) collective-permute-start(bf16[256,512]{1,0:T(8,128)(2,1)} %own_ref.1), channel_id=1, source_target_pairs={{0,2},{1,3},{2,0},{3,1},{4,6},{5,7},{6,4},{7,5},{8,10},{9,11},{10,... | collective-permute-start | bytes 786440 | tf_op jit(solution)/shard_map/ppermute | solution.py:320
  4.7 1.9 %summary.1 = f32[8,24,128]{2,1,0:T(8,128)} custom-call(bf16[256,256]{1,0:T(8,128)(2,1)} %q_ref.3, bf16[256,256]{1,0:T(8,128)(2,1)} %c_ref.3, f32[1,256]{1,0:T(1,128)} %ld_ref.5), custom_call_target="tpu_custom_call" | custom-call | flops 16777216 | bytes 400000 | tf_op jit(solution)/shard_map/summary/pallas_call | solution.py:72
  6.6 10.4 %all_to_all.25.got_ref = f32[8,24,128]{2,1,0:T(8,128)S(1)} all-to-all(f32[8,24,128]{2,1,0:T(8,128)} %summary.1), channel_id=1, replica_groups=mesh['z'=16,'y'=4,'core'=2,'head'=4] {'y','core'}, dimensions={0} | all-to-all | bytes 196608 | tf_op jit(solution)/shard_map/all_to_all | solution.py:311
  17.0 0.7 plane_total.1
  17.6 15.2 %all-to-all-start.1 = ((bf16[16,24,128]{2,1,0:T(8,128)(2,1)}), bf16[16,24,128]{2,1,0:T(8,128)(2,1)S(1)}, u32[]{:S(2)}, u32[]{:S(2)}) async-start(bf16[16,24,128]{2,1,0:T(8,128)(2,1)} %plane_total.1), calls=%async_computation.1 | async-start | bytes 196608 | tf_op jit(solution)/shard_map/all_to_all | solution.py:311
  32.8 0.0 copy-start
  32.8 0.0 copy-start.1
  32.9 0.0 collective-permute-done.2.got_ref
  32.9 0.2 pair_up.1.refs_0_
  33.1 0.0 copy-start.3
  33.1 0.0 copy-start.4
  33.1 3.5 %collective-permute-start.3 = (bf16[2,512,256]{2,1,0:T(8,128)(2,1)S(1)}, bf16[2,512,256]{2,1,0:T(8,128)(2,1)S(1)}, u32[]{:S(2)}, u32[]{:S(2)}) collective-permute-start(bf16[2,512,256]{2,1,0:T(8,128)(2,1)S(1)} %pair_up.1.refs_0_), channel_id=1, source_target_pairs={{0,1},{1,0},{2,3},{3,2},{4,5},{5,4},{6,7},{7,6},{8,9},{9,8},{10,11... | collective-permute-start | bytes 1572872 | tf_op jit(solution)/shard_map/ppermute | solution.py:322
  36.6 1.3 %collective-permute-start = (bf16[256,256]{1,0:T(8,128)(2,1)S(1)}, bf16[256,256]{1,0:T(8,128)(2,1)S(1)}, u32[]{:S(2)}, u32[]{:S(2)}) collective-permute-start(bf16[256,256]{1,0:T(8,128)(2,1)S(1)} %pad_maximum_fusion), channel_id=1, source_target_pairs={{0,4},{4,8},{8,12},{12,16},{16,20},{20,24},{24,28},{28,32},{32,36}... | collective-permute-start | bytes 393224 | tf_op jit(solution)/shard_map/ppermute | solution.py:307
  37.9 0.0 copy-start.5
  38.0 0.1 pad_add_fusion.idx_ref
  38.0 0.9 collective-permute-done.prior_ref
  38.9 1.6 %local.1 = (f32[256,256]{1,0:T(8,128)S(1)}, f32[256,256]{1,0:T(8,128)S(1)}) custom-call(s32[4]{0:T(128)S(1)} %pad_add_fusion.idx_ref, bf16[256,256]{1,0:T(8,128)(2,1)S(1)} %copy-done.3, bf16[256,256]{1,0:T(8,128)(2,1)S(1)} %copy-done.4, bf16[256,128]{1,0:T(8,128)(2,1)S(1)} %copy-done, bf16[256,128]{1,0:T(8,128)(2,1)S(1)} %copy-done.1, ...), custom_call_target="tpu_custom_call" | custom-call | flops 335544320 | bytes 1200000 | tf_op jit(solution)/shard_map/local/pallas_call | solution.py:140
  40.5 1.3 %collective-permute-start.1 = (f32[256,256]{1,0:T(8,128)S(1)}, f32[256,256]{1,0:T(8,128)S(1)}, u32[]{:S(2)}, u32[]{:S(2)}) collective-permute-start(f32[256,256]{1,0:T(8,128)S(1)} %get-tuple-element.7), channel_id=1, source_target_pairs={{4,0},{8,4},{12,8},{16,12},{20,16},{24,20},{28,24},{32,28},{36,32}... | collective-permute-start | bytes 786440 | tf_op jit(solution)/shard_map/ppermute | solution.py:307
  41.8 4.5 %all-to-all-done.1.planes_ref = bf16[16,24,128]{2,1,0:T(8,128)(2,1)S(1)} async-done(((bf16[16,24,128]{2,1,0:T(8,128)(2,1)}), bf16[16,24,128]{2,1,0:T(8,128)(2,1)S(1)}, u32[]{:S(2)}, u32[]{:S(2)}) %all-to-all-start.1) | async-done | bytes 98336 | tf_op jit(solution)/shard_map/all_to_all | solution.py:311
  46.3 1.2 %enter.1 = f32[8,16,128]{2,1,0:T(8,128)} custom-call(s32[4]{0:T(128)S(1)} %pad_add_fusion.idx_ref, f32[8,24,128]{2,1,0:T(8,128)S(1)} %all_to_all.25.got_ref, bf16[16,24,128]{2,1,0:T(8,128)(2,1)S(1)} %all-to-all-done.1.planes_ref), custom_call_target="tpu_custom_call" | custom-call | bytes 400000 | tf_op jit(solution)/shard_map/enter/pallas_call | solution.py:196
  47.5 3.4 %all-to-all-start.2 = ((f32[8,16,128]{2,1,0:T(8,128)}), f32[8,16,128]{2,1,0:T(8,128)S(1)}, u32[]{:S(2)}, u32[]{:S(2)}) async-start(f32[8,16,128]{2,1,0:T(8,128)} %enter.1), calls=%async_computation.2 | async-start | bytes 131072 | tf_op jit(solution)/shard_map/all_to_all | solution.py:311
  50.9 0.0 collective-permute-done.1.back_ref
  50.9 5.6 %all-to-all-done.2.state_ref = f32[8,16,128]{2,1,0:T(8,128)S(1)} async-done(((f32[8,16,128]{2,1,0:T(8,128)}), f32[8,16,128]{2,1,0:T(8,128)S(1)}, u32[]{:S(2)}, u32[]{:S(2)}) %all-to-all-start.2) | async-done | bytes 65568 | tf_op jit(solution)/shard_map/all_to_all | solution.py:311
  56.5 0.0 collective-permute-done.3.refs_1_
  56.5 1.3 %weight_parts.1 = (f32[4,16,16,256]{3,2,1,0:T(8,128)S(1)}, bf16[4,16,16,256]{3,2,1,0:T(8,128)(2,1)S(1)}) custom-call(s32[4]{0:T(128)S(1)} %pad_add_fusion.idx_ref, f32[8,16,128]{2,1,0:T(8,128)S(1)} %all-to-all-done.2.state_ref, f32[256,256]{1,0:T(8,128)S(1)} %get-tuple-element.6.own_ref, f32[256,256]{1,0:T(8,128)S(1)} %collective-permute-done.1.back_ref, ...), custom_call_target="tpu_custom_call" | custom-call | flops 268435456 | bytes 3500000 | tf_op jit(solution)/shard_map/weight_parts/pallas_call | solution.py:236
  57.8 1.9 %collective-permute-start.4 = (bf16[4,16,16,256]{3,2,1,0:T(8,128)(2,1)S(1)}, bf16[4,16,16,256]{3,2,1,0:T(8,128)(2,1)S(1)}, u32[]{:S(2)}, u32[]{:S(2)}) collective-permute-start(bf16[4,16,16,256]{3,2,1,0:T(8,128)(2,1)S(1)} %get-tuple-element.9), channel_id=1, source_target_pairs={{0,4},{4,0},{1,5},{5,1},{2,6},{6,2},{3,7},{7,3},{8,12},{12,8},{9,1... | collective-permute-start | bytes 1572872 | tf_op jit(solution)/shard_map/ppermute | solution.py:330
  59.8 1.9 %collective-permute-done.4.other_ref = bf16[4,16,16,256]{3,2,1,0:T(8,128)(2,1)S(1)} collective-permute-done((bf16[4,16,16,256]{3,2,1,0:T(8,128)(2,1)S(1)}, bf16[4,16,16,256]{3,2,1,0:T(8,128)(2,1)S(1)}, u32[]{:S(2)}, u32[]{:S(2)}) %collective-permute-start.4) | collective-permute-done | bytes 524320 | tf_op jit(solution)/shard_map/ppermute | solution.py:330
  61.6 0.1 merge.1
  61.7 12.6 %all_to_all.26.parts_ref = bf16[4,16,16,256]{3,2,1,0:T(8,128)(2,1)S(1)} all-to-all(bf16[4,16,16,256]{3,2,1,0:T(8,128)(2,1)S(1)} %merge.1), channel_id=1, replica_groups=mesh['z'=16,'y'=4,'core'=2,'head'=4] {'y'}, dimensions={0} | all-to-all | bytes 1048576 | tf_op jit(solution)/shard_map/all_to_all | solution.py:311
  74.3 0.1 fold.1
  74.4 29.3 %all_to_all.27.parts_ref = bf16[16,16,256]{2,1,0:T(8,128)(2,1)S(1)} all-to-all(bf16[16,16,256]{2,1,0:T(8,128)(2,1)S(1)} %fold.1), channel_id=1, replica_groups=mesh['z'=16,'y'=4,'core'=2,'head'=4] {'z'}, dimensions={0} | all-to-all | bytes 262144 | tf_op jit(solution)/shard_map/all_to_all | solution.py:311
  103.7 0.6 finish.1
  (8 shorter events, 0.0 us)
Async XLA Ops:
  0.6 32.2 %collective-permute-start.2 = (bf16[256,512]{1,0:T(8,128)(2,1)}, bf16[256,512]{1,0:T(8,128)(2,1)S(1)}, u32[]{:S(2)}, u32[]{:S(2)}) collective-permute-start(bf16[256,512]{1,0:T(8,128)(2,1)} %own_ref.1), channel_id=1, source_target_pairs={{0,2},{1,3},{2,0},{3,1},{4,6},{5,7},{6,4},{7,5},{8,10},{9,11},{10,... | collective-permute-start | bytes 786440 | tf_op jit(solution)/shard_map/ppermute | solution.py:320
  6.6 26.3 %copy-start.2 = (bf16[256,512]{1,0:T(8,128)(2,1)S(1)}, bf16[256,512]{1,0:T(8,128)(2,1)}, u32[]{:S(2)}) copy-start(bf16[256,512]{1,0:T(8,128)(2,1)} %own_ref.1) | copy-start | bytes 786436
  17.6 28.7 %all-to-all-start.1 = ((bf16[16,24,128]{2,1,0:T(8,128)(2,1)}), bf16[16,24,128]{2,1,0:T(8,128)(2,1)S(1)}, u32[]{:S(2)}, u32[]{:S(2)}) async-start(bf16[16,24,128]{2,1,0:T(8,128)(2,1)} %plane_total.1), calls=%async_computation.1 | async-start | bytes 196608 | tf_op jit(solution)/shard_map/all_to_all | solution.py:311
  32.8 3.7 %copy-start = (bf16[256,128]{1,0:T(8,128)(2,1)S(1)}, bf16[256,128]{1,0:T(8,128)(2,1)}, u32[]{:S(2)}) copy-start(bf16[256,128]{1,0:T(8,128)(2,1)} %k_ref.3) | copy-start | bytes 196612
  32.8 3.7 %copy-start.1 = (bf16[256,128]{1,0:T(8,128)(2,1)S(1)}, bf16[256,128]{1,0:T(8,128)(2,1)}, u32[]{:S(2)}) copy-start(bf16[256,128]{1,0:T(8,128)(2,1)} %v_ref.3) | copy-start | bytes 196612
  33.1 5.8 %copy-start.3 = (bf16[256,256]{1,0:T(8,128)(2,1)S(1)}, bf16[256,256]{1,0:T(8,128)(2,1)}, u32[]{:S(2)}) copy-start(bf16[256,256]{1,0:T(8,128)(2,1)} %q_ref.3) | copy-start | bytes 393220
  33.1 5.8 %copy-start.4 = (bf16[256,256]{1,0:T(8,128)(2,1)S(1)}, bf16[256,256]{1,0:T(8,128)(2,1)}, u32[]{:S(2)}) copy-start(bf16[256,256]{1,0:T(8,128)(2,1)} %c_ref.3) | copy-start | bytes 393220
  33.1 23.4 %collective-permute-start.3 = (bf16[2,512,256]{2,1,0:T(8,128)(2,1)S(1)}, bf16[2,512,256]{2,1,0:T(8,128)(2,1)S(1)}, u32[]{:S(2)}, u32[]{:S(2)}) collective-permute-start(bf16[2,512,256]{2,1,0:T(8,128)(2,1)S(1)} %pair_up.1.refs_0_), channel_id=1, source_target_pairs={{0,1},{1,0},{2,3},{3,2},{4,5},{5,4},{6,7},{7,6},{8,9},{9,8},{10,11... | collective-permute-start | bytes 1572872 | tf_op jit(solution)/shard_map/ppermute | solution.py:322
  36.6 2.3 %collective-permute-start = (bf16[256,256]{1,0:T(8,128)(2,1)S(1)}, bf16[256,256]{1,0:T(8,128)(2,1)S(1)}, u32[]{:S(2)}, u32[]{:S(2)}) collective-permute-start(bf16[256,256]{1,0:T(8,128)(2,1)S(1)} %pad_maximum_fusion), channel_id=1, source_target_pairs={{0,4},{4,8},{8,12},{12,16},{16,20},{20,24},{24,28},{28,32},{32,36}... | collective-permute-start | bytes 393224 | tf_op jit(solution)/shard_map/ppermute | solution.py:307
  37.9 1.0 copy-start.5
  40.5 10.4 %collective-permute-start.1 = (f32[256,256]{1,0:T(8,128)S(1)}, f32[256,256]{1,0:T(8,128)S(1)}, u32[]{:S(2)}, u32[]{:S(2)}) collective-permute-start(f32[256,256]{1,0:T(8,128)S(1)} %get-tuple-element.7), channel_id=1, source_target_pairs={{4,0},{8,4},{12,8},{16,12},{20,16},{24,20},{28,24},{32,28},{36,32}... | collective-permute-start | bytes 786440 | tf_op jit(solution)/shard_map/ppermute | solution.py:307
  47.5 9.0 %all-to-all-start.2 = ((f32[8,16,128]{2,1,0:T(8,128)}), f32[8,16,128]{2,1,0:T(8,128)S(1)}, u32[]{:S(2)}, u32[]{:S(2)}) async-start(f32[8,16,128]{2,1,0:T(8,128)} %enter.1), calls=%async_computation.2 | async-start | bytes 131072 | tf_op jit(solution)/shard_map/all_to_all | solution.py:311
  57.8 3.8 %collective-permute-start.4 = (bf16[4,16,16,256]{3,2,1,0:T(8,128)(2,1)S(1)}, bf16[4,16,16,256]{3,2,1,0:T(8,128)(2,1)S(1)}, u32[]{:S(2)}, u32[]{:S(2)}) collective-permute-start(bf16[4,16,16,256]{3,2,1,0:T(8,128)(2,1)S(1)} %get-tuple-element.9), channel_id=1, source_target_pairs={{0,4},{4,0},{1,5},{5,1},{2,6},{6,2},{3,7},{7,3},{8,12},{12,8},{9,1... | collective-permute-start | bytes 1572872 | tf_op jit(solution)/shard_map/ppermute | solution.py:330

commit v5 on v4

--- a/solution.py
+++ b/solution.py
@@ -80,24 +80,26 @@
     )(q, c, ld)
 
 
-def pair_kernel(own_ref, got_ref, out_ref):
-    out_ref[0] = own_ref[...].T
-    out_ref[1] = got_ref[...].T
-
-
-def pair_up(own, got):
+def pair_kernel(own_ref, got_ref, ld_ref, out_ref):
+    for i, ref in enumerate((own_ref, got_ref)):
+        rows = ref[...].T.reshape(NH * NY, NC, 16, LEN)
+        for core in range(NC):
+            out_ref[i, core] = rows[:, core].reshape(XD // NC, LEN)
+
+
+def pair_up(own, got, ld):
     return pl.pallas_call(
         pair_kernel,
-        out_shape=jax.ShapeDtypeStruct((2, XD, LEN), BF16),
-        in_specs=vmem(2),
+        out_shape=jax.ShapeDtypeStruct((2, NC, XD // NC, LEN), BF16),
+        in_specs=vmem(3),
         out_specs=vmem(1)[0],
         cost_estimate=cost(0, 1000000),
         compiler_params=params(8),
         name="pair_up",
-    )(own, got)
-
-
-def local_kernel(idx_ref, q_ref, c_ref, k_ref, v_ref, prior_ref, ld_ref, own_ref, back_ref):
+    )(own, got, ld)
+
+
+def local_kernel(idx_ref, q_ref, c_ref, k_ref, v_ref, prior_ref, ld_ref, own_ref, back_ref, tail_ref):
     column, row = log_sums(ld_ref[...])
     j = lax.broadcasted_iota(jnp.int32, (LEN, LEN), 0)
     t = lax.broadcasted_iota(jnp.int32, (LEN, LEN), 1)
@@ -133,15 +135,16 @@
     own_ref[:, E:] = own_v * LIN + win_v
     back_ref[:, :E] = old_k * FACTOR
     back_ref[:, E:] = old_v
+    tail_ref[...] = jnp.broadcast_to(jnp.exp(column[LEN - 1 :, :] - column), (LEN, E))
 
 
 def local(idx, q, c, k, v, prior, ld):
     shape = jax.ShapeDtypeStruct((LEN, 2 * E), F32)
     return pl.pallas_call(
         local_kernel,
-        out_shape=(shape, shape),
+        out_shape=(shape, shape, jax.ShapeDtypeStruct((LEN, E), F32)),
         in_specs=[SMEM] + vmem(6),
-        out_specs=tuple(vmem(2)),
+        out_specs=tuple(vmem(3)),
         cost_estimate=cost(2 * 20 * LEN * LEN * E, 1200000),
         compiler_params=params(16),
         name="local",
@@ -204,45 +207,77 @@
     )(idx, got, planes)
 
 
-def weight_kernel(
-    idx_ref, state_ref, own_ref, back_ref, k_ref, v_ref, ld_ref, *refs
+def head_rows(head, i):
+    return pl.ds(lax.bitwise_xor(head, jnp.int32((0, 2, 1, 3)[i])) * NH, NH)
+
+
+def half_weights(near_ref, far_ref, grad, core, head, write):
+    for i in range(NH):
+        x = (near_ref if i < 2 else far_ref)[i % 2, core]
+        found = mm(x, grad, NN).reshape(NH, NY, 16, 2 * E)
+        for y in range(NY):
+            write(y, head_rows(head, i), found[:, y])
+
+
+def send_kernel(
+    idx_ref, state_ref, own_ref, back_ref, k_ref, v_ref, tail_ref, near_ref, far_ref, send_ref, grad_ref
 ):
-    near_ref, far_ref, keep_ref, send_ref, part = refs
-    column, _ = log_sums(ld_ref[...])
-    tail = jnp.exp(column[LEN - 1 :, :] - column)
     state = state_ref[...].reshape(E, E)
     high = state.astype(BF16)
     low = (state - high.astype(F32)).astype(BF16)
-    k, v = k_ref[...], v_ref[...]
+    k, v, tail = k_ref[...], v_ref[...], tail_ref[...]
     far_k = mm(v, high, NT) + mm(v, low, NT)
     far_v = mm(k, high, NN) + mm(k, low, NN)
-    key_grad = (own_ref[:, :E] + back_ref[:, :E] + tail * far_k).astype(BF16)
-    value_grad = (own_ref[:, E:] + back_ref[:, E:] + tail * far_v).astype(BF16)
-    grad = jnp.concatenate([key_grad, value_grad], axis=1)
-    core, head = idx_ref[2], idx_ref[3]
-    for i in range(NH):
-        x = (near_ref if i < 2 else far_ref)[i % 2]
-        found = mm(x, grad, NN).reshape(NH, NY, NC, 16, 2 * E)
-        for y in range(NY):
-            for c in range(NC):
-                part[c, y] = found[:, y, c]
-        where = pl.ds(lax.bitwise_xor(head, jnp.int32((0, 2, 1, 3)[i])) * NH, NH)
-        keep_ref[:, where] = part[core]
-        send_ref[:, where] = part[1 - core].astype(BF16)
-
-
-def weight_parts(idx, state, own, back, k, v, ld, near, far):
-    whole = (NY, NZ, 16, 2 * E)
-    return pl.pallas_call(
-        weight_kernel,
-        out_shape=(jax.ShapeDtypeStruct(whole, F32), jax.ShapeDtypeStruct(whole, BF16)),
+    grad_ref[:, :E] = (own_ref[:, :E] + back_ref[:, :E] + tail * far_k).astype(BF16)
+    grad_ref[:, E:] = (own_ref[:, E:] + back_ref[:, E:] + tail * far_v).astype(BF16)
+
+    def write(y, where, rows):
+        send_ref[y, where] = rows.astype(BF16)
+
+    half_weights(near_ref, far_ref, grad_ref[...], 1 - idx_ref[2], idx_ref[3], write)
+
+
+WHOLE = (NY, NZ, 16, 2 * E)
+
+
+def send_half(idx, *operands):
+    return pl.pallas_call(
+        send_kernel,
+        out_shape=(
+            jax.ShapeDtypeStruct(WHOLE, BF16),
+            jax.ShapeDtypeStruct((LEN, 2 * E), BF16),
+        ),
         in_specs=[SMEM] + vmem(8),
         out_specs=tuple(vmem(2)),
-        scratch_shapes=[pltpu.VMEM((NC, NY, NH, 16, 2 * E), F32)],
-        cost_estimate=cost(2 * NH * XD * LEN * 2 * E, 3500000),
+        cost_estimate=cost(NH * XD * LEN * 2 * E, 2500000),
         compiler_params=params(16),
-        name="weight_parts",
-    )(idx, state, own, back, k, v, ld, near, far)
+        name="send_half",
+    )(idx, *operands)
+
+
+def keep_kernel(idx_ref, grad_ref, near_ref, far_ref, keep_ref):
+    def write(y, where, rows):
+        keep_ref[y, where] = rows
+
+    half_weights(near_ref, far_ref, grad_ref[...], idx_ref[2], idx_ref[3], write)
+
+
+def keep_half(idx, *operands):
+    return pl.pallas_call(
+        keep_kernel,
+        out_shape=jax.ShapeDtypeStruct(WHOLE, F32),
+        in_specs=[SMEM] + vmem(3),
+        out_specs=vmem(1)[0],
+        cost_estimate=cost(NH * XD * LEN * 2 * E, 2500000),
+        compiler_params=params(16),
+        name="keep_half",
+    )(idx, *operands)
+
+
+def shifted(value, steps):
+    count = NZ * NP
+    leading, last = (max(0, -steps), min(count, count - steps))
+    return lax.ppermute(value, CTX, [(source, source + steps) for source in range(leading, last)])
 
 
 def merge_kernel(keep_ref, other_ref, out_ref):
@@ -301,12 +336,6 @@
     )(parts)
 
 
-def shifted(value, steps):
-    count = NZ * NP
-    leading, last = (max(0, -steps), min(count, count - steps))
-    return lax.ppermute(value, CTX, [(source, source + steps) for source in range(leading, last)])
-
-
 def exchange(value, axis):
     return lax.all_to_all(value, axis, 0, 0, tiled=True)
 
@@ -314,20 +343,22 @@
 def on_device(layer_input, queries, keys, values, result_cotangent, log_decay):
     axes = (CTX, "z", "core", "head")
     idx = jnp.stack([lax.axis_index(axis) for axis in axes]).astype(jnp.int32)
-    got = exchange(summary(queries, result_cotangent, log_decay), PLANE)
+    sent = summary(queries, result_cotangent, log_decay)
+    got = exchange(sent, PLANE)
     pair = jnp.concatenate([keys, values], axis=1)
     prior = shifted(pair, 1)
     opposite = lax.ppermute(layer_input, "head", [(i, i ^ 2) for i in range(NH)])
-    near = pair_up(layer_input, opposite)
+    near = pair_up(layer_input, opposite, log_decay)
     far = lax.ppermute(near, "head", [(i, i ^ 1) for i in range(NH)])
     total = plane_total(got)
     planes = exchange(total, "z")
-    own, old = local(idx, queries, result_cotangent, keys, values, prior, log_decay)
+    own, old, tail = local(idx, queries, result_cotangent, keys, values, prior, log_decay)
     back = shifted(old, -1)
     entering = enter(idx, got, planes)
     state = exchange(entering, PLANE)
-    keep, send = weight_parts(idx, state, own, back, keys, values, log_decay, near, far)
+    send, grad = send_half(idx, state, own, back, keys, values, tail, near, far)
     other = lax.ppermute(send, "core", [(0, 1), (1, 0)])
+    keep = keep_half(idx, grad, near, far)
     parts = fold(exchange(merge(keep, other), "y"))
     return finish(exchange(parts, "z"))
 

time: 105 us -> 105 us (level)
    pallas_call x3 -> x4, Pallas kernels: 3.06 us -> 3.72 us  [the longest x1 1.62 us: local(): pl.pallas_call(local_kernel, out_shape=(shape, shape, jax.ShapeDtypeStruc...]
  transfers between devices with their start and end apart: 7 -> 7, of which waited for: 4 -> 4; matrix products, arithmetic and copies ran while one was open for 0% -> 0% of each run, Pallas kernels for 5% -> 6%
where the time goes in v5:
time: 105 us; the launch traced here: 104 us
  blocking collectives  52.3 us (50%)
  starting transfers between devices  30.7 us (29%)
  waiting for transfers between devices  12 us (11%)
  Pallas kernels  8.28 us (8%)
    all_to_all x3, blocking collectives, exchange(): return lax.all_to_all(value, axis, 0, 0, tiled=True)  52.3 us
    all_to_all x2, starting transfers between devices, exchange(): return lax.all_to_all(value, axis, 0, 0, tiled=True)  18.7 us
    all_to_all x2, waiting for transfers between devices, exchange(): return lax.all_to_all(value, axis, 0, 0, tiled=True)  10.1 us
    ppermute x1, starting transfers between devices, on_device(): lax.ppermute(layer_input, 'head', [(i, i ^ 2) for i in range(NH)])  4.04 us
    ppermute x1, starting transfers between devices, on_device(): far = lax.ppermute(near, 'head', [(i, i ^ 1) for i in range(NH)])  3.47 us
    ppermute x2, starting transfers between devices, shifted(): lax.ppermute(value, CTX, [(source, source + steps) for source in range(le...  2.59 us
  transfers between devices with their start and end apart: 7, of which 4 were waited for; matrix products, arithmetic and copies ran while one was open for 0% of the time, Pallas kernels for 6%

profile of v5, /device:TPU:2, one launch (start us, length us, event | category | flops | bytes accessed | tf_op | source)
XLA Modules:
  0.0 104.2 jit_solution(9838340126380187646)
XLA Ops:
  0.6 4.0 %collective-permute-start.2 = (bf16[256,512]{1,0:T(8,128)(2,1)}, bf16[256,512]{1,0:T(8,128)(2,1)S(1)}, u32[]{:S(2)}, u32[]{:S(2)}) collective-permute-start(bf16[256,512]{1,0:T(8,128)(2,1)} %own_ref.1), channel_id=1, source_target_pairs={{0,2},{1,3},{2,0},{3,1},{4,6},{5,7},{6,4},{7,5},{8,10},{9,11},{10,... | collective-permute-start | bytes 786440 | tf_op jit(solution)/shard_map/ppermute | solution.py:350
  4.7 1.9 %summary.1 = f32[8,24,128]{2,1,0:T(8,128)} custom-call(bf16[256,256]{1,0:T(8,128)(2,1)} %q_ref.3, bf16[256,256]{1,0:T(8,128)(2,1)} %c_ref.3, f32[1,256]{1,0:T(1,128)} %ld_ref.5), custom_call_target="tpu_custom_call" | custom-call | flops 16777216 | bytes 400000 | tf_op jit(solution)/shard_map/summary/pallas_call | solution.py:72
  6.6 10.4 %all_to_all.25.got_ref = f32[8,24,128]{2,1,0:T(8,128)S(1)} all-to-all(f32[8,24,128]{2,1,0:T(8,128)} %summary.1), channel_id=1, replica_groups=mesh['z'=16,'y'=4,'core'=2,'head'=4] {'y','core'}, dimensions={0} | all-to-all | bytes 196608 | tf_op jit(solution)/shard_map/all_to_all | solution.py:340
  17.0 0.7 plane_total.1
  17.6 15.3 %all-to-all-start.1 = ((bf16[16,24,128]{2,1,0:T(8,128)(2,1)}), bf16[16,24,128]{2,1,0:T(8,128)(2,1)S(1)}, u32[]{:S(2)}, u32[]{:S(2)}) async-start(bf16[16,24,128]{2,1,0:T(8,128)(2,1)} %plane_total.1), calls=%async_computation.1 | async-start | bytes 196608 | tf_op jit(solution)/shard_map/all_to_all | solution.py:340
  33.0 0.0 copy-start.1
  33.0 0.0 copy-start.2
  33.0 0.0 collective-permute-done.2.got_ref
  33.0 0.2 pair_up.1.near_ref
  33.2 0.0 copy-start.3
  33.2 0.0 copy-start.4
  33.2 3.5 %collective-permute-start.3 = (bf16[2,2,256,256]{3,2,1,0:T(8,128)(2,1)S(1)}, bf16[2,2,256,256]{3,2,1,0:T(8,128)(2,1)S(1)}, u32[]{:S(2)}, u32[]{:S(2)}) collective-permute-start(bf16[2,2,256,256]{3,2,1,0:T(8,128)(2,1)S(1)} %pair_up.1.near_ref), channel_id=1, source_target_pairs={{0,1},{1,0},{2,3},{3,2},{4,5},{5,4},{6,7},{7,6},{8,9},{9,8},{10,11... | collective-permute-start | bytes 1572872 | tf_op jit(solution)/shard_map/ppermute | solution.py:352
  36.8 1.3 %collective-permute-start = (bf16[256,256]{1,0:T(8,128)(2,1)S(1)}, bf16[256,256]{1,0:T(8,128)(2,1)S(1)}, u32[]{:S(2)}, u32[]{:S(2)}) collective-permute-start(bf16[256,256]{1,0:T(8,128)(2,1)S(1)} %pad_maximum_fusion), channel_id=1, source_target_pairs={{0,4},{4,8},{8,12},{12,16},{16,20},{20,24},{24,28},{28,32},{32,36}... | collective-permute-start | bytes 393224 | tf_op jit(solution)/shard_map/ppermute | solution.py:280
  38.1 0.1 pad_add_fusion.idx_ref
  38.2 0.9 collective-permute-done.prior_ref
  39.0 1.6 %local.1 = (f32[256,256]{1,0:T(8,128)S(1)}, f32[256,256]{1,0:T(8,128)S(1)}, f32[256,128]{1,0:T(8,128)S(1)}) custom-call(s32[4]{0:T(128)S(1)} %pad_add_fusion.idx_ref, bf16[256,256]{1,0:T(8,128)(2,1)S(1)} %copy-done.3, bf16[256,256]{1,0:T(8,128)(2,1)S(1)} %copy-done.4, bf16[256,128]{1,0:T(8,128)(2,1)S(1)} %copy-done.1, bf16[256,128]{1,0:T(8,128)(2,1)S(1)} %copy-done.2, ...), custom_call_target="tpu_custom_call" | custom-call | flops 335544320 | bytes 1200000 | tf_op jit(solution)/shard_map/local/pallas_call | solution.py:143
  40.7 1.3 %collective-permute-start.1 = (f32[256,256]{1,0:T(8,128)S(1)}, f32[256,256]{1,0:T(8,128)S(1)}, u32[]{:S(2)}, u32[]{:S(2)}) collective-permute-start(f32[256,256]{1,0:T(8,128)S(1)} %get-tuple-element.8), channel_id=1, source_target_pairs={{4,0},{8,4},{12,8},{16,12},{20,16},{24,20},{28,24},{32,28},{36,32}... | collective-permute-start | bytes 786440 | tf_op jit(solution)/shard_map/ppermute | solution.py:280
  42.0 4.5 %all-to-all-done.1.planes_ref = bf16[16,24,128]{2,1,0:T(8,128)(2,1)S(1)} async-done(((bf16[16,24,128]{2,1,0:T(8,128)(2,1)}), bf16[16,24,128]{2,1,0:T(8,128)(2,1)S(1)}, u32[]{:S(2)}, u32[]{:S(2)}) %all-to-all-start.1) | async-done | bytes 98336 | tf_op jit(solution)/shard_map/all_to_all | solution.py:340
  46.4 1.2 %enter.1 = f32[8,16,128]{2,1,0:T(8,128)} custom-call(s32[4]{0:T(128)S(1)} %pad_add_fusion.idx_ref, f32[8,24,128]{2,1,0:T(8,128)S(1)} %all_to_all.25.got_ref, bf16[16,24,128]{2,1,0:T(8,128)(2,1)S(1)} %all-to-all-done.1.planes_ref), custom_call_target="tpu_custom_call" | custom-call | bytes 400000 | tf_op jit(solution)/shard_map/enter/pallas_call | solution.py:199
  47.7 3.4 %all-to-all-start.2 = ((f32[8,16,128]{2,1,0:T(8,128)}), f32[8,16,128]{2,1,0:T(8,128)S(1)}, u32[]{:S(2)}, u32[]{:S(2)}) async-start(f32[8,16,128]{2,1,0:T(8,128)} %enter.1), calls=%async_computation.2 | async-start | bytes 131072 | tf_op jit(solution)/shard_map/all_to_all | solution.py:340
  51.1 0.0 collective-permute-done.1.back_ref
  51.1 5.6 %all-to-all-done.2.state_ref = f32[8,16,128]{2,1,0:T(8,128)S(1)} async-done(((f32[8,16,128]{2,1,0:T(8,128)}), f32[8,16,128]{2,1,0:T(8,128)S(1)}, u32[]{:S(2)}, u32[]{:S(2)}) %all-to-all-start.2) | async-done | bytes 65568 | tf_op jit(solution)/shard_map/all_to_all | solution.py:340
  56.7 0.0 collective-permute-done.3.far_ref
  56.7 1.1 %send_half.1 = (bf16[4,16,16,256]{3,2,1,0:T(8,128)(2,1)S(1)}, bf16[256,256]{1,0:T(8,128)(2,1)S(1)}) custom-call(s32[4]{0:T(128)S(1)} %pad_add_fusion.idx_ref, f32[8,16,128]{2,1,0:T(8,128)S(1)} %all-to-all-done.2.state_ref, f32[256,256]{1,0:T(8,128)S(1)} %get-tuple-element.7.own_ref, f32[256,256]{1,0:T(8,128)S(1)} %collective-permute-done.1.back_ref, ...), custom_call_target="tpu_custom_call" | custom-call | flops 134217728 | bytes 2500000 | tf_op jit(solution)/shard_map/send_half/pallas_call | solution.py:244
  57.8 1.9 %collective-permute-start.4 = (bf16[4,16,16,256]{3,2,1,0:T(8,128)(2,1)S(1)}, bf16[4,16,16,256]{3,2,1,0:T(8,128)(2,1)S(1)}, u32[]{:S(2)}, u32[]{:S(2)}) collective-permute-start(bf16[4,16,16,256]{3,2,1,0:T(8,128)(2,1)S(1)} %get-tuple-element.11), channel_id=1, source_target_pairs={{0,4},{4,0},{1,5},{5,1},{2,6},{6,2},{3,7},{7,3},{8,12},{12,8},{9,1... | collective-permute-start | bytes 1572872 | tf_op jit(solution)/shard_map/ppermute | solution.py:360
  59.7 0.9 keep_half.1.keep_ref
  60.6 1.0 collective-permute-done.4.other_ref
  61.6 0.1 merge.1
  61.7 12.6 %all_to_all.26.parts_ref = bf16[4,16,16,256]{3,2,1,0:T(8,128)(2,1)S(1)} all-to-all(bf16[4,16,16,256]{3,2,1,0:T(8,128)(2,1)S(1)} %merge.1), channel_id=1, replica_groups=mesh['z'=16,'y'=4,'core'=2,'head'=4] {'y'}, dimensions={0} | all-to-all | bytes 1048576 | tf_op jit(solution)/shard_map/all_to_all | solution.py:340
  74.3 0.1 fold.1
  74.3 29.3 %all_to_all.27.parts_ref = bf16[16,16,256]{2,1,0:T(8,128)(2,1)S(1)} all-to-all(bf16[16,16,256]{2,1,0:T(8,128)(2,1)S(1)} %fold.1), channel_id=1, replica_groups=mesh['z'=16,'y'=4,'core'=2,'head'=4] {'z'}, dimensions={0} | all-to-all | bytes 262144 | tf_op jit(solution)/shard_map/all_to_all | solution.py:340
  103.6 0.6 finish.1
  (9 shorter events, 0.0 us)
Async XLA Ops:
  0.6 32.4 %collective-permute-start.2 = (bf16[256,512]{1,0:T(8,128)(2,1)}, bf16[256,512]{1,0:T(8,128)(2,1)S(1)}, u32[]{:S(2)}, u32[]{:S(2)}) collective-permute-start(bf16[256,512]{1,0:T(8,128)(2,1)} %own_ref.1), channel_id=1, source_target_pairs={{0,2},{1,3},{2,0},{3,1},{4,6},{5,7},{6,4},{7,5},{8,10},{9,11},{10,... | collective-permute-start | bytes 786440 | tf_op jit(solution)/shard_map/ppermute | solution.py:350
  6.6 26.4 %copy-start = (bf16[256,512]{1,0:T(8,128)(2,1)S(1)}, bf16[256,512]{1,0:T(8,128)(2,1)}, u32[]{:S(2)}) copy-start(bf16[256,512]{1,0:T(8,128)(2,1)} %own_ref.1) | copy-start | bytes 786436
  17.6 15.4 %copy-start.5 = (f32[1,256]{1,0:T(1,128)S(1)}, f32[1,256]{1,0:T(1,128)}, u32[]{:S(2)}) copy-start(f32[1,256]{1,0:T(1,128)} %ld_ref.5) | copy-start | bytes 3076
  17.6 28.8 %all-to-all-start.1 = ((bf16[16,24,128]{2,1,0:T(8,128)(2,1)}), bf16[16,24,128]{2,1,0:T(8,128)(2,1)S(1)}, u32[]{:S(2)}, u32[]{:S(2)}) async-start(bf16[16,24,128]{2,1,0:T(8,128)(2,1)} %plane_total.1), calls=%async_computation.1 | async-start | bytes 196608 | tf_op jit(solution)/shard_map/all_to_all | solution.py:340
  33.0 3.8 %copy-start.1 = (bf16[256,128]{1,0:T(8,128)(2,1)S(1)}, bf16[256,128]{1,0:T(8,128)(2,1)}, u32[]{:S(2)}) copy-start(bf16[256,128]{1,0:T(8,128)(2,1)} %k_ref.3) | copy-start | bytes 196612
  33.0 3.8 %copy-start.2 = (bf16[256,128]{1,0:T(8,128)(2,1)S(1)}, bf16[256,128]{1,0:T(8,128)(2,1)}, u32[]{:S(2)}) copy-start(bf16[256,128]{1,0:T(8,128)(2,1)} %v_ref.3) | copy-start | bytes 196612
  33.2 5.8 %copy-start.3 = (bf16[256,256]{1,0:T(8,128)(2,1)S(1)}, bf16[256,256]{1,0:T(8,128)(2,1)}, u32[]{:S(2)}) copy-start(bf16[256,256]{1,0:T(8,128)(2,1)} %q_ref.3) | copy-start | bytes 393220
  33.2 5.8 %copy-start.4 = (bf16[256,256]{1,0:T(8,128)(2,1)S(1)}, bf16[256,256]{1,0:T(8,128)(2,1)}, u32[]{:S(2)}) copy-start(bf16[256,256]{1,0:T(8,128)(2,1)} %c_ref.3) | copy-start | bytes 393220
  33.2 23.5 %collective-permute-start.3 = (bf16[2,2,256,256]{3,2,1,0:T(8,128)(2,1)S(1)}, bf16[2,2,256,256]{3,2,1,0:T(8,128)(2,1)S(1)}, u32[]{:S(2)}, u32[]{:S(2)}) collective-permute-start(bf16[2,2,256,256]{3,2,1,0:T(8,128)(2,1)S(1)} %pair_up.1.near_ref), channel_id=1, source_target_pairs={{0,1},{1,0},{2,3},{3,2},{4,5},{5,4},{6,7},{7,6},{8,9},{9,8},{10,11... | collective-permute-start | bytes 1572872 | tf_op jit(solution)/shard_map/ppermute | solution.py:352
  36.8 2.3 %collective-permute-start = (bf16[256,256]{1,0:T(8,128)(2,1)S(1)}, bf16[256,256]{1,0:T(8,128)(2,1)S(1)}, u32[]{:S(2)}, u32[]{:S(2)}) collective-permute-start(bf16[256,256]{1,0:T(8,128)(2,1)S(1)} %pad_maximum_fusion), channel_id=1, source_target_pairs={{0,4},{4,8},{8,12},{12,16},{16,20},{20,24},{24,28},{28,32},{32,36}... | collective-permute-start | bytes 393224 | tf_op jit(solution)/shard_map/ppermute | solution.py:280
  40.7 10.4 %collective-permute-start.1 = (f32[256,256]{1,0:T(8,128)S(1)}, f32[256,256]{1,0:T(8,128)S(1)}, u32[]{:S(2)}, u32[]{:S(2)}) collective-permute-start(f32[256,256]{1,0:T(8,128)S(1)} %get-tuple-element.8), channel_id=1, source_target_pairs={{4,0},{8,4},{12,8},{16,12},{20,16},{24,20},{28,24},{32,28},{36,32}... | collective-permute-start | bytes 786440 | tf_op jit(solution)/shard_map/ppermute | solution.py:280
  47.7 9.0 %all-to-all-start.2 = ((f32[8,16,128]{2,1,0:T(8,128)}), f32[8,16,128]{2,1,0:T(8,128)S(1)}, u32[]{:S(2)}, u32[]{:S(2)}) async-start(f32[8,16,128]{2,1,0:T(8,128)} %enter.1), calls=%async_computation.2 | async-start | bytes 131072 | tf_op jit(solution)/shard_map/all_to_all | solution.py:340
  57.8 3.8 %collective-permute-start.4 = (bf16[4,16,16,256]{3,2,1,0:T(8,128)(2,1)S(1)}, bf16[4,16,16,256]{3,2,1,0:T(8,128)(2,1)S(1)}, u32[]{:S(2)}, u32[]{:S(2)}) collective-permute-start(bf16[4,16,16,256]{3,2,1,0:T(8,128)(2,1)S(1)} %get-tuple-element.11), channel_id=1, source_target_pairs={{0,4},{4,0},{1,5},{5,1},{2,6},{6,2},{3,7},{7,3},{8,12},{12,8},{9,1... | collective-permute-start | bytes 1572872 | tf_op jit(solution)/shard_map/ppermute | solution.py:360

commit v6 on v5

--- a/solution.py
+++ b/solution.py
@@ -3,12 +3,13 @@
 from jax import lax
 from jax.experimental import pallas as pl
 from jax.experimental.pallas import tpu as pltpu
-from jax.sharding import Mesh, PartitionSpec as P
+from jax.sharding import PartitionSpec as P
 
 
 E = 128
 LEN = 256
-NZ, NY, NC = 16, 4, 2
+NA, NB, NY, NC = 8, 2, 4, 2
+NZ = NA * NB
 NP = NY * NC
 NH = 4
 XD = 512
@@ -19,8 +20,39 @@
 
 neg_fill = -1e30
 
-PLANE = ("y", "core")
-CTX = ("z", "y", "core")
+
+FIRST, ACROSS, LAST, NEAR, FAR = 7, 10, 0, 7, 4
+
+
+def place(z, y, core):
+    return (z * NY + y) * NC + core
+
+
+def plane_groups(lead):
+    return [[z * NP + (q ^ lead) for q in range(NP)] for z in range(NZ)]
+
+
+def z_groups(lead):
+    return [[(q ^ lead) * NP + p for q in range(NZ)] for p in range(NP)]
+
+
+def near_groups(lead):
+    members = [(q ^ lead) for q in range(NB * NY)]
+    return [
+        [place(a * NB + m // NY, m % NY, core) for m in members]
+        for a in range(NA)
+        for core in range(NC)
+    ]
+
+
+def far_groups(lead):
+    return [
+        [place((q ^ lead) * NB + b, y, core) for q in range(NA)]
+        for b in range(NB)
+        for y in range(NY)
+        for core in range(NC)
+    ]
+
 
 NN = (((1,), (0,)), ((), ()))
 NT = (((1,), (1,)), ((), ()))
@@ -64,8 +96,8 @@
         total += mm(q_ref[:, cols], (grow * half).astype(BF16), TN)
     last = jnp.broadcast_to(column[LEN - 1 :, :], (8, E))
     for m in range(NP):
-        out_ref[m, :ROWS, :] = total[m * ROWS : (m + 1) * ROWS] * LIN
-        out_ref[m, ROWS:, :] = last
+        out_ref[m ^ FIRST, :ROWS, :] = total[m * ROWS : (m + 1) * ROWS] * LIN
+        out_ref[m ^ FIRST, ROWS:, :] = last
 
 
 def summary(q, c, ld):
@@ -156,9 +188,9 @@
     low, high = jnp.zeros((8, E), F32), jnp.zeros((8, E), F32)
     for k in range(NP):
         weight = jnp.exp(log)
-        low += weight * got_ref[k, 0:8, :]
-        high += weight * got_ref[k, 8:16, :]
-        log += got_ref[k, ROWS:, :]
+        low += weight * got_ref[k ^ FIRST, 0:8, :]
+        high += weight * got_ref[k ^ FIRST, 8:16, :]
+        log += got_ref[k ^ FIRST, ROWS:, :]
     row = lax.broadcasted_iota(jnp.int32, (8, E), 0)
     first = log.astype(BF16).astype(F32)
     second = (log - first).astype(BF16).astype(F32)
@@ -182,17 +214,18 @@
 
 
 def enter_kernel(idx_ref, got_ref, planes_ref, out_ref):
-    mine = idx_ref[1]
+    mine = lax.div(idx_ref[0], jnp.int32(NP))
     log = jnp.zeros((1, E), F32)
     state = jnp.zeros((ROWS, E), F32)
     for z in range(NZ):
         later = z > mine
-        plane = planes_ref[z].astype(F32)
+        plane = planes_ref[z ^ ACROSS].astype(F32)
         state += jnp.where(later, jnp.exp(log), 0.0) * plane[:ROWS]
         log += jnp.where(later, jnp.sum(plane[ROWS:], axis=0, keepdims=True), 0.0)
     for k in range(NP - 1, -1, -1):
-        out_ref[k] = state
-        state = got_ref[k, :ROWS, :] + jnp.exp(got_ref[k, ROWS : ROWS + 1, :]) * state
+        out_ref[k ^ LAST] = state
+        block = got_ref[k ^ FIRST]
+        state = block[:ROWS] + jnp.exp(block[ROWS : ROWS + 1]) * state
 
 
 def enter(idx, got, planes):
@@ -207,22 +240,22 @@
     )(idx, got, planes)
 
 
-def head_rows(head, i):
-    return pl.ds(lax.bitwise_xor(head, jnp.int32((0, 2, 1, 3)[i])) * NH, NH)
-
-
 def half_weights(near_ref, far_ref, grad, core, head, write):
     for i in range(NH):
         x = (near_ref if i < 2 else far_ref)[i % 2, core]
-        found = mm(x, grad, NN).reshape(NH, NY, 16, 2 * E)
-        for y in range(NY):
-            write(y, head_rows(head, i), found[:, y])
+        found = mm(x, grad, NN).reshape(NH // NB, NB, NY, 16, 2 * E)
+        shard = lax.bitwise_xor(head, jnp.int32((0, 2, 1, 3)[i]))
+        count = NH // NB
+        where = pl.ds(lax.bitwise_xor(shard, jnp.int32(FAR // count)) * count, count)
+        for b in range(NB):
+            for y in range(NY):
+                write((b * NY + y) ^ NEAR, where, found[:, b, y])
 
 
 def send_kernel(
     idx_ref, state_ref, own_ref, back_ref, k_ref, v_ref, tail_ref, near_ref, far_ref, send_ref, grad_ref
 ):
-    state = state_ref[...].reshape(E, E)
+    state = jnp.concatenate([state_ref[m ^ LAST] for m in range(NP)], axis=0)
     high = state.astype(BF16)
     low = (state - high.astype(F32)).astype(BF16)
     k, v, tail = k_ref[...], v_ref[...], tail_ref[...]
@@ -231,13 +264,13 @@
     grad_ref[:, :E] = (own_ref[:, :E] + back_ref[:, :E] + tail * far_k).astype(BF16)
     grad_ref[:, E:] = (own_ref[:, E:] + back_ref[:, E:] + tail * far_v).astype(BF16)
 
-    def write(y, where, rows):
-        send_ref[y, where] = rows.astype(BF16)
-
-    half_weights(near_ref, far_ref, grad_ref[...], 1 - idx_ref[2], idx_ref[3], write)
-
-
-WHOLE = (NY, NZ, 16, 2 * E)
+    def write(near, where, rows):
+        send_ref[near, where] = rows.astype(BF16)
+
+    half_weights(near_ref, far_ref, grad_ref[...], 1 - lax.rem(idx_ref[0], jnp.int32(NC)), idx_ref[1], write)
+
+
+WHOLE = (NB * NY, NA, 16, 2 * E)
 
 
 def send_half(idx, *operands):
@@ -256,10 +289,10 @@
 
 
 def keep_kernel(idx_ref, grad_ref, near_ref, far_ref, keep_ref):
-    def write(y, where, rows):
-        keep_ref[y, where] = rows
-
-    half_weights(near_ref, far_ref, grad_ref[...], idx_ref[2], idx_ref[3], write)
+    def write(near, where, rows):
+        keep_ref[near, where] = rows
+
+    half_weights(near_ref, far_ref, grad_ref[...], lax.rem(idx_ref[0], jnp.int32(NC)), idx_ref[1], write)
 
 
 def keep_half(idx, *operands):
@@ -277,7 +310,7 @@
 def shifted(value, steps):
     count = NZ * NP
     leading, last = (max(0, -steps), min(count, count - steps))
-    return lax.ppermute(value, CTX, [(source, source + steps) for source in range(leading, last)])
+    return lax.ppermute(value, "ctx", [(source, source + steps) for source in range(leading, last)])
 
 
 def merge_kernel(keep_ref, other_ref, out_ref):
@@ -296,11 +329,15 @@
     )(keep, other)
 
 
+def summed(parts_ref):
+    total = parts_ref[0].astype(F32)
+    for i in range(1, parts_ref.shape[0]):
+        total += parts_ref[i].astype(F32)
+    return total
+
+
 def fold_kernel(parts_ref, out_ref):
-    total = parts_ref[0].astype(F32)
-    for y in range(1, NY):
-        total += parts_ref[y].astype(F32)
-    out_ref[...] = total.astype(BF16)
+    out_ref[...] = summed(parts_ref).astype(BF16)
 
 
 def fold(parts):
@@ -309,16 +346,14 @@
         out_shape=jax.ShapeDtypeStruct(parts.shape[1:], BF16),
         in_specs=vmem(1),
         out_specs=vmem(1)[0],
-        cost_estimate=cost(0, 700000),
+        cost_estimate=cost(0, 600000),
         compiler_params=params(8),
         name="fold",
     )(parts)
 
 
 def finish_kernel(parts_ref, key_ref, value_ref):
-    total = parts_ref[0].astype(F32)
-    for z in range(1, NZ):
-        total += parts_ref[z].astype(F32)
+    total = summed(parts_ref)
     key_ref[...] = total[:, :E].astype(BF16)
     value_ref[...] = total[:, E:].astype(BF16)
 
@@ -336,38 +371,36 @@
     )(parts)
 
 
-def exchange(value, axis):
-    return lax.all_to_all(value, axis, 0, 0, tiled=True)
+def exchange(value, groups):
+    return lax.all_to_all(value, "ctx", 0, 0, axis_index_groups=groups, tiled=True)
 
 
 def on_device(layer_input, queries, keys, values, result_cotangent, log_decay):
-    axes = (CTX, "z", "core", "head")
-    idx = jnp.stack([lax.axis_index(axis) for axis in axes]).astype(jnp.int32)
+    idx = jnp.stack([lax.axis_index("ctx"), lax.axis_index("head")]).astype(jnp.int32)
     sent = summary(queries, result_cotangent, log_decay)
-    got = exchange(sent, PLANE)
+    got = exchange(sent, plane_groups(FIRST))
     pair = jnp.concatenate([keys, values], axis=1)
     prior = shifted(pair, 1)
     opposite = lax.ppermute(layer_input, "head", [(i, i ^ 2) for i in range(NH)])
     near = pair_up(layer_input, opposite, log_decay)
     far = lax.ppermute(near, "head", [(i, i ^ 1) for i in range(NH)])
     total = plane_total(got)
-    planes = exchange(total, "z")
+    planes = exchange(total, z_groups(ACROSS))
     own, old, tail = local(idx, queries, result_cotangent, keys, values, prior, log_decay)
     back = shifted(old, -1)
     entering = enter(idx, got, planes)
-    state = exchange(entering, PLANE)
+    state = exchange(entering, plane_groups(LAST))
     send, grad = send_half(idx, state, own, back, keys, values, tail, near, far)
-    other = lax.ppermute(send, "core", [(0, 1), (1, 0)])
+    other = lax.ppermute(send, "ctx", [(i, i ^ 1) for i in range(NZ * NP)])
     keep = keep_half(idx, grad, near, far)
-    parts = fold(exchange(merge(keep, other), "y"))
-    return finish(exchange(parts, "z"))
+    parts = fold(exchange(merge(keep, other), near_groups(NEAR)))
+    return finish(exchange(parts, far_groups(FAR)))
 
 
 def solution(mesh):
-    fine = Mesh(mesh.devices.reshape(NZ, NY, NC, NH), CTX + ("head",))
-    rows = P(CTX, "head")
-    in_specs = (rows, rows, rows, rows, rows, P("head", CTX))
+    rows = P("ctx", "head")
+    in_specs = (rows, rows, rows, rows, rows, P("head", "ctx"))
 
     return jax.shard_map(
-        on_device, mesh=fine, in_specs=in_specs, out_specs=(rows, rows), check_vma=False
+        on_device, mesh=mesh, in_specs=in_specs, out_specs=(rows, rows), check_vma=False
     )

time: 105 us -> 94 us (0.90)
  blocking collectives: 52.3 us -> 39.3 us
  starting transfers between devices: 30.7 us -> 37.3 us
  waiting for transfers between devices: 12 us -> 7.52 us
    all_to_all x3, blocking collectives: 52.3 us -> 39.3 us  [exchange(): lax.all_to_all(value, 'ctx', 0, 0, axis_index_groups=groups, tiled=True)]
    all_to_all x2, starting transfers between devices: 18.7 us -> 25.3 us  [exchange(): lax.all_to_all(value, 'ctx', 0, 0, axis_index_groups=groups, tiled=True)]
    all_to_all x2, waiting for transfers between devices: 10.1 us -> 5.62 us  [exchange(): lax.all_to_all(value, 'ctx', 0, 0, axis_index_groups=groups, tiled=True)]
  transfers between devices with their start and end apart: 7 -> 7, of which waited for: 4 -> 3; matrix products, arithmetic and copies ran while one was open for 0% -> 0% of each run, Pallas kernels for 6% -> 7%
where the time goes in v6:
time: 94 us; the launch traced here: 93.4 us
  blocking collectives  39.3 us (42%)
  starting transfers between devices  37.3 us (40%)
  Pallas kernels  8.27 us (9%)
  waiting for transfers between devices  7.52 us (8%)
    all_to_all x3, blocking collectives, exchange(): lax.all_to_all(value, 'ctx', 0, 0, axis_index_groups=groups, tiled=True)  39.3 us
    all_to_all x2, starting transfers between devices, exchange(): lax.all_to_all(value, 'ctx', 0, 0, axis_index_groups=groups, tiled=True)  25.3 us
    all_to_all x2, waiting for transfers between devices, exchange(): lax.all_to_all(value, 'ctx', 0, 0, axis_index_groups=groups, tiled=True)  5.62 us
    ppermute x1, starting transfers between devices, on_device(): lax.ppermute(layer_input, 'head', [(i, i ^ 2) for i in range(NH)])  4.04 us
    ppermute x1, starting transfers between devices, on_device(): far = lax.ppermute(near, 'head', [(i, i ^ 1) for i in range(NH)])  3.47 us
    ppermute x2, starting transfers between devices, shifted(): lax.ppermute(value, 'ctx', [(source, source + steps) for source in range(...  2.59 us
    ppermute x1, starting transfers between devices, on_device(): other = lax.ppermute(send, 'ctx', [(i, i ^ 1) for i in range(NZ * NP)])  1.92 us
    pallas_call x1, Pallas kernels, summary(): pl.pallas_call(summary_kernel, out_shape=jax.ShapeDtypeStruct((NP, ROWS +...  1.9 us
  transfers between devices with their start and end apart: 7, of which 3 were waited for; matrix products, arithmetic and copies ran while one was open for 0% of the time, Pallas kernels for 7%

profile of v6, /device:TPU:2, one launch (start us, length us, event | category | flops | bytes accessed | tf_op | source)
XLA Modules:
  0.0 93.4 jit_solution(599795176650359009)
XLA Ops:
  0.6 4.0 %collective-permute-start.2 = (bf16[256,512]{1,0:T(8,128)(2,1)}, bf16[256,512]{1,0:T(8,128)(2,1)S(1)}, u32[]{:S(2)}, u32[]{:S(2)}) collective-permute-start(bf16[256,512]{1,0:T(8,128)(2,1)} %own_ref.1), channel_id=1, source_target_pairs={{0,2},{1,3},{2,0},{3,1},{4,6},{5,7},{6,4},{7,5},{8,10},{9,11},{10,... | collective-permute-start | bytes 786440 | tf_op jit(solution)/shard_map/ppermute | solution.py:384
  4.7 1.9 %summary.1 = f32[8,24,128]{2,1,0:T(8,128)} custom-call(bf16[256,256]{1,0:T(8,128)(2,1)} %q_ref.3, bf16[256,256]{1,0:T(8,128)(2,1)} %c_ref.3, f32[1,256]{1,0:T(1,128)} %ld_ref.5), custom_call_target="tpu_custom_call" | custom-call | flops 16777216 | bytes 400000 | tf_op jit(solution)/shard_map/summary/pallas_call | solution.py:104
  6.6 9.3 %all_to_all.25.got_ref = f32[8,24,128]{2,1,0:T(8,128)S(1)} all-to-all(f32[8,24,128]{2,1,0:T(8,128)} %summary.1), channel_id=1, replica_groups={{28,24,20,16,12,8,4,0},{60,56,52,48,44,40,36,32},{92,88,84,80,76,72,68,..., dimensions={0} | all-to-all | bytes 196608 | tf_op jit(solution)/shard_map/all_to_all | solution.py:375
  15.9 0.7 plane_total.1
  16.5 17.2 %all-to-all-start.1 = ((bf16[16,24,128]{2,1,0:T(8,128)(2,1)}), bf16[16,24,128]{2,1,0:T(8,128)(2,1)S(1)}, u32[]{:S(2)}, u32[]{:S(2)}) async-start(bf16[16,24,128]{2,1,0:T(8,128)(2,1)} %plane_total.1), calls=%async_computation.1 | async-start | bytes 196608 | tf_op jit(solution)/shard_map/all_to_all | solution.py:375
  33.7 0.0 copy-start.2
  33.7 0.0 collective-permute-done.2.got_ref
  33.8 0.2 pair_up.1.near_ref
  34.0 0.0 copy-start.3
  34.0 0.0 copy-start.4
  34.0 3.5 %collective-permute-start.3 = (bf16[2,2,256,256]{3,2,1,0:T(8,128)(2,1)S(1)}, bf16[2,2,256,256]{3,2,1,0:T(8,128)(2,1)S(1)}, u32[]{:S(2)}, u32[]{:S(2)}) collective-permute-start(bf16[2,2,256,256]{3,2,1,0:T(8,128)(2,1)S(1)} %pair_up.1.near_ref), channel_id=1, source_target_pairs={{0,1},{1,0},{2,3},{3,2},{4,5},{5,4},{6,7},{7,6},{8,9},{9,8},{10,11... | collective-permute-start | bytes 1572872 | tf_op jit(solution)/shard_map/ppermute | solution.py:386
  37.5 1.3 %collective-permute-start = (bf16[256,256]{1,0:T(8,128)(2,1)S(1)}, bf16[256,256]{1,0:T(8,128)(2,1)S(1)}, u32[]{:S(2)}, u32[]{:S(2)}) collective-permute-start(bf16[256,256]{1,0:T(8,128)(2,1)S(1)} %pad_maximum_fusion), channel_id=1, source_target_pairs={{0,4},{4,8},{8,12},{12,16},{16,20},{20,24},{24,28},{28,32},{32,36}... | collective-permute-start | bytes 393224 | tf_op jit(solution)/shard_map/ppermute | solution.py:313
  38.8 0.1 pad_add_fusion.idx_ref
  38.9 0.9 collective-permute-done.prior_ref
  39.8 0.0 copy-done.3
  39.8 1.6 %local.1 = (f32[256,256]{1,0:T(8,128)S(1)}, f32[256,256]{1,0:T(8,128)S(1)}, f32[256,128]{1,0:T(8,128)S(1)}) custom-call(s32[2]{0:T(128)S(1)} %pad_add_fusion.idx_ref, bf16[256,256]{1,0:T(8,128)(2,1)S(1)} %copy-done.3, bf16[256,256]{1,0:T(8,128)(2,1)S(1)} %copy-done.4, bf16[256,128]{1,0:T(8,128)(2,1)S(1)} %copy-done.1, bf16[256,128]{1,0:T(8,128)(2,1)S(1)} %copy-done.2, ...), custom_call_target="tpu_custom_call" | custom-call | flops 335544320 | bytes 1200000 | tf_op jit(solution)/shard_map/local/pallas_call | solution.py:175
  41.4 1.3 %collective-permute-start.1 = (f32[256,256]{1,0:T(8,128)S(1)}, f32[256,256]{1,0:T(8,128)S(1)}, u32[]{:S(2)}, u32[]{:S(2)}) collective-permute-start(f32[256,256]{1,0:T(8,128)S(1)} %get-tuple-element.8), channel_id=1, source_target_pairs={{4,0},{8,4},{12,8},{16,12},{20,16},{24,20},{28,24},{32,28},{36,32}... | collective-permute-start | bytes 786440 | tf_op jit(solution)/shard_map/ppermute | solution.py:313
  42.7 0.0 all-to-all-done.1.planes_ref
  42.7 1.2 %enter.1 = f32[8,16,128]{2,1,0:T(8,128)} custom-call(s32[2]{0:T(128)S(1)} %pad_add_fusion.idx_ref, f32[8,24,128]{2,1,0:T(8,128)S(1)} %all_to_all.25.got_ref, bf16[16,24,128]{2,1,0:T(8,128)(2,1)S(1)} %all-to-all-done.1.planes_ref), custom_call_target="tpu_custom_call" | custom-call | bytes 400000 | tf_op jit(solution)/shard_map/enter/pallas_call | solution.py:232
  43.9 8.1 %all-to-all-start.2 = ((f32[8,16,128]{2,1,0:T(8,128)}), f32[8,16,128]{2,1,0:T(8,128)S(1)}, u32[]{:S(2)}, u32[]{:S(2)}) async-start(f32[8,16,128]{2,1,0:T(8,128)} %enter.1), calls=%async_computation.2 | async-start | bytes 131072 | tf_op jit(solution)/shard_map/all_to_all | solution.py:375
  52.0 0.0 collective-permute-done.1.back_ref
  52.1 5.6 %all-to-all-done.2.state_ref = f32[8,16,128]{2,1,0:T(8,128)S(1)} async-done(((f32[8,16,128]{2,1,0:T(8,128)}), f32[8,16,128]{2,1,0:T(8,128)S(1)}, u32[]{:S(2)}, u32[]{:S(2)}) %all-to-all-start.2) | async-done | bytes 65568 | tf_op jit(solution)/shard_map/all_to_all | solution.py:375
  57.7 0.0 collective-permute-done.3.far_ref
  57.7 1.1 %send_half.1 = (bf16[8,8,16,256]{3,2,1,0:T(8,128)(2,1)S(1)}, bf16[256,256]{1,0:T(8,128)(2,1)S(1)}) custom-call(s32[2]{0:T(128)S(1)} %pad_add_fusion.idx_ref, f32[8,16,128]{2,1,0:T(8,128)S(1)} %all-to-all-done.2.state_ref, f32[256,256]{1,0:T(8,128)S(1)} %get-tuple-element.7.own_ref, f32[256,256]{1,0:T(8,128)S(1)} %collective-permute-done.1.back_ref, ...), custom_call_target="tpu_custom_call" | custom-call | flops 134217728 | bytes 2500000 | tf_op jit(solution)/shard_map/send_half/pallas_call | solution.py:277
  58.7 1.9 %collective-permute-start.4 = (bf16[8,8,16,256]{3,2,1,0:T(8,128)(2,1)S(1)}, bf16[8,8,16,256]{3,2,1,0:T(8,128)(2,1)S(1)}, u32[]{:S(2)}, u32[]{:S(2)}) collective-permute-start(bf16[8,8,16,256]{3,2,1,0:T(8,128)(2,1)S(1)} %get-tuple-element.11), channel_id=1, source_target_pairs={{0,4},{4,0},{8,12},{12,8},{16,20},{20,16},{24,28},{28,24},{32,36},... | collective-permute-start | bytes 1572872 | tf_op jit(solution)/shard_map/ppermute | solution.py:394
  60.7 0.9 keep_half.1.keep_ref
  61.5 1.0 %collective-permute-done.4.other_ref = bf16[8,8,16,256]{3,2,1,0:T(8,128)(2,1)S(1)} collective-permute-done((bf16[8,8,16,256]{3,2,1,0:T(8,128)(2,1)S(1)}, bf16[8,8,16,256]{3,2,1,0:T(8,128)(2,1)S(1)}, u32[]{:S(2)}, u32[]{:S(2)}) %collective-permute-start.4) | collective-permute-done | bytes 524320 | tf_op jit(solution)/shard_map/ppermute | solution.py:394
  62.6 0.1 merge.1
  62.6 14.9 %all_to_all.26.parts_ref = bf16[8,8,16,256]{3,2,1,0:T(8,128)(2,1)S(1)} all-to-all(bf16[8,8,16,256]{3,2,1,0:T(8,128)(2,1)S(1)} %merge.1), channel_id=1, replica_groups={{56,48,40,32,24,16,8,0},{60,52,44,36,28,20,12,4},{120,112,104,96,88,80,..., dimensions={0} | all-to-all | bytes 1048576 | tf_op jit(solution)/shard_map/all_to_all | solution.py:375
  77.5 0.1 fold.1
  77.6 15.2 %all_to_all.27.parts_ref = bf16[8,16,256]{2,1,0:T(8,128)(2,1)S(1)} all-to-all(bf16[8,16,256]{2,1,0:T(8,128)(2,1)S(1)} %fold.1), channel_id=1, replica_groups={{256,320,384,448,0,64,128,192},{260,324,388,452,4,68,132,196},{264,328,..., dimensions={0} | all-to-all | bytes 131072 | tf_op jit(solution)/shard_map/all_to_all | solution.py:375
  92.8 0.6 finish.1
  (9 shorter events, 0.0 us)
Async XLA Ops:
  0.6 33.1 %collective-permute-start.2 = (bf16[256,512]{1,0:T(8,128)(2,1)}, bf16[256,512]{1,0:T(8,128)(2,1)S(1)}, u32[]{:S(2)}, u32[]{:S(2)}) collective-permute-start(bf16[256,512]{1,0:T(8,128)(2,1)} %own_ref.1), channel_id=1, source_target_pairs={{0,2},{1,3},{2,0},{3,1},{4,6},{5,7},{6,4},{7,5},{8,10},{9,11},{10,... | collective-permute-start | bytes 786440 | tf_op jit(solution)/shard_map/ppermute | solution.py:384
  6.6 27.2 %copy-start = (bf16[256,512]{1,0:T(8,128)(2,1)S(1)}, bf16[256,512]{1,0:T(8,128)(2,1)}, u32[]{:S(2)}) copy-start(bf16[256,512]{1,0:T(8,128)(2,1)} %own_ref.1) | copy-start | bytes 786436
  16.5 17.2 %copy-start.5 = (f32[1,256]{1,0:T(1,128)S(1)}, f32[1,256]{1,0:T(1,128)}, u32[]{:S(2)}) copy-start(f32[1,256]{1,0:T(1,128)} %ld_ref.5) | copy-start | bytes 3076
  16.5 26.2 %all-to-all-start.1 = ((bf16[16,24,128]{2,1,0:T(8,128)(2,1)}), bf16[16,24,128]{2,1,0:T(8,128)(2,1)S(1)}, u32[]{:S(2)}, u32[]{:S(2)}) async-start(bf16[16,24,128]{2,1,0:T(8,128)(2,1)} %plane_total.1), calls=%async_computation.1 | async-start | bytes 196608 | tf_op jit(solution)/shard_map/all_to_all | solution.py:375
  33.7 3.7 %copy-start.1 = (bf16[256,128]{1,0:T(8,128)(2,1)S(1)}, bf16[256,128]{1,0:T(8,128)(2,1)}, u32[]{:S(2)}) copy-start(bf16[256,128]{1,0:T(8,128)(2,1)} %k_ref.3) | copy-start | bytes 196612
  33.7 3.8 %copy-start.2 = (bf16[256,128]{1,0:T(8,128)(2,1)S(1)}, bf16[256,128]{1,0:T(8,128)(2,1)}, u32[]{:S(2)}) copy-start(bf16[256,128]{1,0:T(8,128)(2,1)} %v_ref.3) | copy-start | bytes 196612
  34.0 5.8 %copy-start.3 = (bf16[256,256]{1,0:T(8,128)(2,1)S(1)}, bf16[256,256]{1,0:T(8,128)(2,1)}, u32[]{:S(2)}) copy-start(bf16[256,256]{1,0:T(8,128)(2,1)} %q_ref.3) | copy-start | bytes 393220
  34.0 5.8 %copy-start.4 = (bf16[256,256]{1,0:T(8,128)(2,1)S(1)}, bf16[256,256]{1,0:T(8,128)(2,1)}, u32[]{:S(2)}) copy-start(bf16[256,256]{1,0:T(8,128)(2,1)} %c_ref.3) | copy-start | bytes 393220
  34.0 23.7 %collective-permute-start.3 = (bf16[2,2,256,256]{3,2,1,0:T(8,128)(2,1)S(1)}, bf16[2,2,256,256]{3,2,1,0:T(8,128)(2,1)S(1)}, u32[]{:S(2)}, u32[]{:S(2)}) collective-permute-start(bf16[2,2,256,256]{3,2,1,0:T(8,128)(2,1)S(1)} %pair_up.1.near_ref), channel_id=1, source_target_pairs={{0,1},{1,0},{2,3},{3,2},{4,5},{5,4},{6,7},{7,6},{8,9},{9,8},{10,11... | collective-permute-start | bytes 1572872 | tf_op jit(solution)/shard_map/ppermute | solution.py:386
  37.5 2.3 %collective-permute-start = (bf16[256,256]{1,0:T(8,128)(2,1)S(1)}, bf16[256,256]{1,0:T(8,128)(2,1)S(1)}, u32[]{:S(2)}, u32[]{:S(2)}) collective-permute-start(bf16[256,256]{1,0:T(8,128)(2,1)S(1)} %pad_maximum_fusion), channel_id=1, source_target_pairs={{0,4},{4,8},{8,12},{12,16},{16,20},{20,24},{24,28},{28,32},{32,36}... | collective-permute-start | bytes 393224 | tf_op jit(solution)/shard_map/ppermute | solution.py:313
  41.4 10.6 %collective-permute-start.1 = (f32[256,256]{1,0:T(8,128)S(1)}, f32[256,256]{1,0:T(8,128)S(1)}, u32[]{:S(2)}, u32[]{:S(2)}) collective-permute-start(f32[256,256]{1,0:T(8,128)S(1)} %get-tuple-element.8), channel_id=1, source_target_pairs={{4,0},{8,4},{12,8},{16,12},{20,16},{24,20},{28,24},{32,28},{36,32}... | collective-permute-start | bytes 786440 | tf_op jit(solution)/shard_map/ppermute | solution.py:313
  43.9 13.7 %all-to-all-start.2 = ((f32[8,16,128]{2,1,0:T(8,128)}), f32[8,16,128]{2,1,0:T(8,128)S(1)}, u32[]{:S(2)}, u32[]{:S(2)}) async-start(f32[8,16,128]{2,1,0:T(8,128)} %enter.1), calls=%async_computation.2 | async-start | bytes 131072 | tf_op jit(solution)/shard_map/all_to_all | solution.py:375
  58.7 3.8 %collective-permute-start.4 = (bf16[8,8,16,256]{3,2,1,0:T(8,128)(2,1)S(1)}, bf16[8,8,16,256]{3,2,1,0:T(8,128)(2,1)S(1)}, u32[]{:S(2)}, u32[]{:S(2)}) collective-permute-start(bf16[8,8,16,256]{3,2,1,0:T(8,128)(2,1)S(1)} %get-tuple-element.11), channel_id=1, source_target_pairs={{0,4},{4,0},{8,12},{12,8},{16,20},{20,16},{24,28},{28,24},{32,36},... | collective-permute-start | bytes 1572872 | tf_op jit(solution)/shard_map/ppermute | solution.py:394

commit v7 on v6

--- a/solution.py
+++ b/solution.py
@@ -21,7 +21,7 @@
 neg_fill = -1e30
 
 
-FIRST, ACROSS, LAST, NEAR, FAR = 7, 10, 0, 7, 4
+FIRST, ACROSS, LAST, NEAR, FAR = 7, 10, 2, 6, 4
 
 
 def place(z, y, core):
@@ -150,10 +150,10 @@
         half = (c_ref[:, cols].astype(F32) * 0.5).astype(BF16)
         raw = mm(k, q, NT)
         prod = mm(v, half, NT)
-        scores = jnp.where(inside, raw * FACTOR, mm(prior_k, q, NT) * FACTOR + outside)
+        scores = jnp.where(inside, raw, mm(prior_k, q, NT) + outside) * FACTOR
         dprob = jnp.where(inside, prod, mm(prior_v, half, NT))
         expo = jnp.exp(scores - jnp.max(scores, axis=0, keepdims=True))
-        attend = expo / jnp.sum(expo, axis=0, keepdims=True)
+        attend = expo * (1.0 / jnp.sum(expo, axis=0, keepdims=True))
         delta = jnp.sum(attend * dprob, axis=0, keepdims=True)
         dscore = (attend * (dprob - delta)).astype(BF16)
         low = attend.astype(BF16)

time: 94 us -> 92.6 us (0.985)
  blocking collectives: 39.3 us -> 38.1 us
  waiting for transfers between devices: 7.52 us -> 6.49 us
    all_to_all x3, blocking collectives: 39.3 us -> 38.1 us  [exchange(): lax.all_to_all(value, 'ctx', 0, 0, axis_index_groups=groups, tiled=True)]
    all_to_all x2, waiting for transfers between devices: 5.62 us -> 4.59 us  [exchange(): lax.all_to_all(value, 'ctx', 0, 0, axis_index_groups=groups, tiled=True)]
where the time goes in v7:
time: 92.6 us; the launch traced here: 91.9 us
  starting transfers between devices  38.2 us (41%)
  blocking collectives  38.1 us (41%)
  Pallas kernels  8.28 us (9%)
  waiting for transfers between devices  6.49 us (7%)
    all_to_all x3, blocking collectives, exchange(): lax.all_to_all(value, 'ctx', 0, 0, axis_index_groups=groups, tiled=True)  38.1 us
    all_to_all x2, starting transfers between devices, exchange(): lax.all_to_all(value, 'ctx', 0, 0, axis_index_groups=groups, tiled=True)  26.1 us
    all_to_all x2, waiting for transfers between devices, exchange(): lax.all_to_all(value, 'ctx', 0, 0, axis_index_groups=groups, tiled=True)  4.59 us
    ppermute x1, starting transfers between devices, on_device(): lax.ppermute(layer_input, 'head', [(i, i ^ 2) for i in range(NH)])  4.04 us
    ppermute x1, starting transfers between devices, on_device(): far = lax.ppermute(near, 'head', [(i, i ^ 1) for i in range(NH)])  3.47 us
    ppermute x2, starting transfers between devices, shifted(): lax.ppermute(value, 'ctx', [(source, source + steps) for source in range(...  2.59 us
    ppermute x1, starting transfers between devices, on_device(): other = lax.ppermute(send, 'ctx', [(i, i ^ 1) for i in range(NZ * NP)])  1.92 us
    pallas_call x1, Pallas kernels, summary(): pl.pallas_call(summary_kernel, out_shape=jax.ShapeDtypeStruct((NP, ROWS +...  1.9 us
  transfers between devices with their start and end apart: 7, of which 3 were waited for; matrix products, arithmetic and copies ran while one was open for 0% of the time, Pallas kernels for 7%

profile of v7, /device:TPU:2, one launch (start us, length us, event | category | flops | bytes accessed | tf_op | source)
XLA Modules:
  0.0 91.9 jit_solution(6389650829001272486)
XLA Ops:
  0.6 4.0 %collective-permute-start.2 = (bf16[256,512]{1,0:T(8,128)(2,1)}, bf16[256,512]{1,0:T(8,128)(2,1)S(1)}, u32[]{:S(2)}, u32[]{:S(2)}) collective-permute-start(bf16[256,512]{1,0:T(8,128)(2,1)} %own_ref.1), channel_id=1, source_target_pairs={{0,2},{1,3},{2,0},{3,1},{4,6},{5,7},{6,4},{7,5},{8,10},{9,11},{10,... | collective-permute-start | bytes 786440 | tf_op jit(solution)/shard_map/ppermute | solution.py:384
  4.7 1.9 %summary.1 = f32[8,24,128]{2,1,0:T(8,128)} custom-call(bf16[256,256]{1,0:T(8,128)(2,1)} %q_ref.3, bf16[256,256]{1,0:T(8,128)(2,1)} %c_ref.3, f32[1,256]{1,0:T(1,128)} %ld_ref.5), custom_call_target="tpu_custom_call" | custom-call | flops 16777216 | bytes 400000 | tf_op jit(solution)/shard_map/summary/pallas_call | solution.py:104
  6.6 9.3 %all_to_all.25.got_ref = f32[8,24,128]{2,1,0:T(8,128)S(1)} all-to-all(f32[8,24,128]{2,1,0:T(8,128)} %summary.1), channel_id=1, replica_groups={{28,24,20,16,12,8,4,0},{60,56,52,48,44,40,36,32},{92,88,84,80,76,72,68,..., dimensions={0} | all-to-all | bytes 196608 | tf_op jit(solution)/shard_map/all_to_all | solution.py:375
  15.9 0.7 plane_total.1
  16.5 17.2 %all-to-all-start.1 = ((bf16[16,24,128]{2,1,0:T(8,128)(2,1)}), bf16[16,24,128]{2,1,0:T(8,128)(2,1)S(1)}, u32[]{:S(2)}, u32[]{:S(2)}) async-start(bf16[16,24,128]{2,1,0:T(8,128)(2,1)} %plane_total.1), calls=%async_computation.1 | async-start | bytes 196608 | tf_op jit(solution)/shard_map/all_to_all | solution.py:375
  33.7 0.0 copy-start.2
  33.7 0.0 collective-permute-done.2.got_ref
  33.8 0.2 pair_up.1.near_ref
  34.0 0.0 copy-start.3
  34.0 0.0 copy-start.4
  34.0 3.5 %collective-permute-start.3 = (bf16[2,2,256,256]{3,2,1,0:T(8,128)(2,1)S(1)}, bf16[2,2,256,256]{3,2,1,0:T(8,128)(2,1)S(1)}, u32[]{:S(2)}, u32[]{:S(2)}) collective-permute-start(bf16[2,2,256,256]{3,2,1,0:T(8,128)(2,1)S(1)} %pair_up.1.near_ref), channel_id=1, source_target_pairs={{0,1},{1,0},{2,3},{3,2},{4,5},{5,4},{6,7},{7,6},{8,9},{9,8},{10,11... | collective-permute-start | bytes 1572872 | tf_op jit(solution)/shard_map/ppermute | solution.py:386
  37.5 1.3 %collective-permute-start = (bf16[256,256]{1,0:T(8,128)(2,1)S(1)}, bf16[256,256]{1,0:T(8,128)(2,1)S(1)}, u32[]{:S(2)}, u32[]{:S(2)}) collective-permute-start(bf16[256,256]{1,0:T(8,128)(2,1)S(1)} %pad_maximum_fusion), channel_id=1, source_target_pairs={{0,4},{4,8},{8,12},{12,16},{16,20},{20,24},{24,28},{28,32},{32,36}... | collective-permute-start | bytes 393224 | tf_op jit(solution)/shard_map/ppermute | solution.py:313
  38.8 0.1 pad_add_fusion.idx_ref
  38.9 0.9 collective-permute-done.prior_ref
  39.8 0.0 copy-done.3
  39.8 1.6 %local.1 = (f32[256,256]{1,0:T(8,128)S(1)}, f32[256,256]{1,0:T(8,128)S(1)}, f32[256,128]{1,0:T(8,128)S(1)}) custom-call(s32[2]{0:T(128)S(1)} %pad_add_fusion.idx_ref, bf16[256,256]{1,0:T(8,128)(2,1)S(1)} %copy-done.3, bf16[256,256]{1,0:T(8,128)(2,1)S(1)} %copy-done.4, bf16[256,128]{1,0:T(8,128)(2,1)S(1)} %copy-done.1, bf16[256,128]{1,0:T(8,128)(2,1)S(1)} %copy-done.2, ...), custom_call_target="tpu_custom_call" | custom-call | flops 335544320 | bytes 1200000 | tf_op jit(solution)/shard_map/local/pallas_call | solution.py:175
  41.4 1.3 %collective-permute-start.1 = (f32[256,256]{1,0:T(8,128)S(1)}, f32[256,256]{1,0:T(8,128)S(1)}, u32[]{:S(2)}, u32[]{:S(2)}) collective-permute-start(f32[256,256]{1,0:T(8,128)S(1)} %get-tuple-element.8), channel_id=1, source_target_pairs={{4,0},{8,4},{12,8},{16,12},{20,16},{24,20},{28,24},{32,28},{36,32}... | collective-permute-start | bytes 786440 | tf_op jit(solution)/shard_map/ppermute | solution.py:313
  42.7 0.0 all-to-all-done.1.planes_ref
  42.7 1.2 %enter.1 = f32[8,16,128]{2,1,0:T(8,128)} custom-call(s32[2]{0:T(128)S(1)} %pad_add_fusion.idx_ref, f32[8,24,128]{2,1,0:T(8,128)S(1)} %all_to_all.25.got_ref, bf16[16,24,128]{2,1,0:T(8,128)(2,1)S(1)} %all-to-all-done.1.planes_ref), custom_call_target="tpu_custom_call" | custom-call | bytes 400000 | tf_op jit(solution)/shard_map/enter/pallas_call | solution.py:232
  43.9 9.0 %all-to-all-start.2 = ((f32[8,16,128]{2,1,0:T(8,128)}), f32[8,16,128]{2,1,0:T(8,128)S(1)}, u32[]{:S(2)}, u32[]{:S(2)}) async-start(f32[8,16,128]{2,1,0:T(8,128)} %enter.1), calls=%async_computation.2 | async-start | bytes 131072 | tf_op jit(solution)/shard_map/all_to_all | solution.py:375
  52.9 0.0 collective-permute-done.1.back_ref
  52.9 4.6 %all-to-all-done.2.state_ref = f32[8,16,128]{2,1,0:T(8,128)S(1)} async-done(((f32[8,16,128]{2,1,0:T(8,128)}), f32[8,16,128]{2,1,0:T(8,128)S(1)}, u32[]{:S(2)}, u32[]{:S(2)}) %all-to-all-start.2) | async-done | bytes 65568 | tf_op jit(solution)/shard_map/all_to_all | solution.py:375
  57.5 0.0 collective-permute-done.3.far_ref
  57.5 1.1 %send_half.1 = (bf16[8,8,16,256]{3,2,1,0:T(8,128)(2,1)S(1)}, bf16[256,256]{1,0:T(8,128)(2,1)S(1)}) custom-call(s32[2]{0:T(128)S(1)} %pad_add_fusion.idx_ref, f32[8,16,128]{2,1,0:T(8,128)S(1)} %all-to-all-done.2.state_ref, f32[256,256]{1,0:T(8,128)S(1)} %get-tuple-element.7.own_ref, f32[256,256]{1,0:T(8,128)S(1)} %collective-permute-done.1.back_ref, ...), custom_call_target="tpu_custom_call" | custom-call | flops 134217728 | bytes 2500000 | tf_op jit(solution)/shard_map/send_half/pallas_call | solution.py:277
  58.6 1.9 %collective-permute-start.4 = (bf16[8,8,16,256]{3,2,1,0:T(8,128)(2,1)S(1)}, bf16[8,8,16,256]{3,2,1,0:T(8,128)(2,1)S(1)}, u32[]{:S(2)}, u32[]{:S(2)}) collective-permute-start(bf16[8,8,16,256]{3,2,1,0:T(8,128)(2,1)S(1)} %get-tuple-element.11), channel_id=1, source_target_pairs={{0,4},{4,0},{8,12},{12,8},{16,20},{20,16},{24,28},{28,24},{32,36},... | collective-permute-start | bytes 1572872 | tf_op jit(solution)/shard_map/ppermute | solution.py:394
  60.5 0.9 keep_half.1.keep_ref
  61.4 1.0 %collective-permute-done.4.other_ref = bf16[8,8,16,256]{3,2,1,0:T(8,128)(2,1)S(1)} collective-permute-done((bf16[8,8,16,256]{3,2,1,0:T(8,128)(2,1)S(1)}, bf16[8,8,16,256]{3,2,1,0:T(8,128)(2,1)S(1)}, u32[]{:S(2)}, u32[]{:S(2)}) %collective-permute-start.4) | collective-permute-done | bytes 524320 | tf_op jit(solution)/shard_map/ppermute | solution.py:394
  62.4 0.1 merge.1
  62.5 13.5 %all_to_all.26.parts_ref = bf16[8,8,16,256]{3,2,1,0:T(8,128)(2,1)S(1)} all-to-all(bf16[8,8,16,256]{3,2,1,0:T(8,128)(2,1)S(1)} %merge.1), channel_id=1, replica_groups={{48,56,32,40,16,24,0,8},{52,60,36,44,20,28,4,12},{112,120,96,104,80,88,..., dimensions={0} | all-to-all | bytes 1048576 | tf_op jit(solution)/shard_map/all_to_all | solution.py:375
  76.0 0.1 fold.1
  76.1 15.3 %all_to_all.27.parts_ref = bf16[8,16,256]{2,1,0:T(8,128)(2,1)S(1)} all-to-all(bf16[8,16,256]{2,1,0:T(8,128)(2,1)S(1)} %fold.1), channel_id=1, replica_groups={{256,320,384,448,0,64,128,192},{260,324,388,452,4,68,132,196},{264,328,..., dimensions={0} | all-to-all | bytes 131072 | tf_op jit(solution)/shard_map/all_to_all | solution.py:375
  91.3 0.6 finish.1
  (9 shorter events, 0.0 us)
Async XLA Ops:
  0.6 33.1 %collective-permute-start.2 = (bf16[256,512]{1,0:T(8,128)(2,1)}, bf16[256,512]{1,0:T(8,128)(2,1)S(1)}, u32[]{:S(2)}, u32[]{:S(2)}) collective-permute-start(bf16[256,512]{1,0:T(8,128)(2,1)} %own_ref.1), channel_id=1, source_target_pairs={{0,2},{1,3},{2,0},{3,1},{4,6},{5,7},{6,4},{7,5},{8,10},{9,11},{10,... | collective-permute-start | bytes 786440 | tf_op jit(solution)/shard_map/ppermute | solution.py:384
  6.6 27.2 %copy-start = (bf16[256,512]{1,0:T(8,128)(2,1)S(1)}, bf16[256,512]{1,0:T(8,128)(2,1)}, u32[]{:S(2)}) copy-start(bf16[256,512]{1,0:T(8,128)(2,1)} %own_ref.1) | copy-start | bytes 786436
  16.5 17.2 %copy-start.5 = (f32[1,256]{1,0:T(1,128)S(1)}, f32[1,256]{1,0:T(1,128)}, u32[]{:S(2)}) copy-start(f32[1,256]{1,0:T(1,128)} %ld_ref.5) | copy-start | bytes 3076
  16.5 26.2 %all-to-all-start.1 = ((bf16[16,24,128]{2,1,0:T(8,128)(2,1)}), bf16[16,24,128]{2,1,0:T(8,128)(2,1)S(1)}, u32[]{:S(2)}, u32[]{:S(2)}) async-start(bf16[16,24,128]{2,1,0:T(8,128)(2,1)} %plane_total.1), calls=%async_computation.1 | async-start | bytes 196608 | tf_op jit(solution)/shard_map/all_to_all | solution.py:375
  33.7 3.7 %copy-start.1 = (bf16[256,128]{1,0:T(8,128)(2,1)S(1)}, bf16[256,128]{1,0:T(8,128)(2,1)}, u32[]{:S(2)}) copy-start(bf16[256,128]{1,0:T(8,128)(2,1)} %k_ref.3) | copy-start | bytes 196612
  33.7 3.8 %copy-start.2 = (bf16[256,128]{1,0:T(8,128)(2,1)S(1)}, bf16[256,128]{1,0:T(8,128)(2,1)}, u32[]{:S(2)}) copy-start(bf16[256,128]{1,0:T(8,128)(2,1)} %v_ref.3) | copy-start | bytes 196612
  34.0 5.8 %copy-start.3 = (bf16[256,256]{1,0:T(8,128)(2,1)S(1)}, bf16[256,256]{1,0:T(8,128)(2,1)}, u32[]{:S(2)}) copy-start(bf16[256,256]{1,0:T(8,128)(2,1)} %q_ref.3) | copy-start | bytes 393220
  34.0 5.8 %copy-start.4 = (bf16[256,256]{1,0:T(8,128)(2,1)S(1)}, bf16[256,256]{1,0:T(8,128)(2,1)}, u32[]{:S(2)}) copy-start(bf16[256,256]{1,0:T(8,128)(2,1)} %c_ref.3) | copy-start | bytes 393220
  34.0 23.5 %collective-permute-start.3 = (bf16[2,2,256,256]{3,2,1,0:T(8,128)(2,1)S(1)}, bf16[2,2,256,256]{3,2,1,0:T(8,128)(2,1)S(1)}, u32[]{:S(2)}, u32[]{:S(2)}) collective-permute-start(bf16[2,2,256,256]{3,2,1,0:T(8,128)(2,1)S(1)} %pair_up.1.near_ref), channel_id=1, source_target_pairs={{0,1},{1,0},{2,3},{3,2},{4,5},{5,4},{6,7},{7,6},{8,9},{9,8},{10,11... | collective-permute-start | bytes 1572872 | tf_op jit(solution)/shard_map/ppermute | solution.py:386
  37.5 2.3 %collective-permute-start = (bf16[256,256]{1,0:T(8,128)(2,1)S(1)}, bf16[256,256]{1,0:T(8,128)(2,1)S(1)}, u32[]{:S(2)}, u32[]{:S(2)}) collective-permute-start(bf16[256,256]{1,0:T(8,128)(2,1)S(1)} %pad_maximum_fusion), channel_id=1, source_target_pairs={{0,4},{4,8},{8,12},{12,16},{16,20},{20,24},{24,28},{28,32},{32,36}... | collective-permute-start | bytes 393224 | tf_op jit(solution)/shard_map/ppermute | solution.py:313
  41.4 11.5 %collective-permute-start.1 = (f32[256,256]{1,0:T(8,128)S(1)}, f32[256,256]{1,0:T(8,128)S(1)}, u32[]{:S(2)}, u32[]{:S(2)}) collective-permute-start(f32[256,256]{1,0:T(8,128)S(1)} %get-tuple-element.8), channel_id=1, source_target_pairs={{4,0},{8,4},{12,8},{16,12},{20,16},{24,20},{28,24},{32,28},{36,32}... | collective-permute-start | bytes 786440 | tf_op jit(solution)/shard_map/ppermute | solution.py:313
  43.9 13.5 %all-to-all-start.2 = ((f32[8,16,128]{2,1,0:T(8,128)}), f32[8,16,128]{2,1,0:T(8,128)S(1)}, u32[]{:S(2)}, u32[]{:S(2)}) async-start(f32[8,16,128]{2,1,0:T(8,128)} %enter.1), calls=%async_computation.2 | async-start | bytes 131072 | tf_op jit(solution)/shard_map/all_to_all | solution.py:375
  58.6 3.8 %collective-permute-start.4 = (bf16[8,8,16,256]{3,2,1,0:T(8,128)(2,1)S(1)}, bf16[8,8,16,256]{3,2,1,0:T(8,128)(2,1)S(1)}, u32[]{:S(2)}, u32[]{:S(2)}) collective-permute-start(bf16[8,8,16,256]{3,2,1,0:T(8,128)(2,1)S(1)} %get-tuple-element.11), channel_id=1, source_target_pairs={{0,4},{4,0},{8,12},{12,8},{16,20},{20,16},{24,28},{28,24},{32,36},... | collective-permute-start | bytes 1572872 | tf_op jit(solution)/shard_map/ppermute | solution.py:394

commit v8 on v7

--- a/solution.py
+++ b/solution.py
@@ -21,7 +21,7 @@
 neg_fill = -1e30
 
 
-FIRST, ACROSS, LAST, NEAR, FAR = 7, 10, 2, 6, 4
+FIRST, ACROSS, LAST, NEAR, FAR = 5, 10, 1, 6, 4
 
 
 def place(z, y, core):
@@ -33,11 +33,11 @@
 
 
 def z_groups(lead):
-    return [[(q ^ lead) * NP + p for q in range(NZ)] for p in range(NP)]
+    return [[(q + lead) % NZ * NP + p for q in range(NZ)] for p in range(NP)]
 
 
 def near_groups(lead):
-    members = [(q ^ lead) for q in range(NB * NY)]
+    members = [(q + lead) % (NB * NY) for q in range(NB * NY)]
     return [
         [place(a * NB + m // NY, m % NY, core) for m in members]
         for a in range(NA)
@@ -219,7 +219,7 @@
     state = jnp.zeros((ROWS, E), F32)
     for z in range(NZ):
         later = z > mine
-        plane = planes_ref[z ^ ACROSS].astype(F32)
+        plane = planes_ref[(z - ACROSS) % NZ].astype(F32)
         state += jnp.where(later, jnp.exp(log), 0.0) * plane[:ROWS]
         log += jnp.where(later, jnp.sum(plane[ROWS:], axis=0, keepdims=True), 0.0)
     for k in range(NP - 1, -1, -1):
@@ -249,7 +249,7 @@
         where = pl.ds(lax.bitwise_xor(shard, jnp.int32(FAR // count)) * count, count)
         for b in range(NB):
             for y in range(NY):
-                write((b * NY + y) ^ NEAR, where, found[:, b, y])
+                write((b * NY + y - NEAR) % (NB * NY), where, found[:, b, y])
 
 
 def send_kernel(

time: 92.6 us -> 93.1 us (level)
  no operation moved by 1% of the time
where the time goes in v8:
time: 93.1 us; the launch traced here: 92.5 us
  blocking collectives  38.1 us (41%)
  starting transfers between devices  38 us (41%)
  Pallas kernels  8.29 us (9%)
  waiting for transfers between devices  7.13 us (8%)
    all_to_all x3, blocking collectives, exchange(): lax.all_to_all(value, 'ctx', 0, 0, axis_index_groups=groups, tiled=True)  38.1 us
    all_to_all x2, starting transfers between devices, exchange(): lax.all_to_all(value, 'ctx', 0, 0, axis_index_groups=groups, tiled=True)  26 us
    all_to_all x2, waiting for transfers between devices, exchange(): lax.all_to_all(value, 'ctx', 0, 0, axis_index_groups=groups, tiled=True)  5.23 us
    ppermute x1, starting transfers between devices, on_device(): lax.ppermute(layer_input, 'head', [(i, i ^ 2) for i in range(NH)])  4.04 us
    ppermute x1, starting transfers between devices, on_device(): far = lax.ppermute(near, 'head', [(i, i ^ 1) for i in range(NH)])  3.47 us
    ppermute x2, starting transfers between devices, shifted(): lax.ppermute(value, 'ctx', [(source, source + steps) for source in range(...  2.59 us
    ppermute x1, starting transfers between devices, on_device(): other = lax.ppermute(send, 'ctx', [(i, i ^ 1) for i in range(NZ * NP)])  1.92 us
    pallas_call x1, Pallas kernels, summary(): pl.pallas_call(summary_kernel, out_shape=jax.ShapeDtypeStruct((NP, ROWS +...  1.9 us
  transfers between devices with their start and end apart: 7, of which 3 were waited for; matrix products, arithmetic and copies ran while one was open for 0% of the time, Pallas kernels for 7%

profile of v8, /device:TPU:2, one launch (start us, length us, event | category | flops | bytes accessed | tf_op | source)
XLA Modules:
  0.0 92.5 jit_solution(753191107754261222)
XLA Ops:
  0.6 4.0 %collective-permute-start.2 = (bf16[256,512]{1,0:T(8,128)(2,1)}, bf16[256,512]{1,0:T(8,128)(2,1)S(1)}, u32[]{:S(2)}, u32[]{:S(2)}) collective-permute-start(bf16[256,512]{1,0:T(8,128)(2,1)} %own_ref.1), channel_id=1, source_target_pairs={{0,2},{1,3},{2,0},{3,1},{4,6},{5,7},{6,4},{7,5},{8,10},{9,11},{10,... | collective-permute-start | bytes 786440 | tf_op jit(solution)/shard_map/ppermute | solution.py:384
  4.7 1.9 %summary.1 = f32[8,24,128]{2,1,0:T(8,128)} custom-call(bf16[256,256]{1,0:T(8,128)(2,1)} %q_ref.3, bf16[256,256]{1,0:T(8,128)(2,1)} %c_ref.3, f32[1,256]{1,0:T(1,128)} %ld_ref.5), custom_call_target="tpu_custom_call" | custom-call | flops 16777216 | bytes 400000 | tf_op jit(solution)/shard_map/summary/pallas_call | solution.py:104
  6.6 8.9 %all_to_all.25.got_ref = f32[8,24,128]{2,1,0:T(8,128)S(1)} all-to-all(f32[8,24,128]{2,1,0:T(8,128)} %summary.1), channel_id=1, replica_groups={{20,16,28,24,4,0,12,8},{52,48,60,56,36,32,44,40},{84,80,92,88,68,64,76,..., dimensions={0} | all-to-all | bytes 196608 | tf_op jit(solution)/shard_map/all_to_all | solution.py:375
  15.4 0.7 plane_total.1
  16.1 17.2 %all-to-all-start.1 = ((bf16[16,24,128]{2,1,0:T(8,128)(2,1)}), bf16[16,24,128]{2,1,0:T(8,128)(2,1)S(1)}, u32[]{:S(2)}, u32[]{:S(2)}) async-start(bf16[16,24,128]{2,1,0:T(8,128)(2,1)} %plane_total.1), calls=%async_computation.1 | async-start | bytes 196608 | tf_op jit(solution)/shard_map/all_to_all | solution.py:375
  33.3 0.0 copy-start.2
  33.3 0.0 collective-permute-done.2.got_ref
  33.3 0.0 copy-done
  33.3 0.2 pair_up.1.near_ref
  33.5 0.0 copy-start.3
  33.5 0.0 copy-start.4
  33.6 3.5 %collective-permute-start.3 = (bf16[2,2,256,256]{3,2,1,0:T(8,128)(2,1)S(1)}, bf16[2,2,256,256]{3,2,1,0:T(8,128)(2,1)S(1)}, u32[]{:S(2)}, u32[]{:S(2)}) collective-permute-start(bf16[2,2,256,256]{3,2,1,0:T(8,128)(2,1)S(1)} %pair_up.1.near_ref), channel_id=1, source_target_pairs={{0,1},{1,0},{2,3},{3,2},{4,5},{5,4},{6,7},{7,6},{8,9},{9,8},{10,11... | collective-permute-start | bytes 1572872 | tf_op jit(solution)/shard_map/ppermute | solution.py:386
  37.1 1.3 %collective-permute-start = (bf16[256,256]{1,0:T(8,128)(2,1)S(1)}, bf16[256,256]{1,0:T(8,128)(2,1)S(1)}, u32[]{:S(2)}, u32[]{:S(2)}) collective-permute-start(bf16[256,256]{1,0:T(8,128)(2,1)S(1)} %pad_maximum_fusion), channel_id=1, source_target_pairs={{0,4},{4,8},{8,12},{12,16},{16,20},{20,24},{24,28},{28,32},{32,36}... | collective-permute-start | bytes 393224 | tf_op jit(solution)/shard_map/ppermute | solution.py:313
  38.4 0.1 pad_add_fusion.idx_ref
  38.5 0.9 collective-permute-done.prior_ref
  39.4 1.6 %local.1 = (f32[256,256]{1,0:T(8,128)S(1)}, f32[256,256]{1,0:T(8,128)S(1)}, f32[256,128]{1,0:T(8,128)S(1)}) custom-call(s32[2]{0:T(128)S(1)} %pad_add_fusion.idx_ref, bf16[256,256]{1,0:T(8,128)(2,1)S(1)} %copy-done.3, bf16[256,256]{1,0:T(8,128)(2,1)S(1)} %copy-done.4, bf16[256,128]{1,0:T(8,128)(2,1)S(1)} %copy-done.1, bf16[256,128]{1,0:T(8,128)(2,1)S(1)} %copy-done.2, ...), custom_call_target="tpu_custom_call" | custom-call | flops 335544320 | bytes 1200000 | tf_op jit(solution)/shard_map/local/pallas_call | solution.py:175
  41.0 1.3 %collective-permute-start.1 = (f32[256,256]{1,0:T(8,128)S(1)}, f32[256,256]{1,0:T(8,128)S(1)}, u32[]{:S(2)}, u32[]{:S(2)}) collective-permute-start(f32[256,256]{1,0:T(8,128)S(1)} %get-tuple-element.8), channel_id=1, source_target_pairs={{4,0},{8,4},{12,8},{16,12},{20,16},{24,20},{28,24},{32,28},{36,32}... | collective-permute-start | bytes 786440 | tf_op jit(solution)/shard_map/ppermute | solution.py:313
  42.3 0.0 all-to-all-done.1.planes_ref
  42.3 1.2 %enter.1 = f32[8,16,128]{2,1,0:T(8,128)} custom-call(s32[2]{0:T(128)S(1)} %pad_add_fusion.idx_ref, f32[8,24,128]{2,1,0:T(8,128)S(1)} %all_to_all.25.got_ref, bf16[16,24,128]{2,1,0:T(8,128)(2,1)S(1)} %all-to-all-done.1.planes_ref), custom_call_target="tpu_custom_call" | custom-call | bytes 400000 | tf_op jit(solution)/shard_map/enter/pallas_call | solution.py:232
  43.5 8.8 %all-to-all-start.2 = ((f32[8,16,128]{2,1,0:T(8,128)}), f32[8,16,128]{2,1,0:T(8,128)S(1)}, u32[]{:S(2)}, u32[]{:S(2)}) async-start(f32[8,16,128]{2,1,0:T(8,128)} %enter.1), calls=%async_computation.2 | async-start | bytes 131072 | tf_op jit(solution)/shard_map/all_to_all | solution.py:375
  52.3 0.0 collective-permute-done.1.back_ref
  52.3 5.2 %all-to-all-done.2.state_ref = f32[8,16,128]{2,1,0:T(8,128)S(1)} async-done(((f32[8,16,128]{2,1,0:T(8,128)}), f32[8,16,128]{2,1,0:T(8,128)S(1)}, u32[]{:S(2)}, u32[]{:S(2)}) %all-to-all-start.2) | async-done | bytes 65568 | tf_op jit(solution)/shard_map/all_to_all | solution.py:375
  57.6 0.0 collective-permute-done.3.far_ref
  57.6 1.1 %send_half.1 = (bf16[8,8,16,256]{3,2,1,0:T(8,128)(2,1)S(1)}, bf16[256,256]{1,0:T(8,128)(2,1)S(1)}) custom-call(s32[2]{0:T(128)S(1)} %pad_add_fusion.idx_ref, f32[8,16,128]{2,1,0:T(8,128)S(1)} %all-to-all-done.2.state_ref, f32[256,256]{1,0:T(8,128)S(1)} %get-tuple-element.7.own_ref, f32[256,256]{1,0:T(8,128)S(1)} %collective-permute-done.1.back_ref, ...), custom_call_target="tpu_custom_call" | custom-call | flops 134217728 | bytes 2500000 | tf_op jit(solution)/shard_map/send_half/pallas_call | solution.py:277
  58.6 1.9 %collective-permute-start.4 = (bf16[8,8,16,256]{3,2,1,0:T(8,128)(2,1)S(1)}, bf16[8,8,16,256]{3,2,1,0:T(8,128)(2,1)S(1)}, u32[]{:S(2)}, u32[]{:S(2)}) collective-permute-start(bf16[8,8,16,256]{3,2,1,0:T(8,128)(2,1)S(1)} %get-tuple-element.11), channel_id=1, source_target_pairs={{0,4},{4,0},{8,12},{12,8},{16,20},{20,16},{24,28},{28,24},{32,36},... | collective-permute-start | bytes 1572872 | tf_op jit(solution)/shard_map/ppermute | solution.py:394
  60.6 0.9 keep_half.1.keep_ref
  61.4 1.0 %collective-permute-done.4.other_ref = bf16[8,8,16,256]{3,2,1,0:T(8,128)(2,1)S(1)} collective-permute-done((bf16[8,8,16,256]{3,2,1,0:T(8,128)(2,1)S(1)}, bf16[8,8,16,256]{3,2,1,0:T(8,128)(2,1)S(1)}, u32[]{:S(2)}, u32[]{:S(2)}) %collective-permute-start.4) | collective-permute-done | bytes 524320 | tf_op jit(solution)/shard_map/ppermute | solution.py:394
  62.4 0.1 merge.1
  62.5 14.0 %all_to_all.26.parts_ref = bf16[8,8,16,256]{3,2,1,0:T(8,128)(2,1)S(1)} all-to-all(bf16[8,8,16,256]{3,2,1,0:T(8,128)(2,1)S(1)} %merge.1), channel_id=1, replica_groups={{48,56,0,8,16,24,32,40},{52,60,4,12,20,28,36,44},{112,120,64,72,80,88,9..., dimensions={0} | all-to-all | bytes 1048576 | tf_op jit(solution)/shard_map/all_to_all | solution.py:375
  76.6 0.1 fold.1
  76.6 15.3 %all_to_all.27.parts_ref = bf16[8,16,256]{2,1,0:T(8,128)(2,1)S(1)} all-to-all(bf16[8,16,256]{2,1,0:T(8,128)(2,1)S(1)} %fold.1), channel_id=1, replica_groups={{256,320,384,448,0,64,128,192},{260,324,388,452,4,68,132,196},{264,328,..., dimensions={0} | all-to-all | bytes 131072 | tf_op jit(solution)/shard_map/all_to_all | solution.py:375
  91.9 0.6 finish.1
  (9 shorter events, 0.0 us)
Async XLA Ops:
  0.6 32.7 %collective-permute-start.2 = (bf16[256,512]{1,0:T(8,128)(2,1)}, bf16[256,512]{1,0:T(8,128)(2,1)S(1)}, u32[]{:S(2)}, u32[]{:S(2)}) collective-permute-start(bf16[256,512]{1,0:T(8,128)(2,1)} %own_ref.1), channel_id=1, source_target_pairs={{0,2},{1,3},{2,0},{3,1},{4,6},{5,7},{6,4},{7,5},{8,10},{9,11},{10,... | collective-permute-start | bytes 786440 | tf_op jit(solution)/shard_map/ppermute | solution.py:384
  6.6 26.7 %copy-start = (bf16[256,512]{1,0:T(8,128)(2,1)S(1)}, bf16[256,512]{1,0:T(8,128)(2,1)}, u32[]{:S(2)}) copy-start(bf16[256,512]{1,0:T(8,128)(2,1)} %own_ref.1) | copy-start | bytes 786436
  16.1 17.2 %copy-start.5 = (f32[1,256]{1,0:T(1,128)S(1)}, f32[1,256]{1,0:T(1,128)}, u32[]{:S(2)}) copy-start(f32[1,256]{1,0:T(1,128)} %ld_ref.5) | copy-start | bytes 3076
  16.1 26.2 %all-to-all-start.1 = ((bf16[16,24,128]{2,1,0:T(8,128)(2,1)}), bf16[16,24,128]{2,1,0:T(8,128)(2,1)S(1)}, u32[]{:S(2)}, u32[]{:S(2)}) async-start(bf16[16,24,128]{2,1,0:T(8,128)(2,1)} %plane_total.1), calls=%async_computation.1 | async-start | bytes 196608 | tf_op jit(solution)/shard_map/all_to_all | solution.py:375
  33.3 3.8 %copy-start.1 = (bf16[256,128]{1,0:T(8,128)(2,1)S(1)}, bf16[256,128]{1,0:T(8,128)(2,1)}, u32[]{:S(2)}) copy-start(bf16[256,128]{1,0:T(8,128)(2,1)} %k_ref.3) | copy-start | bytes 196612
  33.3 3.8 %copy-start.2 = (bf16[256,128]{1,0:T(8,128)(2,1)S(1)}, bf16[256,128]{1,0:T(8,128)(2,1)}, u32[]{:S(2)}) copy-start(bf16[256,128]{1,0:T(8,128)(2,1)} %v_ref.3) | copy-start | bytes 196612
  33.5 5.8 %copy-start.3 = (bf16[256,256]{1,0:T(8,128)(2,1)S(1)}, bf16[256,256]{1,0:T(8,128)(2,1)}, u32[]{:S(2)}) copy-start(bf16[256,256]{1,0:T(8,128)(2,1)} %q_ref.3) | copy-start | bytes 393220
  33.5 5.8 %copy-start.4 = (bf16[256,256]{1,0:T(8,128)(2,1)S(1)}, bf16[256,256]{1,0:T(8,128)(2,1)}, u32[]{:S(2)}) copy-start(bf16[256,256]{1,0:T(8,128)(2,1)} %c_ref.3) | copy-start | bytes 393220
  33.6 24.0 %collective-permute-start.3 = (bf16[2,2,256,256]{3,2,1,0:T(8,128)(2,1)S(1)}, bf16[2,2,256,256]{3,2,1,0:T(8,128)(2,1)S(1)}, u32[]{:S(2)}, u32[]{:S(2)}) collective-permute-start(bf16[2,2,256,256]{3,2,1,0:T(8,128)(2,1)S(1)} %pair_up.1.near_ref), channel_id=1, source_target_pairs={{0,1},{1,0},{2,3},{3,2},{4,5},{5,4},{6,7},{7,6},{8,9},{9,8},{10,11... | collective-permute-start | bytes 1572872 | tf_op jit(solution)/shard_map/ppermute | solution.py:386
  37.1 2.3 %collective-permute-start = (bf16[256,256]{1,0:T(8,128)(2,1)S(1)}, bf16[256,256]{1,0:T(8,128)(2,1)S(1)}, u32[]{:S(2)}, u32[]{:S(2)}) collective-permute-start(bf16[256,256]{1,0:T(8,128)(2,1)S(1)} %pad_maximum_fusion), channel_id=1, source_target_pairs={{0,4},{4,8},{8,12},{12,16},{16,20},{20,24},{24,28},{28,32},{32,36}... | collective-permute-start | bytes 393224 | tf_op jit(solution)/shard_map/ppermute | solution.py:313
  41.0 11.3 %collective-permute-start.1 = (f32[256,256]{1,0:T(8,128)S(1)}, f32[256,256]{1,0:T(8,128)S(1)}, u32[]{:S(2)}, u32[]{:S(2)}) collective-permute-start(f32[256,256]{1,0:T(8,128)S(1)} %get-tuple-element.8), channel_id=1, source_target_pairs={{4,0},{8,4},{12,8},{16,12},{20,16},{24,20},{28,24},{32,28},{36,32}... | collective-permute-start | bytes 786440 | tf_op jit(solution)/shard_map/ppermute | solution.py:313
  43.5 14.0 %all-to-all-start.2 = ((f32[8,16,128]{2,1,0:T(8,128)}), f32[8,16,128]{2,1,0:T(8,128)S(1)}, u32[]{:S(2)}, u32[]{:S(2)}) async-start(f32[8,16,128]{2,1,0:T(8,128)} %enter.1), calls=%async_computation.2 | async-start | bytes 131072 | tf_op jit(solution)/shard_map/all_to_all | solution.py:375
  58.6 3.8 %collective-permute-start.4 = (bf16[8,8,16,256]{3,2,1,0:T(8,128)(2,1)S(1)}, bf16[8,8,16,256]{3,2,1,0:T(8,128)(2,1)S(1)}, u32[]{:S(2)}, u32[]{:S(2)}) collective-permute-start(bf16[8,8,16,256]{3,2,1,0:T(8,128)(2,1)S(1)} %get-tuple-element.11), channel_id=1, source_target_pairs={{0,4},{4,0},{8,12},{12,8},{16,20},{20,16},{24,28},{28,24},{32,36},... | collective-permute-start | bytes 1572872 | tf_op jit(solution)/shard_map/ppermute | solution.py:394
